TPU v7x, 32 devices: a whole 2x2x4 slice. The times are simulated.
32 devices in a mesh: rep: 4 (over y, x), grp: 8 (over z, core).
Axes of the slice: x: 2, y: 2, z: 4, core: 2. Of those that a mesh axis runs over, the one named last changes fastest.
Arguments:
- hidden_in: bfloat16 [2, 4, 1024, 768], P(None, 'rep', 'grp'), may hold values from -6 to 6
- seq_lengths: int32 [2, 4], P(None, 'rep'), may hold values from 256 to 1024, as said below
- latent_query: float32 [768, 768], P('grp'), may hold values from -0.3125 to 0.3125
- latent_key: float32 [768, 768], P('grp'), may hold values from -0.3125 to 0.3125
- latent_value: float32 [768, 768], P('grp'), may hold values from -0.21875 to 0.21875
- latent_out: float32 [768, 768], P('grp'), may hold values from -4 to 4
- latent_up: float32 [3072, 768], P('grp'), may hold values from -0.3125 to 0.3125
- latent_down: float32 [768, 3072], P('grp'), may hold values from -0.3125 to 0.3125
- bias_query: float32 [768], replicated, may hold values from -3 to 3
- bias_value: float32 [768], replicated, may hold values from -3 to 3
- bias_out: float32 [768], replicated, may hold values from -3 to 3
- bias_up: float32 [3072], replicated, may hold values from -3 to 3
- bias_down: float32 [768], replicated, may hold values from -3 to 3
- gain_first: float32 [768], replicated, may hold values from 0.5 to 1.5
- shift_first: float32 [768], replicated, may hold values from -3 to 3
- gain_second: float32 [768], replicated, may hold values from 0.5 to 1.5
- shift_second: float32 [768], replicated, may hold values from -3 to 3
- clip_input: float32 [768], replicated, may hold values from 1 to 3
- teacher_query: bfloat16 [768, 768], P('grp'), may hold values from -0.3125 to 0.3125
- teacher_key: bfloat16 [768, 768], P('grp'), may hold values from -0.3125 to 0.3125
- teacher_value: bfloat16 [768, 768], P('grp'), may hold values from -0.21875 to 0.21875
- teacher_out: bfloat16 [768, 768], P('grp'), may hold values from -4 to 4
- teacher_up: bfloat16 [3072, 768], P('grp'), may hold values from -0.3125 to 0.3125
- teacher_down: bfloat16 [768, 3072], P('grp'), may hold values from -0.3125 to 0.3125
- teacher_biases: float32 [4, 768], replicated, may hold values from -3 to 3
- teacher_inner: float32 [3072], replicated, may hold values from -3 to 3
- teacher_gains: float32 [2, 768], replicated, may hold values from 0.5 to 1.5
- teacher_shifts: float32 [2, 768], replicated, may hold values from -3 to 3
Outputs:
- layer_out: bfloat16 [2, 4, 1024, 768], P(None, 'rep', 'grp')
- distill_loss: float32 [], replicated
- grad_input: float32 [2, 4, 1024, 768], P(None, 'rep', 'grp')
- grad_query: float32 [768, 768], P('grp')
- grad_key: float32 [768, 768], P('grp')
- grad_value: float32 [768, 768], P('grp')
- grad_out: float32 [768, 768], P('grp')
- grad_up: float32 [3072, 768], P('grp')
- grad_down: float32 [768, 3072], P('grp')
- grad_bias_query: float32 [768], P('grp')
- grad_bias_value: float32 [768], P('grp')
- grad_bias_out: float32 [768], P('grp')
- grad_bias_up: float32 [3072], P('grp')
- grad_bias_down: float32 [768], P('grp')
- grad_gain_first: float32 [768], P('grp')
- grad_shift_first: float32 [768], P('grp')
- grad_gain_second: float32 [768], P('grp')
- grad_shift_second: float32 [768], P('grp')
Inputs may be any that keep to these rules, and one draw needn't show every extreme that they name: `seq_lengths`: A sequence's valid positions are its first ones; in every draw some sequence is valid over all 1024 positions.
All inputs are finite; a program needn't handle non-finite values.
Results may differ from a plain program's by a relative error of at most 0.023.
Values may be sent and summed in bfloat16 or wider, within the bound.
No kernel may reach another device: no remote copies, remote signals or barrier semaphores. Data moves between devices by JAX's collectives and lax.ppermute only.
A program may use at most 192 MiB of HBM per device.

v0:
```python
import jax
import jax.numpy as jnp
from jax import lax
from jax.sharding import PartitionSpec as P

H = 12
DH = 64


NEG_FILL = -1e30
NORM_EPS = 1e-05


def layer_norm(tensor, gain_row, shift_row):
    centre = tensor - jnp.mean(tensor, axis=-1, keepdims=True)
    spread = jnp.mean(centre * centre, axis=-1, keepdims=True)
    return centre * lax.rsqrt(spread + NORM_EPS) * gain_row + shift_row


def gelu_exact(tensor):
    return 0.5 * tensor * (1.0 + lax.erf(tensor * 0.7071067811865476))


def times_rows(operand, weight):
    return lax.dot_general(
        operand, weight, (((1,), (1,)), ((), ())), preferred_element_type=jnp.float32
    )


def binarize(latent_rows):
    magnitude = jnp.mean(jnp.abs(latent_rows), axis=1, keepdims=True)
    return (magnitude * jnp.sign(latent_rows)).astype(jnp.bfloat16)


def student_project(operand, latent):
    return times_rows(
        operand,
        binarize(
            lax.all_gather(latent.astype(jnp.bfloat16), "grp", axis=0, tiled=True).astype(
                jnp.float32
            )
        ),
    )


def teacher_project(operand, weight):
    return times_rows(operand, lax.all_gather(weight, "grp", axis=0, tiled=True))


def add_columns(grads_low, weight_rows):
    return jnp.dot(grads_low, weight_rows, preferred_element_type=jnp.float32)


def student_back(grads_low, latent):
    return add_columns(
        grads_low,
        binarize(
            lax.all_gather(latent.astype(jnp.bfloat16), "grp", axis=0, tiled=True).astype(
                jnp.float32
            )
        ),
    )


def weight_grad(grads_low, operand):
    return lax.dot_general(
        grads_low, operand, (((0,), (0,)), ((), ())), preferred_element_type=jnp.float32
    )


def head_scores(queries, keys):
    seq_count, query_rows = (queries.shape[0], queries.shape[1])
    key_rows = keys.shape[1]
    query_heads = queries.reshape(seq_count, query_rows, H, DH)
    key_heads = keys.reshape(seq_count, key_rows, H, DH)
    return jnp.einsum(
        "schd,snhd->shcn", query_heads, key_heads, preferred_element_type=jnp.float32
    ) * DH ** (-0.5)


def key_mask(lengths, first_row, key_rows):
    positions = first_row + jnp.arange(key_rows, dtype=jnp.int32)
    return (positions[None, :] < lengths[:, None])[:, None, None, :]


def in_blocks(block_step, state_in, pieces):
    total_rows = pieces[0].shape[1]
    block_rows = 512

    def scan_step(running, block_index):
        offset = block_index * block_rows
        sliced = tuple(
            (lax.dynamic_slice_in_dim(member, offset, block_rows, 1) for member in pieces)
        )
        return (block_step(running, sliced, offset), None)

    state_out, unused = lax.scan(
        scan_step, state_in, jnp.arange(total_rows // block_rows, dtype=jnp.int32)
    )
    return state_out


def attention_forward(queries, keys, values, lengths):
    seq_count, query_rows, width_all = queries.shape
    stat_shape = (seq_count, H, query_rows)

    def stat_step(state_in, pieces, first_row):
        row_top, row_sum = state_in
        key_part = pieces[0]
        scores = jnp.where(
            key_mask(lengths, first_row, key_part.shape[1]),
            head_scores(queries, key_part),
            NEG_FILL,
        )
        new_top = jnp.maximum(row_top, jnp.max(scores, axis=3))
        row_sum = row_sum * jnp.exp(row_top - new_top) + jnp.sum(
            jnp.exp(scores - new_top[..., None]), axis=3
        )
        return (new_top, row_sum)

    stat_init = (jnp.full(stat_shape, NEG_FILL, jnp.float32), jnp.zeros(stat_shape, jnp.float32))
    row_top, row_sum = in_blocks(
        stat_step, stat_init, (lax.all_gather(keys, "grp", axis=1, tiled=True),)
    )
    log_total = row_top + jnp.log(row_sum)
    head_shape = (seq_count, query_rows, H, DH)

    def mix_step(state_in, pieces, first_row):
        key_part, value_part = pieces
        key_rows = key_part.shape[1]
        scores = jnp.where(
            key_mask(lengths, first_row, key_rows), head_scores(queries, key_part), NEG_FILL
        )
        softmax_w = jnp.exp(scores - log_total[..., None])
        value_heads = value_part.reshape(seq_count, key_rows, H, DH)
        return state_in + jnp.einsum(
            "shcn,snhd->schd",
            softmax_w.astype(jnp.bfloat16),
            value_heads,
            preferred_element_type=jnp.float32,
        )

    context_heads = in_blocks(
        mix_step,
        jnp.zeros(head_shape, jnp.float32),
        (
            lax.all_gather(keys, "grp", axis=1, tiled=True),
            lax.all_gather(values, "grp", axis=1, tiled=True),
        ),
    )
    return (context_heads, log_total)


def query_grads(queries, keys, values, lengths, log_total, delta_heads, dcontext):
    seq_count, query_rows, width_all = queries.shape
    dcontext_heads = dcontext.reshape(seq_count, query_rows, H, DH)

    def query_grad_step(running, pieces, first_row):
        key_part, value_part = pieces
        key_rows = key_part.shape[1]
        scores = jnp.where(
            key_mask(lengths, first_row, key_rows), head_scores(queries, key_part), NEG_FILL
        )
        softmax_w = jnp.exp(scores - log_total[..., None])
        value_heads = value_part.reshape(seq_count, key_rows, H, DH)
        key_heads = key_part.reshape(seq_count, key_rows, H, DH)
        dweights = jnp.einsum(
            "schd,snhd->shcn", dcontext_heads, value_heads, preferred_element_type=jnp.float32
        )
        dscores = (softmax_w * (dweights - delta_heads[..., None])).astype(jnp.bfloat16)
        return running + jnp.einsum(
            "shcn,snhd->schd", dscores, key_heads, preferred_element_type=jnp.float32
        )

    zero_heads = jnp.zeros((seq_count, query_rows, H, DH), jnp.float32)
    folded = in_blocks(
        query_grad_step,
        zero_heads,
        (
            lax.all_gather(keys, "grp", axis=1, tiled=True),
            lax.all_gather(values, "grp", axis=1, tiled=True),
        ),
    )
    return (folded * DH ** (-0.5)).reshape(seq_count, query_rows, width_all)


def key_grads(queries, keys, values, lengths, log_rows, delta_rows, dcontext):
    seq_count, key_rows, width_all = keys.shape
    log_all, delta_all = (
        lax.all_gather(log_rows, "grp", axis=1, tiled=True),
        lax.all_gather(delta_rows, "grp", axis=1, tiled=True),
    )
    own_mask = key_mask(lengths, lax.axis_index("grp") * key_rows, key_rows)
    value_heads = values.reshape(seq_count, key_rows, H, DH)

    def key_grad_step(running, pieces, first_row):
        query_part, dcontext_part = pieces
        query_count = query_part.shape[1]
        log_part = jnp.transpose(
            lax.dynamic_slice_in_dim(log_all, first_row, query_count, 1), (0, 2, 1)
        )
        delta_part = jnp.transpose(
            lax.dynamic_slice_in_dim(delta_all, first_row, query_count, 1), (0, 2, 1)
        )
        scores = jnp.where(own_mask, head_scores(query_part, keys), NEG_FILL)
        softmax_w = jnp.exp(scores - log_part[..., None])
        dcontext_heads = dcontext_part.reshape(seq_count, query_count, H, DH)
        query_heads = query_part.reshape(seq_count, query_count, H, DH)
        dweights = jnp.einsum(
            "schd,snhd->shcn", dcontext_heads, value_heads, preferred_element_type=jnp.float32
        )
        dscores = (softmax_w * (dweights - delta_part[..., None])).astype(jnp.bfloat16)
        dkey_sum = running[0] + jnp.einsum(
            "shcn,schd->snhd", dscores, query_heads, preferred_element_type=jnp.float32
        )
        dvalue_sum = running[1] + jnp.einsum(
            "shcn,schd->snhd",
            softmax_w.astype(jnp.bfloat16),
            dcontext_heads,
            preferred_element_type=jnp.float32,
        )
        return (dkey_sum, dvalue_sum)

    zero_heads = jnp.zeros((seq_count, key_rows, H, DH), jnp.float32)
    dkey_sum, dvalue_sum = in_blocks(
        key_grad_step,
        (zero_heads, zero_heads),
        (
            lax.all_gather(queries, "grp", axis=1, tiled=True),
            lax.all_gather(dcontext, "grp", axis=1, tiled=True),
        ),
    )
    return (
        (dkey_sum * DH ** (-0.5)).reshape(seq_count, key_rows, width_all),
        dvalue_sum.reshape(seq_count, key_rows, width_all),
    )


def forward(hidden, lengths, project, vectors, clips):
    b_query, b_value, b_out, b_up, b_down, gain_one, shift_one, gain_two, shift_two = vectors
    seq_count = lengths.shape[0]
    query_rows = hidden.shape[0] // seq_count
    width_all = hidden.shape[1]
    entering = hidden if clips is None else jnp.clip(hidden, -clips[0], clips[0])
    inputs = entering.astype(jnp.bfloat16)
    queries = (
        (project(inputs, 0) + b_query)
        .astype(jnp.bfloat16)
        .reshape(seq_count, query_rows, width_all)
    )
    keys = project(inputs, 1).astype(jnp.bfloat16).reshape(seq_count, query_rows, width_all)
    values = (
        (project(inputs, 2) + b_value)
        .astype(jnp.bfloat16)
        .reshape(seq_count, query_rows, width_all)
    )
    context_heads, log_total = attention_forward(queries, keys, values, lengths)
    context_low = context_heads.reshape(hidden.shape).astype(jnp.bfloat16)
    first_sum = hidden + project(context_low, 3) + b_out
    first_norm = layer_norm(first_sum, gain_one, shift_one)
    upper_in = first_norm.astype(jnp.bfloat16)
    gate_pre = project(upper_in, 4) + b_up
    lower_in = gelu_exact(gate_pre).astype(jnp.bfloat16)
    second_sum = first_norm + project(lower_in, 5) + b_down
    output = layer_norm(second_sum, gain_two, shift_two)
    kept_values = (
        inputs,
        queries,
        keys,
        values,
        context_heads,
        log_total,
        context_low,
        first_sum,
        first_norm,
        upper_in,
        gate_pre,
        lower_in,
        second_sum,
    )
    return (output, kept_values)


def backward(grad_output, hidden, lengths, latents, vectors, clips, kept_values):
    (
        inputs,
        queries,
        keys,
        values,
        context_heads,
        log_total,
        context_low,
        first_sum,
        first_norm,
        upper_in,
        gate_pre,
        lower_in,
        second_sum,
    ) = kept_values
    w_query, w_key, w_value, w_out, w_up, w_down = latents
    gain_one, shift_one, gain_two, shift_two = (vectors[5], vectors[6], vectors[7], vectors[8])
    seq_count, query_rows, width_all = queries.shape
    unused, pull_two = jax.vjp(layer_norm, second_sum, gain_two, shift_two)
    dsecond, dgain_two, dshift_two = pull_two(grad_output)
    dsecond_low = dsecond.astype(jnp.bfloat16)
    grad_down = weight_grad(dsecond_low, lower_in)
    dlower = student_back(dsecond_low, w_down)
    unused, pull_gate = jax.vjp(gelu_exact, gate_pre)
    dgate = pull_gate(dlower)[0]
    dgate_low = dgate.astype(jnp.bfloat16)
    grad_up = weight_grad(dgate_low, upper_in)
    dupper = student_back(dgate_low, w_up)
    dfirst = dsecond + dupper
    unused, pull_one = jax.vjp(layer_norm, first_sum, gain_one, shift_one)
    dfirst_sum, dgain_one, dshift_one = pull_one(dfirst)
    dbranch_low = dfirst_sum.astype(jnp.bfloat16)
    grad_out = weight_grad(dbranch_low, context_low)
    dcontext = (
        student_back(dbranch_low, w_out)
        .astype(jnp.bfloat16)
        .reshape(seq_count, query_rows, width_all)
    )
    delta_rows = jnp.sum(
        dcontext.reshape(seq_count, query_rows, H, DH).astype(jnp.float32) * context_heads, axis=3
    )
    dqueries = query_grads(
        queries, keys, values, lengths, log_total, jnp.transpose(delta_rows, (0, 2, 1)), dcontext
    )
    dkeys, dvalues = key_grads(
        queries, keys, values, lengths, jnp.transpose(log_total, (0, 2, 1)), delta_rows, dcontext
    )
    all_rows = seq_count * query_rows
    dqueries_low = dqueries.reshape(all_rows, width_all).astype(jnp.bfloat16)
    dkeys_low = dkeys.reshape(all_rows, width_all).astype(jnp.bfloat16)
    dvalues_low = dvalues.reshape(all_rows, width_all).astype(jnp.bfloat16)
    grad_query = weight_grad(dqueries_low, inputs)
    grad_key = weight_grad(dkeys_low, inputs)
    grad_value = weight_grad(dvalues_low, inputs)
    dinputs = (
        student_back(dqueries_low, w_query)
        + student_back(dkeys_low, w_key)
        + student_back(dvalues_low, w_value)
    )
    unused, pull_input = jax.vjp(lambda tensor: jnp.clip(tensor, -clips[0], clips[0]), hidden)
    grad_hidden = dfirst_sum + pull_input(dinputs)[0]
    weight_parts = (grad_query, grad_key, grad_value, grad_out, grad_up, grad_down)
    vector_parts = (
        jnp.sum(dqueries_low.astype(jnp.float32), axis=0),
        jnp.sum(dvalues_low.astype(jnp.float32), axis=0),
        jnp.sum(dfirst_sum, axis=0),
        jnp.sum(dgate, axis=0),
        jnp.sum(dsecond, axis=0),
        dgain_one,
        dshift_one,
        dgain_two,
        dshift_two,
    )
    return (weight_parts, vector_parts, grad_hidden)


def shards(
    hidden_in,
    seq_lengths,
    latent_query,
    latent_key,
    latent_value,
    latent_out,
    latent_up,
    latent_down,
    bias_query,
    bias_value,
    bias_out,
    bias_up,
    bias_down,
    gain_first,
    shift_first,
    gain_second,
    shift_second,
    clip_input,
    teacher_query,
    teacher_key,
    teacher_value,
    teacher_out,
    teacher_up,
    teacher_down,
    teacher_biases,
    teacher_inner,
    teacher_gains,
    teacher_shifts,
):
    latents = (latent_query, latent_key, latent_value, latent_out, latent_up, latent_down)
    tutors = (teacher_query, teacher_key, teacher_value, teacher_out, teacher_up, teacher_down)
    vectors = (
        bias_query,
        bias_value,
        bias_out,
        bias_up,
        bias_down,
        gain_first,
        shift_first,
        gain_second,
        shift_second,
    )
    tutor_vectors = (
        teacher_biases[0],
        teacher_biases[1],
        teacher_biases[2],
        teacher_inner,
        teacher_biases[3],
        teacher_gains[0],
        teacher_shifts[0],
        teacher_gains[1],
        teacher_shifts[1],
    )
    clips = (clip_input,)
    micro_count, seq_count, local_rows, width_all = hidden_in.shape
    positions = lax.axis_index("grp") * local_rows + jnp.arange(local_rows, dtype=jnp.int32)

    def student_weight(operand, slot_index):
        return student_project(operand, latents[slot_index])

    def tutor_weight(operand, slot_index):
        return teacher_project(operand, tutors[slot_index])

    weight_sums = None
    vector_sums = [jnp.zeros(vector.shape, jnp.float32) for vector in vectors]
    error_sum = jnp.zeros((), jnp.float32)
    outputs_all = []
    grads_all = []
    for micro_index in range(micro_count):
        hidden = (
            hidden_in[micro_index].astype(jnp.float32).reshape(seq_count * local_rows, width_all)
        )
        lengths = seq_lengths[micro_index]
        targets, unused = forward(hidden, lengths, tutor_weight, tutor_vectors, None)
        output, kept_values = forward(hidden, lengths, student_weight, vectors, clips)
        row_keep = (
            (positions[None, :] < lengths[:, None])
            .astype(jnp.float32)
            .reshape(seq_count * local_rows, 1)
        )
        difference = output - targets
        error_sum = error_sum + 0.5 * jnp.sum(row_keep * difference * difference)
        weight_parts, vector_parts, grad_hidden = backward(
            row_keep * difference, hidden, lengths, latents, vectors, clips, kept_values
        )
        if weight_sums is None:
            weight_sums = list(weight_parts)
        else:
            weight_sums = [running + added for running, added in zip(weight_sums, weight_parts)]
        vector_sums = [running + added for running, added in zip(vector_sums, vector_parts)]
        outputs_all.append(output.astype(jnp.bfloat16).reshape(seq_count, local_rows, width_all))
        grads_all.append(grad_hidden.reshape(seq_count, local_rows, width_all))
    weight_sums = (
        lax.psum_scatter(
            weight_sums[0].astype(jnp.bfloat16), "grp", scatter_dimension=0, tiled=True
        ).astype(jnp.float32),
        lax.psum_scatter(
            weight_sums[1].astype(jnp.bfloat16), "grp", scatter_dimension=0, tiled=True
        ).astype(jnp.float32),
        lax.psum_scatter(
            weight_sums[2].astype(jnp.bfloat16), "grp", scatter_dimension=0, tiled=True
        ).astype(jnp.float32),
        lax.psum_scatter(
            weight_sums[3].astype(jnp.bfloat16), "grp", scatter_dimension=0, tiled=True
        ).astype(jnp.float32),
        lax.psum_scatter(
            weight_sums[4].astype(jnp.bfloat16), "grp", scatter_dimension=0, tiled=True
        ).astype(jnp.float32),
        lax.psum_scatter(
            weight_sums[5].astype(jnp.bfloat16), "grp", scatter_dimension=0, tiled=True
        ).astype(jnp.float32),
    )
    vector_shards = (
        lax.psum_scatter(
            vector_sums[0].astype(jnp.bfloat16), "grp", scatter_dimension=0, tiled=True
        ).astype(jnp.float32),
        lax.psum_scatter(
            vector_sums[1].astype(jnp.bfloat16), "grp", scatter_dimension=0, tiled=True
        ).astype(jnp.float32),
        lax.psum_scatter(
            vector_sums[2].astype(jnp.bfloat16), "grp", scatter_dimension=0, tiled=True
        ).astype(jnp.float32),
        lax.psum_scatter(
            vector_sums[3].astype(jnp.bfloat16), "grp", scatter_dimension=0, tiled=True
        ).astype(jnp.float32),
        lax.psum_scatter(
            vector_sums[4].astype(jnp.bfloat16), "grp", scatter_dimension=0, tiled=True
        ).astype(jnp.float32),
        lax.psum_scatter(
            vector_sums[5].astype(jnp.bfloat16), "grp", scatter_dimension=0, tiled=True
        ).astype(jnp.float32),
        lax.psum_scatter(
            vector_sums[6].astype(jnp.bfloat16), "grp", scatter_dimension=0, tiled=True
        ).astype(jnp.float32),
        lax.psum_scatter(
            vector_sums[7].astype(jnp.bfloat16), "grp", scatter_dimension=0, tiled=True
        ).astype(jnp.float32),
        lax.psum_scatter(
            vector_sums[8].astype(jnp.bfloat16), "grp", scatter_dimension=0, tiled=True
        ).astype(jnp.float32),
    )
    totals = (
        lax.psum(weight_sums[0].astype(jnp.bfloat16), "rep").astype(jnp.float32),
        lax.psum(weight_sums[1].astype(jnp.bfloat16), "rep").astype(jnp.float32),
        lax.psum(weight_sums[2].astype(jnp.bfloat16), "rep").astype(jnp.float32),
        lax.psum(weight_sums[3].astype(jnp.bfloat16), "rep").astype(jnp.float32),
        lax.psum(weight_sums[4].astype(jnp.bfloat16), "rep").astype(jnp.float32),
        lax.psum(weight_sums[5].astype(jnp.bfloat16), "rep").astype(jnp.float32),
        lax.psum(vector_shards[0].astype(jnp.bfloat16), "rep").astype(jnp.float32),
        lax.psum(vector_shards[1].astype(jnp.bfloat16), "rep").astype(jnp.float32),
        lax.psum(vector_shards[2].astype(jnp.bfloat16), "rep").astype(jnp.float32),
        lax.psum(vector_shards[3].astype(jnp.bfloat16), "rep").astype(jnp.float32),
        lax.psum(vector_shards[4].astype(jnp.bfloat16), "rep").astype(jnp.float32),
        lax.psum(vector_shards[5].astype(jnp.bfloat16), "rep").astype(jnp.float32),
        lax.psum(vector_shards[6].astype(jnp.bfloat16), "rep").astype(jnp.float32),
        lax.psum(vector_shards[7].astype(jnp.bfloat16), "rep").astype(jnp.float32),
        lax.psum(vector_shards[8].astype(jnp.bfloat16), "rep").astype(jnp.float32),
    )
    error_all = lax.psum(error_sum, ("rep", "grp"))
    entries = (
        micro_count
        * seq_count
        * lax.axis_size("rep")
        * local_rows
        * lax.axis_size("grp")
        * width_all
    )
    distill_loss = error_all / entries
    return (
        jnp.stack(outputs_all),
        distill_loss,
        jnp.stack(grads_all),
        totals[0],
        totals[1],
        totals[2],
        totals[3],
        totals[4],
        totals[5],
        totals[6],
        totals[7],
        totals[8],
        totals[9],
        totals[10],
        totals[11],
        totals[12],
        totals[13],
        totals[14],
    )


def solution(mesh):
    return jax.shard_map(
        shards,
        mesh=mesh,
        in_specs=(
            P(None, "rep", "grp", None),
            P(None, "rep"),
            P("grp", None),
            P("grp", None),
            P("grp", None),
            P("grp", None),
            P("grp", None),
            P("grp", None),
            P(),
            P(),
            P(),
            P(),
            P(),
            P(),
            P(),
            P(),
            P(),
            P(),
            P("grp", None),
            P("grp", None),
            P("grp", None),
            P("grp", None),
            P("grp", None),
            P("grp", None),
            P(),
            P(),
            P(),
            P(),
        ),
        out_specs=(
            P(None, "rep", "grp", None),
            P(),
            P(None, "rep", "grp", None),
            P("grp", None),
            P("grp", None),
            P("grp", None),
            P("grp", None),
            P("grp", None),
            P("grp", None),
            P("grp"),
            P("grp"),
            P("grp"),
            P("grp"),
            P("grp"),
            P("grp"),
            P("grp"),
            P("grp"),
            P("grp"),
        ),
        check_vma=False,
    )
```

profile of v0, /device:TPU:0, one launch (start us, length us, event | category | flops | bytes accessed | tf_op | source)
XLA Modules:
  0.0 1162.6 jit_solution(15904432215581982177)
XLA Ops:
  16.3 19.4 %all-gather.39.cloned.1.call-done = bf16[768,768]{1,0:T(8,128)(2,1)} async-done(((bf16[96,768]{1,0:T(8,128)(2,1)}), bf16[768,768]{1,0:T(8,128)(2,1)}) %all-gather.39.cloned.1.call-update) | async-done | bytes 1179664 | tf_op jit(solution)/shard_map/all_gather | solution.py:39
  42.1 18.2 %all-gather.41.cloned.1.call-done = bf16[768,768]{1,0:T(8,128)(2,1)} async-done(((bf16[96,768]{1,0:T(8,128)(2,1)}), bf16[768,768]{1,0:T(8,128)(2,1)}) %all-gather.41.cloned.1.call-update) | async-done | bytes 1179664 | tf_op jit(solution)/shard_map/all_gather | solution.py:39
  66.7 17.7 %all-gather.53.cloned.1.call-done = bf16[768,768]{1,0:T(8,128)(2,1)} async-done(((bf16[96,768]{1,0:T(8,128)(2,1)}), bf16[768,768]{1,0:T(8,128)(2,1)}) %all-gather.53.cloned.1.call-update) | async-done | bytes 1179664 | tf_op jit(solution)/shard_map/all_gather | solution.py:47
  90.2 18.2 %all-gather.51.cloned.1.call-done = bf16[768,768]{1,0:T(8,128)(2,1)} async-done(((bf16[96,768]{1,0:T(8,128)(2,1)}), bf16[768,768]{1,0:T(8,128)(2,1)}) %all-gather.51.cloned.1.call-update) | async-done | bytes 1179664 | tf_op jit(solution)/shard_map/all_gather | solution.py:47
  120.6 12.3 %all-gather.43.cloned.1.call-done = bf16[768,768]{1,0:T(8,128)(2,1)} async-done(((bf16[96,768]{1,0:T(8,128)(2,1)}), bf16[768,768]{1,0:T(8,128)(2,1)}) %all-gather.43.cloned.1.call-update) | async-done | bytes 1179664 | tf_op jit(solution)/shard_map/all_gather | solution.py:39
  138.2 18.7 %all-gather.45.cloned.1.call-done = bf16[768,768]{1,0:T(8,128)(2,1)} async-done(((bf16[96,768]{1,0:T(8,128)(2,1)}), bf16[768,768]{1,0:T(8,128)(2,1)}) %all-gather.45.cloned.1.call-update) | async-done | bytes 1179664 | tf_op jit(solution)/shard_map/all_gather | solution.py:39
  159.1 21.9 %all-gather.55.cloned.1.call-done = bf16[768,768]{1,0:T(8,128)(2,1)} async-done(((bf16[96,768]{1,0:T(8,128)(2,1)}), bf16[768,768]{1,0:T(8,128)(2,1)}) %all-gather.55.cloned.1.call-update) | async-done | bytes 1179664 | tf_op jit(solution)/shard_map/all_gather | solution.py:47
  186.2 21.8 %all-gather.67.cloned.1.call-done = bf16[1024,768]{1,0:T(8,128)(2,1)} async-done(((bf16[128,768]{1,0:T(8,128)(2,1)}), bf16[1024,768]{1,0:T(8,128)(2,1)}) %all-gather.67.cloned.1.call-update) | async-done | bytes 1572880 | tf_op jit(solution)/shard_map/all_gather | solution.py:148
  210.9 24.0 %all-gather.63.cloned.1.call-done = bf16[1024,768]{1,0:T(8,128)(2,1)} async-done(((bf16[128,768]{1,0:T(8,128)(2,1)}), bf16[1024,768]{1,0:T(8,128)(2,1)}) %all-gather.63.cloned.1.call-update) | async-done | bytes 1572880 | tf_op jit(solution)/shard_map/all_gather | solution.py:148
  237.5 24.1 %all-gather.69.cloned.1.call-done = bf16[1024,768]{1,0:T(8,128)(2,1)} async-done(((bf16[128,768]{1,0:T(8,128)(2,1)}), bf16[1024,768]{1,0:T(8,128)(2,1)}) %all-gather.69.cloned.1.call-update) | async-done | bytes 1572880 | tf_op jit(solution)/shard_map/all_gather | solution.py:147
  263.3 24.5 %all-gather.65.cloned.1.call-done = bf16[1024,768]{1,0:T(8,128)(2,1)} async-done(((bf16[128,768]{1,0:T(8,128)(2,1)}), bf16[1024,768]{1,0:T(8,128)(2,1)}) %all-gather.65.cloned.1.call-update) | async-done | bytes 1572880 | tf_op jit(solution)/shard_map/all_gather | solution.py:147
  290.1 9.9 while.146
  300.4 9.9 while.144
  317.6 13.8 %while.148 = (s32[]{:T(128)}, f32[1,12,128]{2,1,0:T(8,128)S(1)}, f32[1,12,128]{2,1,0:T(8,128)}, s32[2]{0:T(128)}, s32[1,1]{1,0:T(1,128)}, /*index=5*/bf16[1,1024...) while((s32[]{:T(128)}, f32[1,12,128]{2,1,0:T(8,128)S(1)}, ...), condition=%wide.region_29.30_spmd.clone, body=%wide.region_26.29_spmd.clone.sunk | while | flops 106177032 | bytes 8978174 | solution.py:97
  331.5 9.8 all-gather.77.cloned.1.call-done
  344.4 13.8 %while.150 = (s32[]{:T(128)}, f32[1,12,128]{2,1,0:T(8,128)S(1)}, f32[1,12,128]{2,1,0:T(8,128)}, s32[2]{0:T(128)}, s32[1,1]{1,0:T(1,128)}, /*index=5*/bf16[1,1024...) while((s32[]{:T(128)}, f32[1,12,128]{2,1,0:T(8,128)S(1)}, ...), condition=%wide.region_40.41_spmd.clone, body=%wide.region_37.40_spmd.clone.sunk | while | flops 106177032 | bytes 8978174 | solution.py:97
  359.6 8.5 all-gather.75.cloned.1.call-done
  368.6 26.2 %while.151 = (s32[]{:T(128)}, f32[1,128,12,64]{1,3,2,0:T(8,128)}, s32[2]{0:T(128)}, bf16[1,1024,768]{2,1,0:T(8,128)(2,1)}, s32[1,1]{1,0:T(1,128)}, /*index=5*/bf...) while((s32[]{:T(128)}, f32[1,128,12,64]{1,3,2,0:T(8,128)}, ...), condition=%wide.region_42.43_spmd.clone, body=%wide.region_41.42_spmd.clone.sunk | while | flops 204669952 | bytes 7306477 | solution.py:97
  400.6 17.5 %all-gather.71.cloned.1.call-done = bf16[1024,768]{1,0:T(8,128)(2,1)} async-done(((bf16[128,768]{1,0:T(8,128)(2,1)}), bf16[1024,768]{1,0:T(8,128)(2,1)}) %all-gather.71.cloned.1.call-update) | async-done | bytes 1572880 | tf_op jit(solution)/shard_map/all_gather | solution.py:148
  418.1 25.5 %while.149 = (s32[]{:T(128)}, f32[1,128,12,64]{1,3,2,0:T(8,128)}, s32[2]{0:T(128)S(1)}, bf16[1,1024,768]{2,1,0:T(8,128)(2,1)}, s32[1,1]{1,0:T(1,128)}, /*index=5...) while((s32[]{:T(128)}, f32[1,128,12,64]{1,3,2,0:T(8,128)}, ...), condition=%wide.region_31.32_spmd.clone, body=%wide.region_30.31_spmd.clone.sunk | while | flops 204669952 | bytes 7306477 | solution.py:97
  449.3 18.1 %while.147 = (s32[]{:T(128)}, f32[1,128,12,64]{1,3,2,0:T(8,128)}, s32[2]{0:T(128)}, bf16[1,1024,768]{1,2,0:T(8,128)(2,1)}, s32[1,1]{1,0:T(1,128)}, /*index=5*/bf...) while((s32[]{:T(128)}, f32[1,128,12,64]{1,3,2,0:T(8,128)}, ...), condition=%wide.region_21.22_spmd.clone, body=%wide.region_20.21_spmd.clone.sunk | while | flops 204669952 | bytes 5709005 | solution.py:97
  470.2 26.8 %while.145 = (s32[]{:T(128)}, f32[1,128,12,64]{1,3,2,0:T(8,128)}, s32[2]{0:T(128)}, bf16[1,1024,768]{1,2,0:T(8,128)(2,1)}, s32[1,1]{1,0:T(1,128)}, /*index=5*/bf...) while((s32[]{:T(128)}, f32[1,128,12,64]{1,3,2,0:T(8,128)}, ...), condition=%wide.region_8.9_spmd.clone, body=%wide.region_7.8_spmd.clone.sunk | while | flops 204669952 | bytes 5733609 | solution.py:97
  504.5 18.4 %all-gather.61.cloned.1.call-done = bf16[768,3072]{1,0:T(8,128)(2,1)} async-done(((bf16[96,3072]{1,0:T(8,128)(2,1)}), bf16[768,3072]{1,0:T(8,128)(2,1)}) %all-gather.61.cloned.1.call-update) | async-done | bytes 4718608 | tf_op jit(solution)/shard_map/all_gather | solution.py:47
  522.9 8.5 fusion.262
  534.4 8.6 fusion.268
  545.3 29.8 %all-gather.47.cloned.1.call-done = bf16[3072,768]{1,0:T(8,128)(2,1)} async-done(((bf16[384,768]{1,0:T(8,128)(2,1)}), bf16[3072,768]{1,0:T(8,128)(2,1)}) %all-gather.47.cloned.1.call-update) | async-done | bytes 4718608 | tf_op jit(solution)/shard_map/all_gather | solution.py:39
  579.1 48.1 %all-gather.49.cloned.1.call-done = bf16[768,3072]{1,0:T(8,128)(2,1)} async-done(((bf16[96,3072]{1,0:T(8,128)(2,1)}), bf16[768,3072]{1,0:T(8,128)(2,1)}) %all-gather.49.cloned.1.call-update) | async-done | bytes 4718608 | tf_op jit(solution)/shard_map/all_gather | solution.py:39
  666.9 15.3 %all_gather.141 = f32[1,1024,12]{1,2,0:T(8,128)} all-gather(f32[1,128,12]{1,2,0:T(8,128)} %bitcast.35), channel_id=1, replica_groups=mesh['rep'=4,'grp'=8] {'grp'}, dimensions={1}, use_global_device_ids=true | all-gather | bytes 55296 | tf_op jit(solution)/shard_map/all_gather | solution.py:190
  682.2 15.2 %all_gather.137 = f32[1,1024,12]{1,2,0:T(8,128)} all-gather(f32[1,128,12]{1,2,0:T(8,128)S(1)} %bitcast.734), channel_id=1, replica_groups=mesh['rep'=4,'grp'=8] {'grp'}, dimensions={1}, use_global_device_ids=true | all-gather | bytes 55296 | tf_op jit(solution)/shard_map/all_gather | solution.py:190
  705.6 15.1 %all-gather.10 = f32[1024,12]{0,1:T(8,128)} all-gather(f32[128,12]{0,1:T(8,128)S(1)} %multiply_reduce_fusion.7), channel_id=12, replica_groups=mesh['rep'=4,'grp'=8] {'grp'}, dimensions={0}, use_global_device_ids=true | all-gather | bytes 55296 | tf_op jit(solution)/shard_map/all_gather | solution.py:191
  722.4 15.3 %all-gather.13 = f32[1024,12]{0,1:T(8,128)} all-gather(f32[128,12]{0,1:T(8,128)} %multiply_reduce_fusion.4), channel_id=15, replica_groups=mesh['rep'=4,'grp'=8] {'grp'}, dimensions={0}, use_global_device_ids=true | all-gather | bytes 55296 | tf_op jit(solution)/shard_map/all_gather | solution.py:191
  738.2 26.3 %while.152 = (s32[]{:T(128)}, f32[1,128,12,64]{1,3,2,0:T(8,128)}, s32[2]{0:T(128)}, bf16[1,1024,768]{1,2,0:T(8,128)(2,1)S(1)}, s32[1,1]{1,0:T(1,128)}, /*index=5...) while((s32[]{:T(128)}, f32[1,128,12,64]{1,3,2,0:T(8,128)}, ...), condition=%wide.region_55.56_spmd.clone, body=%wide.region_54.55_spmd.clone.sunk | while | flops 306906112 | bytes 16135417 | solution.py:97
  746.7 4.6 fusion.453
  759.7 4.8 fusion.453
  770.8 21.9 %while.154 = (s32[]{:T(128)}, f32[1,128,12,64]{1,3,2,0:T(8,128)}, s32[2]{0:T(128)}, bf16[1,1024,768]{1,2,0:T(8,128)(2,1)S(1)}, s32[1,1]{1,0:T(1,128)}, /*index=5...) while((s32[]{:T(128)}, f32[1,128,12,64]{1,3,2,0:T(8,128)}, ...), condition=%wide.region_64.66_spmd.clone, body=%wide.region_63.65_spmd.clone.sunk | while | flops 306906112 | bytes 12989661 | solution.py:97
  798.3 35.5 %while.153 = (s32[]{:T(128)}, f32[1,128,12,64]{1,3,2,0:T(8,128)}, f32[1,128,12,64]{1,3,2,0:T(8,128)}, s32[2]{0:T(128)}, bf16[1,1024,768]{2,1,0:T(8,128)(2,1)}, /...) while((s32[]{:T(128)}, f32[1,128,12,64]{1,3,2,0:T(8,128)}, ...), condition=%wide.region_57.58_spmd.clone, body=%wide.region_56.57_spmd.clone.sunk | while | flops 410910976 | bytes 21013104 | solution.py:97
  808.4 4.5 fusion.462
  826.0 4.7 fusion.462
  834.3 35.4 %while.155 = (s32[]{:T(128)}, f32[1,128,12,64]{1,3,2,0:T(8,128)}, f32[1,128,12,64]{1,3,2,0:T(8,128)}, s32[2]{0:T(128)}, bf16[1,1024,768]{2,1,0:T(8,128)(2,1)}, /...) while((s32[]{:T(128)}, f32[1,128,12,64]{1,3,2,0:T(8,128)}, ...), condition=%wide.region_66.68_spmd.clone, body=%wide.region_65.67_spmd.clone.sunk | while | flops 410910976 | bytes 21013104 | solution.py:97
  844.3 4.5 fusion.479
  861.9 4.7 fusion.479
  901.5 5.1 reduce-scatter.11.cloned.1.call-done
  906.6 33.9 %reduce-scatter.9.cloned.1.call-done = bf16[96,768]{1,0:T(8,128)(2,1)} async-done(((bf16[768,768]{1,0:T(8,128)(2,1)}), bf16[96,768]{1,0:T(8,128)(2,1)}) %reduce-scatter.9.cloned.1.call-update) | async-done | bytes 147472 | tf_op jit(solution)/shard_map/reduce_scatter | solution.py:458
  940.5 55.6 %reduce-scatter.17.cloned.1.call-done = bf16[96,3072]{1,0:T(8,128)(2,1)} async-done(((bf16[768,3072]{1,0:T(8,128)(2,1)}), bf16[96,3072]{1,0:T(8,128)(2,1)}) %reduce-scatter.17.cloned.1.call-update) | async-done | bytes 589840 | tf_op jit(solution)/shard_map/reduce_scatter | solution.py:470
  996.2 55.5 %reduce-scatter.15.cloned.1.call-done = bf16[384,768]{1,0:T(8,128)(2,1)} async-done(((bf16[3072,768]{1,0:T(8,128)(2,1)}), bf16[384,768]{1,0:T(8,128)(2,1)}) %reduce-scatter.15.cloned.1.call-update) | async-done | bytes 589840 | tf_op jit(solution)/shard_map/reduce_scatter | solution.py:467
  1053.6 38.0 %psum.112 = f32[]{:T(128)} all-reduce(f32[]{:T(128)S(6)} %add.817), channel_id=1, replica_groups=mesh['rep'=4,'grp'=8] {'rep','grp'}, use_global_device_ids=true, to_apply=%region_48.49 | all-reduce | flops 1 | bytes 8 | tf_op jit(solution)/shard_map/psum | solution.py:520
  1095.5 26.8 %all-reduce.9 = (bf16[768]{0:T(1024)(128)(2,1)S(1)}, bf16[768]{0:T(1024)(128)(2,1)S(1)}, bf16[768]{0:T(1024)(128)(2,1)S(1)}, bf16[3072]{0:T(1024)(128)(2,1)S(1)}...) all-reduce(bf16[768]{0:T(1024)(128)(2,1)S(1)} %convert_element_type, ...), channel_id=22, replica_groups=mesh['rep'=4,'grp'=8] {'grp'}, use_global_device_ids=true, to_apply=%region_81.83.clone | all-reduce | flops 9216 | bytes 36864
  1123.0 10.1 all-reduce.10
  (806 shorter events, 432.2 us)
Async XLA Ops:
  7.2 28.4 %all-gather.39.cloned.1.call-start = ((), (), s32[]{:S(2)}) async-start(), calls=%async_computation.6 | async-start | bytes 1327104 | tf_op jit(solution)/shard_map/all_gather | solution.py:39
  9.0 51.4 %all-gather.41.cloned.1.call-start = ((), (), s32[]{:S(2)}) async-start(), calls=%async_computation.7 | async-start | bytes 1327104 | tf_op jit(solution)/shard_map/all_gather | solution.py:39
  10.7 73.8 %all-gather.53.cloned.1.call-start = ((), (), s32[]{:S(2)}) async-start(), calls=%async_computation.13 | async-start | bytes 1327104 | tf_op jit(solution)/shard_map/all_gather | solution.py:47
  11.4 97.0 %all-gather.51.cloned.1.call-start = ((), (), s32[]{:S(2)}) async-start(), calls=%async_computation.12 | async-start | bytes 1327104 | tf_op jit(solution)/shard_map/all_gather | solution.py:47
  12.0 120.9 %all-gather.43.cloned.1.call-start = ((), (), s32[]{:S(2)}) async-start(), calls=%async_computation.8 | async-start | bytes 1327104 | tf_op jit(solution)/shard_map/all_gather | solution.py:39
  13.7 143.2 %all-gather.45.cloned.1.call-start = ((), (), s32[]{:S(2)}) async-start(), calls=%async_computation.9 | async-start | bytes 1327104 | tf_op jit(solution)/shard_map/all_gather | solution.py:39
  15.4 165.5 %all-gather.55.cloned.1.call-start = ((), (), s32[]{:S(2)}) async-start(), calls=%async_computation.14 | async-start | bytes 1327104 | tf_op jit(solution)/shard_map/all_gather | solution.py:47
  16.2 191.9 %all-gather.67.cloned.1.call-start = ((), (), s32[]{:S(2)}) async-start(), calls=%async_computation.26 | async-start | bytes 1769472 | tf_op jit(solution)/shard_map/all_gather | solution.py:148
  16.2 120.8 %copy-start.80 = (f32[768]{0:T(1024)}, f32[768]{0:T(1024)S(1)}, u32[]{:S(2)}) copy-start(f32[768]{0:T(1024)S(1)} %neg.24) | copy-start | bytes 9220
  40.3 194.6 %all-gather.63.cloned.1.call-start = ((), (), s32[]{:S(2)}) async-start(), calls=%async_computation.24 | async-start | bytes 1769472 | tf_op jit(solution)/shard_map/all_gather | solution.py:148
  42.0 219.5 %all-gather.69.cloned.1.call-start = ((), (), s32[]{:S(2)}) async-start(), calls=%async_computation.27 | async-start | bytes 1769472 | tf_op jit(solution)/shard_map/all_gather | solution.py:147
  65.0 222.9 %all-gather.65.cloned.1.call-start = ((), (), s32[]{:S(2)}) async-start(), calls=%async_computation.25 | async-start | bytes 1769472 | tf_op jit(solution)/shard_map/all_gather | solution.py:147
  66.7 247.8 %all-gather.73.cloned.1.call-start = ((), (), s32[]{:S(2)}) async-start(), calls=%async_computation.29 | async-start | bytes 1769472 | tf_op jit(solution)/shard_map/all_gather | solution.py:147
  87.0 254.4 %all-gather.77.cloned.1.call-start = ((), (), s32[]{:S(2)}) async-start(), calls=%async_computation.31 | async-start | bytes 1769472 | tf_op jit(solution)/shard_map/all_gather | solution.py:147
  89.5 278.5 %all-gather.75.cloned.1.call-start = ((), (), s32[]{:S(2)}) async-start(), calls=%async_computation.30 | async-start | bytes 1769472 | tf_op jit(solution)/shard_map/all_gather | solution.py:148
  111.0 285.5 %all-gather.57.cloned.1.call-start = ((), (), s32[]{:S(2)}) async-start(), calls=%async_computation.15 | async-start | bytes 1327104 | tf_op jit(solution)/shard_map/all_gather | solution.py:47
  111.6 306.5 %all-gather.71.cloned.1.call-start = ((), (), s32[]{:S(2)}) async-start(), calls=%async_computation.28 | async-start | bytes 1769472 | tf_op jit(solution)/shard_map/all_gather | solution.py:148
  114.3 390.2 %all-gather.59.cloned.1.call-start = ((), (), s32[]{:S(2)}) async-start(), calls=%async_computation.16 | async-start | bytes 5308416 | tf_op jit(solution)/shard_map/all_gather | solution.py:47
  114.8 408.1 %all-gather.61.cloned.1.call-start = ((), (), s32[]{:S(2)}) async-start(), calls=%async_computation.17 | async-start | bytes 5308416 | tf_op jit(solution)/shard_map/all_gather | solution.py:47
  115.5 459.7 %all-gather.47.cloned.1.call-start = ((), (), s32[]{:S(2)}) async-start(), calls=%async_computation.10 | async-start | bytes 5308416 | tf_op jit(solution)/shard_map/all_gather | solution.py:39
  116.4 510.7 %all-gather.49.cloned.1.call-start = ((), (), s32[]{:S(2)}) async-start(), calls=%async_computation.11 | async-start | bytes 5308416 | tf_op jit(solution)/shard_map/all_gather | solution.py:39
  117.4 680.3 %all-gather.79.cloned.1.call-start = ((), (), s32[]{:S(2)}) async-start(), calls=%async_computation.32 | async-start | bytes 1769472 | tf_op jit(solution)/shard_map/all_gather | solution.py:229
  159.1 638.7 %all-gather.81.cloned.1.call-start = ((), (), s32[]{:S(2)}) async-start(), calls=%async_computation.33 | async-start | bytes 1769472 | tf_op jit(solution)/shard_map/all_gather | solution.py:230
  500.6 154.5 %copy-start.95 = (f32[128]{0:T(128)}, f32[128]{0:T(128)S(1)}, u32[]{:S(2)}) copy-start(f32[128]{0:T(128)S(1)} %broadcast_multiply_fusion.13) | copy-start | bytes 1540
  502.5 152.7 %copy-start.97 = (f32[128]{0:T(128)}, f32[128]{0:T(128)S(1)}, u32[]{:S(2)}) copy-start(f32[128]{0:T(128)S(1)} %broadcast_multiply_fusion.11) | copy-start | bytes 1540
  659.1 174.7 %all-gather.83.cloned.1.call-start = ((), (), s32[]{:S(2)}) async-start(), calls=%async_computation.34 | async-start | bytes 1769472 | tf_op jit(solution)/shard_map/all_gather | solution.py:229
  659.8 173.9 %all-gather.85.cloned.1.call-start = ((), (), s32[]{:S(2)}) async-start(), calls=%async_computation.35 | async-start | bytes 1769472 | tf_op jit(solution)/shard_map/all_gather | solution.py:230
  704.5 197.0 %reduce-scatter.13.cloned.1.call-start = ((), (), s32[]{:S(2)}) async-start(), calls=%async_computation.21 | async-start | bytes 1327104 | tf_op jit(solution)/shard_map/reduce_scatter | solution.py:464
  770.2 131.3 %reduce-scatter.7.cloned.1.call-start = ((), (), s32[]{:S(2)}) async-start(), calls=%async_computation.18 | async-start | bytes 1327104 | tf_op jit(solution)/shard_map/reduce_scatter | solution.py:455
  797.7 108.9 %reduce-scatter.11.cloned.1.call-start = ((), (), s32[]{:S(2)}) async-start(), calls=%async_computation.20 | async-start | bytes 1327104 | tf_op jit(solution)/shard_map/reduce_scatter | solution.py:461
  875.2 65.3 %reduce-scatter.9.cloned.1.call-start = ((), (), s32[]{:S(2)}) async-start(), calls=%async_computation.19 | async-start | bytes 1327104 | tf_op jit(solution)/shard_map/reduce_scatter | solution.py:458
  878.4 117.8 %reduce-scatter.17.cloned.1.call-start = ((), (), s32[]{:S(2)}) async-start(), calls=%async_computation.23 | async-start | bytes 5308416 | tf_op jit(solution)/shard_map/reduce_scatter | solution.py:470
  884.8 166.9 %reduce-scatter.15.cloned.1.call-start = ((), (), s32[]{:S(2)}) async-start(), calls=%async_computation.22 | async-start | bytes 5308416 | tf_op jit(solution)/shard_map/reduce_scatter | solution.py:467
  891.4 252.8 %all-reduce.14.cloned.1.call-start = ((), (), s32[]{:S(2)}) async-start(), calls=%async_computation.36 | async-start | bytes 3538944 | tf_op jit(solution)/shard_map/psum | solution.py:504
  901.4 193.9 %copy-start.90 = (f32[12,64]{1,0:T(8,128)S(1)}, f32[12,64]{1,0:T(8,128)}, u32[]{:S(2)}) copy-start(f32[12,64]{1,0:T(8,128)} %get-tuple-element.1508) | copy-start | bytes 9220
  901.4 193.9 %copy-start.91 = (f32[12,64]{1,0:T(8,128)S(1)}, f32[12,64]{1,0:T(8,128)}, u32[]{:S(2)}) copy-start(f32[12,64]{1,0:T(8,128)} %get-tuple-element.1506) | copy-start | bytes 9220
  901.4 194.0 %copy-start.94 = (bf16[3072]{0:T(1024)(128)(2,1)S(1)}, bf16[3072]{0:T(1024)(128)(2,1)}, u32[]{:S(2)}) copy-start(bf16[3072]{0:T(1024)(128)(2,1)} %add_convert_fusion.10) | copy-start | bytes 18436
  901.4 194.0 %copy-start.122 = (bf16[768]{0:T(1024)(128)(2,1)S(1)}, bf16[768]{0:T(1024)(128)(2,1)}, u32[]{:S(2)}) copy-start(bf16[768]{0:T(1024)(128)(2,1)} %add_convert_fusion.14) | copy-start | bytes 4612
  901.4 194.0 %copy-start.123 = (bf16[768]{0:T(1024)(128)(2,1)S(1)}, bf16[768]{0:T(1024)(128)(2,1)}, u32[]{:S(2)}) copy-start(bf16[768]{0:T(1024)(128)(2,1)} %add_convert_fusion.13) | copy-start | bytes 4612
  901.4 194.0 %copy-start.124 = (bf16[768]{0:T(1024)(128)(2,1)S(1)}, bf16[768]{0:T(1024)(128)(2,1)}, u32[]{:S(2)}) copy-start(bf16[768]{0:T(1024)(128)(2,1)} %add_convert_fusion.17) | copy-start | bytes 4612
  901.4 194.0 %copy-start.125 = (bf16[768]{0:T(1024)(128)(2,1)S(1)}, bf16[768]{0:T(1024)(128)(2,1)}, u32[]{:S(2)}) copy-start(bf16[768]{0:T(1024)(128)(2,1)} %add_convert_fusion.16) | copy-start | bytes 4612
  901.4 194.0 %copy-start.126 = (bf16[768]{0:T(1024)(128)(2,1)S(1)}, bf16[768]{0:T(1024)(128)(2,1)}, u32[]{:S(2)}) copy-start(bf16[768]{0:T(1024)(128)(2,1)} %add_convert_fusion.15) | copy-start | bytes 4612
  901.5 194.0 %copy-start.127 = (bf16[768]{0:T(1024)(128)(2,1)S(1)}, bf16[768]{0:T(1024)(128)(2,1)}, u32[]{:S(2)}) copy-start(bf16[768]{0:T(1024)(128)(2,1)} %add_convert_fusion.18) | copy-start | bytes 4612
  1051.6 86.2 %copy-start.64 = (f32[128,768]{1,0:T(8,128)S(1)}, f32[128,768]{1,0:T(8,128)}, u32[]{:S(2)}) copy-start(f32[128,768]{1,0:T(8,128)} %fusion.244) | copy-start | bytes 1179652
  1051.6 86.2 %copy-start.87 = (f32[768]{0:T(1024)S(1)}, f32[768]{0:T(1024)}, u32[]{:S(2)}) copy-start(f32[768]{0:T(1024)} %copy-done.86) | copy-start | bytes 9220
  1051.7 87.1 %copy-start.61 = (bf16[1,128,12,64]{1,3,2,0:T(8,128)(2,1)S(1)}, bf16[1,128,12,64]{1,3,2,0:T(8,128)(2,1)}, u32[]{:S(2)}) copy-start(bf16[1,128,12,64]{1,3,2,0:T(8,128)(2,1)} %copy-done.60) | copy-start | bytes 589828
  1051.7 87.1 %copy-start.139 = (f32[768]{0:T(1024)S(1)}, f32[768]{0:T(1024)}, u32[]{:S(2)}) copy-start(f32[768]{0:T(1024)} %copy-done.138) | copy-start | bytes 9220
  1051.7 87.1 %copy-start.151 = (f32[128]{0:T(128)S(1)}, f32[128]{0:T(128)}, u32[]{:S(2)}) copy-start(f32[128]{0:T(128)} %copy-done.148) | copy-start | bytes 1540
  (169 other events, 1069.6 us)
Sparse Core Ops, SparseCore 0:
  10.3 25.3 all-gather.38
  37.9 22.4 all-gather.40
  62.0 22.4 all-gather.52
  85.9 22.4 all-gather.50
  110.5 22.4 all-gather.42
  134.4 22.4 all-gather.44
  158.5 22.4 all-gather.54
  183.2 24.8 all-gather.66
  210.3 24.5 all-gather.62
  236.9 24.5 all-gather.68
  263.2 24.5 all-gather.64
  289.9 24.5 all-gather.72
  316.7 24.5 all-gather.76
  343.4 24.6 all-gather.74
  369.5 22.1 all-gather.56
  393.3 24.8 all-gather.70
  419.6 51.2 all-gather.58
  472.4 50.5 all-gather.60
  524.6 50.5 all-gather.46
  576.6 50.4 all-gather.48
  628.8 23.8 all-gather.78
  659.2 24.2 all-gather.80
  685.2 24.4 all-gather.82
  711.8 24.9 all-gather.84
  770.4 31.5 reduce-scatter.12
  804.6 30.9 reduce-scatter.6
  875.3 31.2 reduce-scatter.10
  909.5 31.0 reduce-scatter.8
  942.8 53.2 reduce-scatter.16
  998.3 53.2 reduce-scatter.14
  1055.4 63.9 all-reduce.13
where the time goes:
time: 1170 us; the launch traced here: 1160 us
  waiting for transfers between devices  512 us (44%)
  matrix products  205 us (18%)
  local copies, waits for them, and re-layouts  145 us (12%)
  blocking collectives  136 us (12%)
  other arithmetic  116 us (10%)
  loops' own time  25.1 us (2%)
  between operations  21.6 us (2%)
    all_gather x6, waiting for transfers between devices, student_project(): lax.all_gather(latent.astype(jnp.bfloat16), 'grp', axis=0, tiled=True)  147 us
    all_gather x6, waiting for transfers between devices, teacher_project(): lax.all_gather(weight, 'grp', axis=0, tiled=True)  76.2 us
    all_gather x4, waiting for transfers between devices, attention_forward(): lax.all_gather(values, 'grp', axis=1, tiled=True)  71.8 us
    dynamic_slice x40, local copies, waits for them, and re-layouts, scan_step(): lax.dynamic_slice_in_dim(member, offset, block_rows, 1)  62.7 us
    all_gather x4, waiting for transfers between devices, attention_forward(): lax.all_gather(keys, 'grp', axis=1, tiled=True)  62.7 us
    dot_general x22, matrix products, times_rows(): lax.dot_general(operand, weight, (((1,), (1,)), ((), ())), preferred_elem...  57.5 us
    reduce_scatter x1, waiting for transfers between devices, shards(): lax.psum_scatter(weight_sums[5].astype(jnp.bfloat16), 'grp', scatter_dime...  55.6 us
    reduce_scatter x1, waiting for transfers between devices, shards(): lax.psum_scatter(weight_sums[4].astype(jnp.bfloat16), 'grp', scatter_dime...  55.5 us
  transfers between devices with their start and end apart: 31, of which 22 were waited for; matrix products, arithmetic and copies ran while one was open for 38% of the time, Pallas kernels for 0%

commit v1 on v0

--- a/solution.py
+++ b/solution.py
@@ -1,6 +1,10 @@
+import functools
+
 import jax
 import jax.numpy as jnp
 from jax import lax
+from jax.experimental import pallas as pl
+from jax.experimental.pallas import tpu as pltpu
 from jax.sharding import PartitionSpec as P
 
 H = 12
@@ -549,9 +553,836 @@
     )
 
 
+F32 = jnp.float32
+BF16 = jnp.bfloat16
+ANY = pl.BlockSpec(memory_space=pl.ANY)
+VM = pl.BlockSpec(memory_space=pltpu.VMEM)
+SM = pl.BlockSpec(memory_space=pltpu.SMEM)
+VMEM_LIMIT = 60 * 1024 * 1024
+
+I_CORE, I_REP, I_Z, I_LEN, I_RING = 0, 1, 2, 3, 4
+
+
+def z_ring(line):
+    return list(range(0, line, 2)) + list(range(1, line, 2))[::-1]
+
+
+def dims(a, b, ca, cb):
+    return lax.dot_general(a, b, (((ca,), (cb,)), ((), ())), preferred_element_type=F32)
+
+
+def params(**kw):
+    return pltpu.CompilerParams(vmem_limit_bytes=VMEM_LIMIT, **kw)
+
+
+def cost(flops, nbytes, trans=0):
+    return pl.CostEstimate(flops=int(flops), bytes_accessed=int(nbytes), transcendentals=int(trans))
+
+
+def wait_all(ref, sem):
+    pltpu.make_async_copy(ref, ref, sem).wait()
+
+
+def binary_rows(latent):
+    level = jnp.mean(jnp.abs(latent), axis=1, keepdims=True)
+    return jnp.where(latent > 0, level, jnp.where(latent < 0, -level, 0.0)).astype(BF16)
+
+
+def pack_kernel(
+    info, hid, lq, lk, lv, lo, lu, ld, tq, tk, tv, to, tu, td, qkv, own, mine, keep, send
+):
+    core, rep = info[I_CORE], info[I_REP]
+    keep[...] = hid[core]
+    send[...] = hid[1 - core]
+    for slot, ref in enumerate((lq, lk, lv)):
+        qkv[0, slot] = binary_rows(ref[...])
+    for slot, ref in enumerate((tq, tk, tv)):
+        qkv[1, slot] = ref[...]
+    rows, width = lq.shape
+    quarter = own.shape[0]
+    half = rows // 2
+
+    def fill(base, up, down):
+        for r in range(quarter):
+            own[r, base : base + rows] = up[r * rows : (r + 1) * rows]
+            own[r, base + rows : base + 2 * rows] = down[:, r * width : (r + 1) * width]
+
+    fill(0, binary_rows(lu[...]), binary_rows(ld[...]))
+    fill(2 * rows, tu, td)
+    student_out = binary_rows(lo[...])
+    for h in range(2):
+        own[h, 4 * rows :] = student_out[h * half : (h + 1) * half]
+        own[2 + h, 4 * rows :] = to[h * half : (h + 1) * half]
+    mine[...] = own[rep]
+
+
+def pack(info, hid, latents, tutors):
+    rows, width = latents[0].shape
+    piece = 4 * rows + rows // 2
+    half = hid.shape[1:]
+    return pl.pallas_call(
+        pack_kernel,
+        out_shape=(
+            jax.ShapeDtypeStruct((2, 3, rows, width), BF16),
+            jax.ShapeDtypeStruct((4, piece, width), BF16),
+            jax.ShapeDtypeStruct((piece, width), BF16),
+            jax.ShapeDtypeStruct(half, BF16),
+            jax.ShapeDtypeStruct(half, BF16),
+        ),
+        in_specs=[SM] + [VM] * 13,
+        out_specs=(VM,) * 5,
+        compiler_params=params(),
+        cost_estimate=cost(4e6, 12e6),
+        name="pack",
+    )(info, hid, *latents, *tutors)
+
+
+def load_tokens(info, xs, pieces, sem):
+    core = info[I_CORE]
+    for k, piece in enumerate(pieces):
+        for j in range(2):
+            spot = jnp.where(j == 0, core, 1 - core)
+            pltpu.make_async_copy(piece.at[j], xs.at[info[I_RING + k], spot], sem).start()
+
+
+def load_rows(info, ws, own, sib, sem):
+    core = info[I_CORE]
+    for slot in range(3):
+        pltpu.make_async_copy(own.at[slot], ws.at[slot, core], sem).start()
+        pltpu.make_async_copy(sib.at[slot], ws.at[slot, 1 - core], sem).start()
+
+
+def attend_kernel(student, info, *refs):
+    pieces, refs = refs[:4], refs[4:]
+    own, sib, bq, bv, clip = refs[:5]
+    refs = refs[5:]
+    if student:
+        out, qkv_out, lse_out, ctx_out, xs, ws, qs, ks, vt, ct, sems = refs
+    else:
+        out, xs, ws, qs, ks, vt, ct, sems = refs
+    load_tokens(info, xs, pieces, sems.at[0])
+    load_rows(info, ws, own, sib, sems.at[1])
+    line, _, half, width = xs.shape
+    block = 2 * half
+    feats = qs.shape[1]
+    total = qs.shape[0]
+    heads = feats // DH
+    place = info[I_Z]
+    length = info[I_LEN]
+    bq_row, bv_row = bq[place], bv[place]
+    wait_all(xs, sems.at[0])
+    wait_all(ws, sems.at[1])
+
+    def project(b, carry):
+        rows = pl.ds(pl.multiple_of(b * block, block), block)
+        x = xs[b].reshape(block, width)
+        if student:
+            lim = clip[...]
+            x = jnp.clip(x.astype(F32), -lim, lim).astype(BF16)
+        q = (dims(x, ws[0].reshape(feats, width), 1, 1) + bq_row).astype(BF16)
+        k = dims(x, ws[1].reshape(feats, width), 1, 1).astype(BF16)
+        v = (dims(x, ws[2].reshape(feats, width), 1, 1) + bv_row).astype(BF16)
+        q = q * jnp.asarray(DH ** (-0.5), BF16)
+        qs[rows] = q
+        ks[rows] = k
+        vt[:, rows] = v.astype(F32).T.astype(BF16)
+        if student:
+            qkv_out[0, rows] = q
+            qkv_out[1, rows] = k
+            qkv_out[2, rows] = v
+        return carry
+
+    lax.fori_loop(0, line, project, 0)
+    fill = jnp.where(
+        lax.broadcasted_iota(jnp.int32, (total, 1), 0) < length, 0.0, NEG_FILL
+    ).astype(F32)
+    lane_head = lax.broadcasted_iota(jnp.int32, (1, feats), 1) // DH
+
+    def mix(b, carry):
+        rows = pl.ds(pl.multiple_of(b * block, block), block)
+        q = qs[rows]
+        for h in range(heads):
+            q_h = jnp.where(lane_head == h, q, jnp.zeros_like(q))
+            scores = dims(ks[...], q_h, 1, 1) + fill
+            top = jnp.max(scores, axis=0, keepdims=True)
+            weight = jnp.exp(scores - top)
+            mass = jnp.sum(weight, axis=0, keepdims=True)
+            head = slice(h * DH, (h + 1) * DH)
+            mixed = dims(vt[head], weight.astype(BF16), 1, 0) * (1.0 / mass)
+            ct[head, rows] = mixed
+            if student:
+                lse_out[h : h + 1, rows] = top + jnp.log(mass)
+        return carry
+
+    lax.fori_loop(0, line, mix, 0)
+    for b in range(line):
+        out[b] = ct[:, b * block : (b + 1) * block].T.astype(BF16)
+    if student:
+        ctx_out[...] = ct[...]
+
+
+def attend(info, pieces, own, sib, bq, bv, clip, student):
+    _, half, width = pieces[0].shape
+    line = len(pieces)
+    total = line * 2 * half
+    rows = own.shape[1]
+    feats = 2 * rows
+    outs = [jax.ShapeDtypeStruct((line, 2 * half, feats), BF16)]
+    if student:
+        outs += [
+            jax.ShapeDtypeStruct((3, total, feats), BF16),
+            jax.ShapeDtypeStruct((8, total), F32),
+            jax.ShapeDtypeStruct((feats, total), F32),
+        ]
+    return pl.pallas_call(
+        functools.partial(attend_kernel, student),
+        out_shape=tuple(outs),
+        in_specs=[SM] + [ANY] * 6 + [VM] * 3,
+        out_specs=(VM,) * len(outs),
+        scratch_shapes=[
+            pltpu.VMEM((line, 2, half, width), BF16),
+            pltpu.VMEM((3, 2, rows, width), BF16),
+            pltpu.VMEM((total, feats), BF16),
+            pltpu.VMEM((total, feats), BF16),
+            pltpu.VMEM((feats, total), BF16),
+            pltpu.VMEM((feats, total), F32),
+            pltpu.SemaphoreType.DMA((2,)),
+        ],
+        compiler_params=params(),
+        cost_estimate=cost(6e9, 4e6, 3e6),
+        name="attend_student" if student else "attend_tutor",
+    )(info, *pieces, own, sib, bq, bv, clip)
+
+
+def attend_back_kernel(info, *refs):
+    pieces, refs = refs[:4], refs[4:]
+    (own, sib, clip, qkv, lse, ctx, dctx, part0, part1, part2, part3, keep, send) = refs[:13]
+    (xs, ws, kt, dct, dq, dk, dv, sems) = refs[13:]
+    parts = (part0, part1, part2, part3)
+    load_tokens(info, xs, pieces, sems.at[0])
+    load_rows(info, ws, own, sib, sems.at[1])
+    line, _, half, width = xs.shape
+    block = 2 * half
+    total, feats = dk.shape
+    heads = feats // DH
+    core = info[I_CORE]
+    length = info[I_LEN]
+    lim = clip[...]
+    for b in range(line):
+        cols = slice(b * block, (b + 1) * block)
+        kt[:, cols] = qkv[1, cols].astype(F32).T.astype(BF16)
+        dct[:, cols] = dctx[b].astype(F32).T
+    dk[...] = jnp.zeros_like(dk)
+    dv[...] = jnp.zeros_like(dv)
+    fill = jnp.where(
+        lax.broadcasted_iota(jnp.int32, (total, 1), 0) < length, 0.0, NEG_FILL
+    ).astype(F32)
+    lane_head = lax.broadcasted_iota(jnp.int32, (1, feats), 1) // DH
+
+    def body(b, carry):
+        rows = pl.ds(pl.multiple_of(b * block, block), block)
+        q = qkv[0, rows]
+        g = dctx[b]
+        dk_add = dv_add = None
+        for h in range(heads):
+            head = slice(h * DH, (h + 1) * DH)
+            q_h = jnp.where(lane_head == h, q, jnp.zeros_like(q))
+            g_h = jnp.where(lane_head == h, g, jnp.zeros_like(g))
+            delta = jnp.sum(dct[head, rows] * ctx[head, rows], axis=0, keepdims=True)
+            probs = jnp.exp(dims(qkv[1], q_h, 1, 1) + fill - lse[h : h + 1, rows])
+            dprobs = dims(qkv[2], g_h, 1, 1)
+            dscores = (probs * (dprobs - delta)).astype(BF16)
+            dv_h = dims(probs.astype(BF16), g_h, 1, 0)
+            dk_h = dims(dscores, q_h, 1, 0)
+            dk_add = dk_h if dk_add is None else dk_add + dk_h
+            dv_add = dv_h if dv_add is None else dv_add + dv_h
+            dq[head, rows] = dims(kt[head], dscores, 1, 0) * (DH ** (-0.5))
+        dk[...] += dk_add
+        dv[...] += dv_add
+        return carry
+
+    lax.fori_loop(0, line, body, 0)
+    wait_all(xs, sems.at[0])
+    wait_all(ws, sems.at[1])
+    dq_t = dq[...].astype(BF16)
+    dq_low = dq_t.astype(F32).T.astype(BF16)
+    dk_low = dk[...].astype(BF16)
+    dv_low = dv[...].astype(BF16)
+    dk_t = dk_low.astype(F32).T.astype(BF16)
+    dv_t = dv_low.astype(F32).T.astype(BF16)
+    qkv_flat = [ws[slot].reshape(feats, width) for slot in range(3)]
+    for k in range(line):
+        spot = info[I_RING + k]
+        rows = pl.ds(pl.multiple_of(spot * block, block), block)
+        dk_rows = dk[rows].astype(BF16)
+        dv_rows = dv[rows].astype(BF16)
+        dq_rows = dq[:, rows].T.astype(BF16)
+        parts[k][...] = (
+            dims(dq_rows, qkv_flat[0], 1, 0)
+            + dims(dk_rows, qkv_flat[1], 1, 0)
+            + dims(dv_rows, qkv_flat[2], 1, 0)
+        ).astype(BF16)
+    grads = []
+    for low_t in (dq_t, dk_t, dv_t):
+        acc = None
+        for b in range(line):
+            x = jnp.clip(xs[b].reshape(block, width).astype(F32), -lim, lim).astype(BF16)
+            one = dims(low_t[:, b * block : (b + 1) * block], x, 1, 0)
+            acc = one if acc is None else acc + one
+        grads.append(acc)
+    rows = feats // 2
+    bias_q = jnp.sum(dq_low.astype(F32), axis=0, keepdims=True)
+    bias_v = jnp.sum(dv_low.astype(F32), axis=0, keepdims=True)
+    for rel, ref in ((0, keep), (1, send)):
+        for c in range(2):
+
+            @pl.when((core if rel == 0 else 1 - core) == c)
+            def _():
+                for slot, grad in enumerate(grads):
+                    ref[slot * rows : (slot + 1) * rows] = grad[c * rows : (c + 1) * rows].astype(
+                        ref.dtype
+                    )
+                tail = jnp.concatenate(
+                    [
+                        bias_q[:, c * rows : (c + 1) * rows],
+                        bias_v[:, c * rows : (c + 1) * rows],
+                        jnp.zeros((1, width - 2 * rows), F32),
+                    ],
+                    axis=1,
+                )
+                ref[3 * rows :] = jnp.broadcast_to(tail, (16, width)).astype(ref.dtype)
+
+
+def attend_back(info, pieces, own, sib, clip, qkv, lse, ctx, dctx):
+    _, half, width = pieces[0].shape
+    line = len(pieces)
+    total = line * 2 * half
+    rows = own.shape[1]
+    feats = 2 * rows
+    part = jax.ShapeDtypeStruct((2 * half, width), BF16)
+    grad = jax.ShapeDtypeStruct((3 * rows + 16, width), BF16)
+    return pl.pallas_call(
+        attend_back_kernel,
+        out_shape=(part,) * 4 + (grad, grad),
+        in_specs=[SM] + [ANY] * 6 + [VM] * 5,
+        out_specs=(VM,) * 6,
+        scratch_shapes=[
+            pltpu.VMEM((line, 2, half, width), BF16),
+            pltpu.VMEM((3, 2, rows, width), BF16),
+            pltpu.VMEM((feats, total), BF16),
+            pltpu.VMEM((feats, total), F32),
+            pltpu.VMEM((feats, total), F32),
+            pltpu.VMEM((total, feats), F32),
+            pltpu.VMEM((total, feats), F32),
+            pltpu.SemaphoreType.DMA((2,)),
+        ],
+        compiler_params=params(),
+        cost_estimate=cost(12e9, 6e6, 3e6),
+        name="attend_back",
+    )(info, *pieces, own, sib, clip, qkv, lse, ctx, dctx)
+
+
+V_OUT, V_DOWN, V_G1, V_S1, V_G2, V_S2, V_UP = 0, 1, 2, 3, 4, 5, 6
+S_OUT, S_DOWN, S_G1, S_S1, S_G2, S_S2, S_UP, S_ERR = 0, 1, 2, 3, 4, 5, 6, 10
+PAD = 32
+
+
+def norm_parts(v):
+    centre = v - jnp.mean(v, axis=-1, keepdims=True)
+    inv = lax.rsqrt(jnp.mean(centre * centre, axis=-1, keepdims=True) + NORM_EPS)
+    return centre * inv, inv
+
+
+def norm_back(dnormed, normed, inv):
+    return inv * (
+        dnormed
+        - jnp.mean(dnormed, axis=-1, keepdims=True)
+        - normed * jnp.mean(dnormed * normed, axis=-1, keepdims=True)
+    )
+
+
+def turned(v):
+    return v.T.astype(BF16)
+
+
+def middle_kernel(info, own, sib, *refs):
+    chunks, refs = refs[:30], refs[30:]
+    (x_own, ctx_s, ctx_t, vecs) = refs[:4]
+    (out_keep, out_send, dfirst_keep, dctx_out, sums) = refs[4:9]
+    grads = refs[9:17]
+    (w_up, w_dn, w_out, gate_pre, lower, gup, gdn, base, aim, acc, sems) = refs[17:]
+    core, rep, place, length = info[I_CORE], info[I_REP], info[I_Z], info[I_LEN]
+    _, groups, quarters, rows, width = w_up.shape
+    tokens = ctx_s.shape[1]
+    line = groups // 2
+    hidden = groups * rows
+    half = rows // 2
+
+    def place_piece(src, first, last, r, g):
+        fields = (
+            (0, rows, lambda: w_up.at[0, g, r], 0),
+            (rows, 2 * rows, lambda: w_dn.at[0, r, g], 1),
+            (2 * rows, 3 * rows, lambda: w_up.at[1, g, r], 2),
+            (3 * rows, 4 * rows, lambda: w_dn.at[1, r, g], 3),
+            (4 * rows, 4 * rows + half, lambda: w_out.at[r // 2, g, lax.rem(r, 2)], 4),
+        )
+        for lo, hi, dst, sem in fields:
+            if first <= lo and hi <= last:
+                pltpu.make_async_copy(
+                    src.at[pl.ds(lo - first, hi - lo)], dst(), sems.at[sem]
+                ).start()
+
+    piece = 4 * rows + half
+    for rel, ref in ((0, own), (1, sib)):
+        member = 2 * place + (core if rel == 0 else 1 - core)
+        for r in range(quarters):
+            place_piece(ref.at[r], 0, piece, r, member)
+    for k in range(1, line):
+        for rel in range(2):
+            member = 2 * info[I_RING + k] + (core if rel == 0 else 1 - core)
+            mine, from_x, from_y, far_a, far_b = chunks[((k - 1) * 2 + rel) * 5 :][:5]
+            place_piece(mine, 0, piece, rep, member)
+            place_piece(from_x, 0, piece, rep ^ 1, member)
+            place_piece(from_y, 0, piece, rep ^ 2, member)
+            place_piece(far_a, 0, 2 * rows, rep ^ 3, member)
+            place_piece(far_b, 2 * rows, piece, rep ^ 3, member)
+
+    wait_all(w_out, sems.at[4])
+    x_low = jnp.concatenate(
+        [x_own[jnp.where(core == j, 0, 1)] for j in range(2)], axis=0
+    ).astype(F32)
+
+    def row(net, which):
+        return vecs[net, which]
+
+    def context_of(ref):
+        return jnp.concatenate([ref[zb] for zb in range(line)], axis=1)
+
+    def upper(net, ctx):
+        first = (
+            x_low + dims(ctx, w_out[net].reshape(width, width), 1, 1) + row(net, V_OUT)
+        )
+        normed, inv = norm_parts(first)
+        return normed, inv, normed * row(net, V_G1) + row(net, V_S1)
+
+    def lower_half(net, upper_in, keep):
+        acc[...] = jnp.zeros_like(acc)
+
+        def step(r, carry):
+            gate = (
+                dims(upper_in, w_up[net, pl.ds(2 * r, 2)].reshape(hidden, width), 1, 1)
+                + vecs[net, V_UP + r]
+            )
+            low = gelu_exact(gate).astype(BF16)
+            if keep:
+                gate_pre[r] = gate
+                lower[r] = low
+            acc[...] += dims(low, w_dn[net, r].reshape(width, hidden), 1, 1)
+            return carry
+
+        lax.fori_loop(0, quarters, step, 0)
+        return acc[...]
+
+    ctx_tutor = context_of(ctx_t)
+    _, _, first_norm = upper(1, ctx_tutor)
+    ctx_low = context_of(ctx_s)
+    normed_one, inv_one, first_norm_s = upper(0, ctx_low)
+    base[...] = first_norm_s
+    wait_all(w_up.at[1], sems.at[2])
+    wait_all(w_dn.at[1], sems.at[3])
+    second = first_norm + lower_half(1, first_norm.astype(BF16), False) + row(1, V_DOWN)
+    normed, _ = norm_parts(second)
+    aim[...] = normed * row(1, V_G2) + row(1, V_S2)
+
+    wait_all(w_up.at[0], sems.at[0])
+    wait_all(w_dn.at[0], sems.at[1])
+    upper_in = first_norm_s.astype(BF16)
+    second = base[...] + lower_half(0, upper_in, True) + row(0, V_DOWN)
+    normed_two, inv_two = norm_parts(second)
+    output = normed_two * row(0, V_G2) + row(0, V_S2)
+    aim[...] = output - aim[...]
+    acc[...] = output
+
+    def part_of(ref, j):
+        return ref[pl.ds(pl.multiple_of(j * (tokens // 2), tokens // 2), tokens // 2)]
+
+    out_keep[...] = part_of(acc, core).astype(BF16)
+    out_send[...] = part_of(acc, 1 - core).astype(BF16)
+    where = place * tokens + lax.broadcasted_iota(jnp.int32, (tokens, 1), 0)
+    kept = jnp.where(where < length, 1.0, 0.0).astype(F32)
+    dout = kept * aim[...]
+    sums[...] = jnp.zeros_like(sums)
+    error = 0.5 * jnp.sum(dout * dout)
+    sums[S_ERR] = jnp.full((1, width), error, F32)
+    sums[S_G2] = jnp.sum(dout * normed_two, axis=0, keepdims=True)
+    sums[S_S2] = jnp.sum(dout, axis=0, keepdims=True)
+    dsecond = norm_back(dout * row(0, V_G2), normed_two, inv_two)
+    sums[S_DOWN] = jnp.sum(dsecond, axis=0, keepdims=True)
+    g_down = dsecond.astype(BF16)
+    g_down_t = turned(dsecond)
+    acc[...] = dsecond
+
+    def back(r, carry):
+        low = lower[r]
+        gdn[r, :, 0:rows] = dims(g_down_t, low, 1, 0).astype(BF16).reshape(groups, rows, hidden)
+        dlower = dims(g_down, w_dn[0, r].reshape(width, hidden), 1, 0)
+        gate = gate_pre[r]
+        slope = 0.5 * (1.0 + lax.erf(gate * 0.7071067811865476)) + gate * (
+            0.3989422804014327 * jnp.exp(-0.5 * gate * gate)
+        )
+        dgate = dlower * slope
+        sums[S_UP + r] = jnp.sum(dgate, axis=0, keepdims=True)
+        gup_r = dims(turned(dgate), upper_in, 1, 0).astype(BF16)
+        gup[pl.ds(2 * r, 2)] = gup_r.reshape(2, quarters, rows, width)
+        acc[...] += dims(
+            dgate.astype(BF16), w_up[0, pl.ds(2 * r, 2)].reshape(hidden, width), 1, 0
+        )
+        return carry
+
+    lax.fori_loop(0, quarters, back, 0)
+    dfirst = acc[...]
+    sums[S_G1] = jnp.sum(dfirst * normed_one, axis=0, keepdims=True)
+    sums[S_S1] = jnp.sum(dfirst, axis=0, keepdims=True)
+    dsum = norm_back(dfirst * row(0, V_G1), normed_one, inv_one)
+    sums[S_OUT] = jnp.sum(dsum, axis=0, keepdims=True)
+    dfirst_keep[...] = dsum
+    g_out = dsum.astype(BF16)
+    dctx = dims(g_out, w_out[0].reshape(width, width), 1, 0).astype(BF16)
+    feats = width // line
+    for zb in range(line):
+        dctx_out[zb] = dctx[:, zb * feats : (zb + 1) * feats]
+    gout = dims(turned(dsum), ctx_low, 1, 0).reshape(groups, quarters, rows // quarters, width)
+    slim = rows // quarters
+    for r in range(quarters):
+        for g in range(groups):
+            gdn[r, g, rows : rows + slim] = gout[g, r].astype(BF16)
+            gdn[r, g, rows + slim :] = jnp.zeros((PAD - slim, width), BF16)
+
+    for rel in range(2):
+        a_keep, a_send, b_keep, b_send = grads[rel * 4 : rel * 4 + 4]
+        for far in range(4):
+            r = rep ^ far
+            for k in range(line):
+                g = 2 * info[I_RING + k] + (core if rel == 0 else 1 - core)
+                a_ref = a_send if far & 1 else a_keep
+                b_ref = b_send if far & 2 else b_keep
+                pltpu.make_async_copy(
+                    gup.at[g, r], a_ref.at[far >> 1, k], sems.at[5 + rel * 4 + (far & 1)]
+                ).start()
+                pltpu.make_async_copy(
+                    gdn.at[r, g], b_ref.at[far & 1, k], sems.at[7 + rel * 4 + (far >> 1)]
+                ).start()
+    for rel in range(2):
+        for slot in range(4):
+            ref = grads[rel * 4 + slot]
+            wait_all(ref, sems.at[5 + rel * 4 + slot])
+
+
+def middle(info, own, sib, chunks, x_own, ctx_s, ctx_t, vecs):
+    line, tokens, feats = ctx_s.shape
+    width = line * feats
+    quarters = own.shape[0]
+    groups = 2 * line
+    rows = width // groups
+    half = (tokens // 2, width)
+    a_shape = jax.ShapeDtypeStruct((2, line, rows, width), BF16)
+    b_shape = jax.ShapeDtypeStruct((2, line, rows + PAD, width), BF16)
+    outs = (
+        jax.ShapeDtypeStruct(half, BF16),
+        jax.ShapeDtypeStruct(half, BF16),
+        jax.ShapeDtypeStruct((tokens, width), F32),
+        jax.ShapeDtypeStruct((line, tokens, feats), BF16),
+        jax.ShapeDtypeStruct((16, 1, width), F32),
+    ) + (a_shape, a_shape, b_shape, b_shape) * 2
+    return pl.pallas_call(
+        middle_kernel,
+        out_shape=outs,
+        in_specs=[SM] + [ANY] * 32 + [VM] * 4,
+        out_specs=(VM,) * 5 + (ANY,) * 8,
+        scratch_shapes=[
+            pltpu.VMEM((2, groups, quarters, rows, width), BF16),
+            pltpu.VMEM((2, quarters, groups, rows, width), BF16),
+            pltpu.VMEM((2, groups, 2, rows // 2, width), BF16),
+            pltpu.VMEM((quarters, tokens, width), F32),
+            pltpu.VMEM((quarters, tokens, width), BF16),
+            pltpu.VMEM((groups, quarters, rows, width), BF16),
+            pltpu.VMEM((quarters, groups, rows + PAD, width), BF16),
+            pltpu.VMEM((tokens, width), F32),
+            pltpu.VMEM((tokens, width), F32),
+            pltpu.VMEM((tokens, width), F32),
+            pltpu.SemaphoreType.DMA((13,)),
+        ],
+        compiler_params=params(),
+        cost_estimate=cost(15e9, 30e6, 4e6),
+        name="middle",
+    )(info, own, sib, *chunks, x_own, ctx_s, ctx_t, vecs)
+
+
+def finish_kernel(info, *refs):
+    pieces, refs = refs[:4], refs[4:]
+    grad_qkv, up, down, out, gq, gk, gv, scr, sem = refs
+    rep = info[I_REP]
+    for far, ref in enumerate(pieces):
+        pltpu.make_async_copy(ref, scr.at[rep ^ far], sem.at[0]).start()
+    rows, width = gq.shape
+    for slot, ref in enumerate((gq, gk, gv)):
+        ref[...] = grad_qkv[slot * rows : (slot + 1) * rows].astype(F32)
+    wait_all(scr, sem.at[0])
+    slim = rows // len(pieces)
+    for r in range(len(pieces)):
+        up[r * rows : (r + 1) * rows] = scr[r, 0:rows].astype(F32)
+        down[:, r * width : (r + 1) * width] = scr[r, rows : 2 * rows].astype(F32)
+        out[r * slim : (r + 1) * slim] = scr[r, 2 * rows : 2 * rows + PAD].astype(F32)[:slim]
+
+
+def finish(info, pieces, grad_qkv):
+    high, width = pieces[0].shape
+    rows = (high - PAD) // 2
+    small = jax.ShapeDtypeStruct((rows, width), F32)
+    return pl.pallas_call(
+        finish_kernel,
+        out_shape=(
+            jax.ShapeDtypeStruct((4 * rows, width), F32),
+            jax.ShapeDtypeStruct((rows, 4 * width), F32),
+            small,
+            small,
+            small,
+            small,
+        ),
+        in_specs=[SM] + [ANY] * 4 + [VM],
+        out_specs=(VM,) * 6,
+        scratch_shapes=[
+            pltpu.VMEM((4, high, width), BF16),
+            pltpu.SemaphoreType.DMA((1,)),
+        ],
+        compiler_params=params(),
+        cost_estimate=cost(1e6, 8e6),
+        name="finish",
+    )(info, *pieces, grad_qkv)
+
+
+def add_low(*terms):
+    total = terms[0].astype(F32)
+    for term in terms[1:]:
+        total = total + term.astype(F32)
+    return total.astype(BF16)
+
+
+def line_shards(line, *args):
+    hidden_in, seq_lengths = args[0], args[1]
+    latents, vectors, clip_input = args[2:8], args[8:17], args[17]
+    tutors = args[18:24]
+    tutor_biases, tutor_inner, tutor_gains, tutor_shifts = args[24:28]
+    micro_count, _, local_rows, width = hidden_in.shape
+    rep, grp = lax.axis_index("rep"), lax.axis_index("grp")
+    place, core = grp // 2, lax.rem(grp, 2)
+    ring = z_ring(line)
+    behind = [[ring[(ring.index(z) - k) % line] for k in range(line)] for z in range(line)]
+
+    def over_z(x, pairs):
+        return lax.ppermute(x, "grp", [(2 * a + c, 2 * b + c) for a, b in pairs for c in range(2)])
+
+    def next_z(x):
+        return over_z(x, [(ring[i], ring[(i + 1) % line]) for i in range(line)])
+
+    def swap(x):
+        return lax.ppermute(x, "grp", [(g, g ^ 1) for g in range(2 * line)])
+
+    def to_rep(x, bit):
+        return lax.ppermute(x, "rep", [(i, i ^ bit) for i in range(4)])
+
+    def to_tokens(x):
+        groups = [[2 * z + c for z in range(line)] for c in range(2)]
+        return lax.all_to_all(x, "grp", 0, 0, axis_index_groups=groups, tiled=True)
+
+    length = seq_lengths[core, 0]
+    info = jnp.concatenate(
+        [
+            jnp.stack([core, rep, place, length]).astype(jnp.int32),
+            jnp.asarray(behind, jnp.int32)[place],
+        ]
+    )
+    clip = clip_input.reshape(1, width)
+    qkv_own, own, piece, keep, send = pack(info, hidden_in[:, 0], latents, tutors)
+    x_own = jnp.stack([keep, swap(send)])
+    qkv_sib = swap(qkv_own)
+    sib = swap(own)
+    tokens_in = [x_own]
+    for _ in range(line - 1):
+        tokens_in.append(next_z(tokens_in[-1]))
+
+    rows = latents[0].shape[0]
+    chunks = []
+    for _ in range(line - 1):
+        piece = next_z(piece)
+        from_x, from_y = to_rep(piece, 1), to_rep(piece, 2)
+        far_a = to_rep(from_x[: 2 * rows], 2)
+        far_b = to_rep(from_y[2 * rows :], 1)
+        got = [piece, from_x, from_y, far_a, far_b]
+        chunks += got + [swap(one) for one in got]
+
+    def heads_row(vector):
+        return vector.reshape(line, 1, width // line)
+
+    ctx_s, qkv, lse, ctx = attend(
+        info,
+        tokens_in,
+        qkv_own[0],
+        qkv_sib[0],
+        heads_row(vectors[0]),
+        heads_row(vectors[1]),
+        clip,
+        True,
+    )
+    (ctx_t,) = attend(
+        info,
+        tokens_in,
+        qkv_own[1],
+        qkv_sib[1],
+        heads_row(tutor_biases[0]),
+        heads_row(tutor_biases[1]),
+        clip,
+        False,
+    )
+    ctx_s, ctx_t = to_tokens(ctx_s), to_tokens(ctx_t)
+    vecs = jnp.concatenate(
+        [
+            vectors[2],
+            vectors[4],
+            vectors[5],
+            vectors[6],
+            vectors[7],
+            vectors[8],
+            vectors[3],
+            tutor_biases[2],
+            tutor_biases[3],
+            tutor_gains[0],
+            tutor_shifts[0],
+            tutor_gains[1],
+            tutor_shifts[1],
+            tutor_inner,
+        ]
+    ).reshape(2, 10, 1, width)
+    (
+        out_keep,
+        out_send,
+        dfirst,
+        dctx,
+        sums,
+        a_keep,
+        a_send,
+        b_keep,
+        b_send,
+        a_keep_sib,
+        a_send_sib,
+        b_keep_sib,
+        b_send_sib,
+    ) = middle(info, own, sib, chunks, x_own, ctx_s, ctx_t, vecs)
+
+    def by_micro(kept, got):
+        return jnp.where(
+            core == 0, jnp.stack([kept, got]), jnp.stack([got, kept])
+        )[:, None]
+
+    dctx = to_tokens(dctx)
+    a_out = add_low(a_send, swap(a_send_sib))
+    b_out = add_low(b_send, swap(b_send_sib))
+    a_keep_sib, b_keep_sib = swap(a_keep_sib), swap(b_keep_sib)
+    a_in, b_in = to_rep(a_out, 1), to_rep(b_out, 2)
+    a_next = to_rep(add_low(a_keep[1], a_keep_sib[1], a_in[1]), 2)
+    b_next = to_rep(add_low(b_keep[1], b_keep_sib[1], b_in[1]), 1)
+    both = jnp.concatenate(
+        [
+            add_low(a_keep[0], a_keep_sib[0], a_in[0], a_next),
+            add_low(b_keep[0], b_keep_sib[0], b_in[0], b_next),
+        ],
+        axis=1,
+    )
+    layer_out = by_micro(out_keep, swap(out_send))
+
+    part0, part1, part2, part3, gqkv, gqkv_sib = attend_back(
+        info, tokens_in, qkv_own[0], qkv_sib[0], clip, qkv, lse, ctx, dctx
+    )
+    moving = next_z(part1)
+    moving = next_z(add_low(moving, part2))
+    moving = next_z(add_low(moving, part3))
+    grads = next_z(both[1])
+    grads = next_z(add_low(grads, both[2]))
+    grads = next_z(add_low(grads, both[3]))
+    grads = add_low(grads, both[0])
+    quarter = [grads, to_rep(grads, 1), to_rep(grads, 2), to_rep(grads, 3)]
+
+    gqkv = add_low(gqkv, swap(gqkv_sib))
+    gqkv = add_low(gqkv, to_rep(gqkv, 1))
+    gqkv = add_low(gqkv, to_rep(gqkv, 2))
+    grad_up, grad_down, grad_out, grad_q, grad_k, grad_v = finish(info, quarter, gqkv)
+
+    total = sums.reshape(16, width)
+    total = total + swap(total)
+    total = total + to_rep(total, 1)
+    total = total + to_rep(total, 2)
+    bit = 1
+    while bit < line:
+        total = total + over_z(total, [(z, z ^ bit) for z in range(line)])
+        bit *= 2
+    own_cols = lax.dynamic_slice_in_dim(total.reshape(16, 2 * line, rows), grp, 1, 1)[:, 0]
+    own_up = lax.dynamic_slice_in_dim(
+        total[S_UP : S_UP + 4].reshape(2 * line, 4 * rows), grp, 1, 0
+    )[0]
+    entries = micro_count * 4 * 2 * line * local_rows * width
+    loss = total[S_ERR, 0] / entries
+
+    order = jnp.stack([jnp.where(core == 0, 0, 1), jnp.where(core == 0, 1, 0)])
+    hidden_tokens = x_own[order].reshape(2 * local_rows, width).astype(F32)
+    dxin = moving.astype(F32) + part0.astype(F32)
+    grad_input = dfirst + jnp.where(jnp.abs(hidden_tokens) < clip, dxin, 0.0)
+    halves = grad_input.reshape(2, local_rows, width)
+    grad_input = by_micro(
+        jnp.where(core == 0, halves[0], halves[1]),
+        swap(jnp.where(core == 0, halves[1], halves[0])),
+    )
+    bias = gqkv[3 * rows].astype(F32)
+    return (
+        layer_out,
+        loss,
+        grad_input,
+        grad_q,
+        grad_k,
+        grad_v,
+        grad_out,
+        grad_up,
+        grad_down,
+        bias[:rows],
+        bias[rows : 2 * rows],
+        own_cols[S_OUT],
+        own_up,
+        own_cols[S_DOWN],
+        own_cols[S_G1],
+        own_cols[S_S1],
+        own_cols[S_G2],
+        own_cols[S_S2],
+    )
+
+
+def fits_line(mesh, args):
+    line = mesh.shape["grp"] // 2
+    micro_count, seq_count, total, width = args[0].shape
+    hidden = args[6].shape[0]
+    return (
+        mesh.shape["rep"] == 4
+        and line == 4
+        and H % line == 0
+        and micro_count == 2
+        and seq_count == mesh.shape["rep"]
+        and total == 8 * 128
+        and hidden == 4 * width
+    )
+
+
 def solution(mesh):
-    return jax.shard_map(
-        shards,
+    def mapped(body):
+        return jax.shard_map(
+        body,
         mesh=mesh,
         in_specs=(
             P(None, "rep", "grp", None),
@@ -605,3 +1436,11 @@
         ),
         check_vma=False,
     )
+
+    def step(*args):
+        if fits_line(mesh, args):
+            line = mesh.shape["grp"] // 2
+            return mapped(functools.partial(line_shards, line))(*args)
+        return mapped(shards)(*args)
+
+    return step

time: 1170 us -> 343 us (0.29)
  waiting for transfers between devices: 512 us -> 123 us
  matrix products: 205 us -> 0 us
  blocking collectives: 136 us -> 0 us
  local copies, waits for them, and re-layouts: 145 us -> 45.2 us
  other arithmetic: 116 us -> 16.5 us
  Pallas kernels: 0 us -> 83.4 us
  starting transfers between devices: 1.48 us -> 69.9 us
  loops' own time: 25.1 us -> 0 us
  between operations: 21.6 us -> 3.28 us
    all_gather x24 -> x0, waiting for transfers between devices: 357 us -> none  [the longest x6 147 us: student_project(): lax.all_gather(latent.astype(jnp.bfloat16), 'grp', axis=0, tiled=True)]
    dot_general x82 -> x0, matrix products: 205 us -> none  [the longest x22 57.5 us: times_rows(): lax.dot_general(operand, weight, (((1,), (1,)), ((), ())), preferred_elem...]
    reduce_scatter x6 -> x0, waiting for transfers between devices: 150 us -> none  [the longest x1 55.6 us: shards(): lax.psum_scatter(weight_sums[5].astype(jnp.bfloat16), 'grp', scatter_dime...]
    ppermute x0 -> x63, waiting for transfers between devices: none -> 123 us  [the longest x14 68.6 us: over_z(): lax.ppermute(x, 'grp', [(2 * a + c, 2 * b + c) for a, b in pairs for c in...]
    dynamic_slice x64 -> x2, local copies, waits for them, and re-layouts: 91.2 us -> 1.18 us  [the longest x1 0.6 us: line_shards(): lax.dynamic_slice_in_dim(total[S_UP:S_UP + 4].reshape(2 * line, 4 * rows)...]
    pallas_call x0 -> x6, Pallas kernels: none -> 83.4 us  [the longest x1 31.8 us: middle(): pl.pallas_call(middle_kernel, out_shape=outs, in_specs=[SM] + [ANY] * 32...]
    all_gather x4 -> x0, blocking collectives: 60.8 us -> none  [the longest x2 30.5 us: key_grads(): lax.all_gather(log_rows, 'grp', axis=1, tiled=True)]
    ppermute x0 -> x63, starting transfers between devices: none -> 56.7 us  [the longest x14 28.9 us: over_z(): lax.ppermute(x, 'grp', [(2 * a + c, 2 * b + c) for a, b in pairs for c in...]
  transfers between devices with their start and end apart: 31 -> 66, of which waited for: 22 -> 24; matrix products, arithmetic and copies ran while one was open for 38% -> 16% of each run, Pallas kernels for 0% -> 12%
where the time goes in v1:
time: 343 us; the launch traced here: 341 us
  waiting for transfers between devices  123 us (36%)
  Pallas kernels  83.4 us (24%)
  starting transfers between devices  69.9 us (20%)
  local copies, waits for them, and re-layouts  45.2 us (13%)
  other arithmetic  16.5 us (5%)
    ppermute x14, waiting for transfers between devices, over_z(): lax.ppermute(x, 'grp', [(2 * a + c, 2 * b + c) for a, b in pairs for c in...  68.6 us
    ppermute x23, waiting for transfers between devices, to_rep(): return lax.ppermute(x, 'rep', [(i, i ^ bit) for i in range(4)])  52 us
    pallas_call x1, Pallas kernels, middle(): pl.pallas_call(middle_kernel, out_shape=outs, in_specs=[SM] + [ANY] * 32...  31.8 us
    ppermute x14, starting transfers between devices, over_z(): lax.ppermute(x, 'grp', [(2 * a + c, 2 * b + c) for a, b in pairs for c in...  28.9 us
    pallas_call x2, Pallas kernels, attend(): pl.pallas_call(functools.partial(attend_kernel, student), out_shape=tuple...  26.8 us
    ppermute x23, starting transfers between devices, to_rep(): return lax.ppermute(x, 'rep', [(i, i ^ bit) for i in range(4)])  24.1 us
    unnamed x124, local copies, waits for them, and re-layouts  22.7 us
    pallas_call x1, Pallas kernels, attend_back(): pl.pallas_call(attend_back_kernel, out_shape=(part,) * 4 + (grad, grad),...  15.2 us
  transfers between devices with their start and end apart: 66, of which 24 were waited for; matrix products, arithmetic and copies ran while one was open for 16% of the time, Pallas kernels for 12%

profile of v1, /device:TPU:0, one launch (start us, length us, event | category | flops | bytes accessed | tf_op | source)
XLA Modules:
  0.0 340.8 jit_solution(741891616735130967)
XLA Ops:
  3.2 5.6 %pack.1 = (bf16[2,3,96,768]{3,2,1,0:T(8,128)(2,1)}, bf16[4,432,768]{2,1,0:T(8,128)(2,1)}, bf16[432,768]{1,0:T(8,128)(2,1)}, bf16[128,768]{1,0:T(8,128)(2,1)}, bf16[128,768]{1,0:T(8,128)(2,1)}) custom-call(s32[8]{0:T(128)} %concatenate.56.info, bf16[2,128,768]{2,1,0:T(8,128)(2,1)} %bitcast.82, f32[96,768]{1,0:T(8,128)} %lq.1, f32[96,768]{1,0:T(8,128)} %lk.1, ...), custom_call_target="tpu_custom_call" | custom-call | flops 4000000 | bytes 12000000 | tf_op jit(solution)/shard_map/pack/pallas_call | solution.py:623
  8.9 4.1 %collective-permute-start.1 = (bf16[432,768]{1,0:T(8,128)(2,1)}, bf16[432,768]{1,0:T(8,128)(2,1)}, u32[]{:S(2)}, u32[]{:S(2)}) collective-permute-start(bf16[432,768]{1,0:T(8,128)(2,1)} %get-tuple-element.53), channel_id=1, source_target_pairs={{0,4},{1,5},{4,6},{5,7},{6,2},{7,3},{2,0},{3,1},{8,12},{9,13},{12,... | collective-permute-start | bytes 1990664 | tf_op jit(solution)/shard_map/ppermute | solution.py:1183
  13.0 14.5 %collective-permute-done.1.refs_0_ = bf16[432,768]{1,0:T(8,128)(2,1)} collective-permute-done((bf16[432,768]{1,0:T(8,128)(2,1)}, bf16[432,768]{1,0:T(8,128)(2,1)}, u32[]{:S(2)}, u32[]{:S(2)}) %collective-permute-start.1) | collective-permute-done | bytes 663584 | tf_op jit(solution)/shard_map/ppermute | solution.py:1183
  30.0 3.4 %collective-permute-start.32 = (bf16[2,128,768]{2,1,0:T(8,128)(2,1)S(1)}, bf16[2,128,768]{2,1,0:T(8,128)(2,1)S(1)}, u32[]{:S(2)}, u32[]{:S(2)}) collective-permute-start(bf16[2,128,768]{2,1,0:T(8,128)(2,1)S(1)} %pad_maximum_fusion.refs_0_.refs_30_), channel_id=1, source_target_pairs={{0,4},{1,5},{4,6},{5,7},{6,2},{7,3},{2,0},{3,1},{8,12},{9,13},{12,... | collective-permute-start | bytes 1179656 | tf_op jit(solution)/shard_map/ppermute | solution.py:1183
  35.6 7.4 %collective-permute-done.32.refs_1_ = bf16[2,128,768]{2,1,0:T(8,128)(2,1)S(1)} collective-permute-done((bf16[2,128,768]{2,1,0:T(8,128)(2,1)S(1)}, bf16[2,128,768]{2,1,0:T(8,128)(2,1)S(1)}, u32[]{:S(2)}, u32[]{:S(2)}) %collective-permute-start.32) | collective-permute-done | bytes 393248 | tf_op jit(solution)/shard_map/ppermute | solution.py:1183
  43.0 3.4 collective-permute-start.33
  47.4 15.9 %collective-permute-done.33.refs_2_ = bf16[2,128,768]{2,1,0:T(8,128)(2,1)S(1)} collective-permute-done((bf16[2,128,768]{2,1,0:T(8,128)(2,1)S(1)}, bf16[2,128,768]{2,1,0:T(8,128)(2,1)S(1)}, u32[]{:S(2)}, u32[]{:S(2)}) %collective-permute-start.33) | collective-permute-done | bytes 393248 | tf_op jit(solution)/shard_map/ppermute | solution.py:1183
  65.5 3.4 collective-permute-start.34
  75.1 3.7 %collective-permute-done.34.refs_3_ = bf16[2,128,768]{2,1,0:T(8,128)(2,1)S(1)} collective-permute-done((bf16[2,128,768]{2,1,0:T(8,128)(2,1)}, bf16[2,128,768]{2,1,0:T(8,128)(2,1)S(1)}, u32[]{:S(2)}, u32[]{:S(2)}) %collective-permute-start.34) | collective-permute-done | bytes 393248 | tf_op jit(solution)/shard_map/ppermute | solution.py:1183
  80.1 1.8 collective-permute-done.5.refs_4_
  83.9 5.6 %collective-permute-done.21.refs_20_ = bf16[432,768]{1,0:T(8,128)(2,1)} collective-permute-done((bf16[432,768]{1,0:T(8,128)(2,1)}, bf16[432,768]{1,0:T(8,128)(2,1)}, u32[]{:S(2)}, u32[]{:S(2)}) %collective-permute-start.21) | collective-permute-done | bytes 663584 | tf_op jit(solution)/shard_map/ppermute | solution.py:1183
  90.8 1.5 collective-permute-done.12.refs_11_
  94.8 2.9 collective-permute-done.13.refs_12_
  107.7 13.3 %attend_tutor.1 = bf16[4,256,192]{2,1,0:T(8,128)(2,1)} custom-call(s32[8]{0:T(128)} %concatenate.56.info, bf16[2,128,768]{2,1,0:T(8,128)(2,1)} %copy-done.3, bf16[2,128,768]{2,1,0:T(8,128)(2,1)} %copy-done.43, bf16[2,128,768]{2,1,0:T(8,128)(2,1)} %copy-done.44, bf16[2,128,768]{2,1,0:T(8,128)(2,1)} %copy-done.45, ...), custom_call_target="tpu_custom_call" | custom-call | flops 6000000000 | bytes 4000000 | tf_op jit(solution)/shard_map/attend_tutor/pallas_call | solution.py:737
  121.0 2.1 copy.48
  123.0 4.5 %all-to-all-start.1 = ((bf16[4,256,192]{1,2,0:T(8,128)(2,1)}), bf16[4,256,192]{1,2,0:T(8,128)(2,1)S(1)}, u32[]{:S(2)}, u32[]{:S(2)}) async-start(bf16[4,256,192]{1,2,0:T(8,128)(2,1)} %copy.48), calls=%async_computation.1 | async-start | bytes 786432 | tf_op jit(solution)/shard_map/all_to_all | solution.py:1196
  132.7 13.5 %attend_student.1 = (bf16[4,256,192]{2,1,0:T(8,128)(2,1)}, bf16[3,1024,192]{2,1,0:T(8,128)(2,1)}, f32[8,1024]{1,0:T(8,128)}, f32[192,1024]{1,0:T(8,128)}) custom-call(s32[8]{0:T(128)} %concatenate.56.info, bf16[2,128,768]{2,1,0:T(8,128)(2,1)} %copy-done.3, bf16[2,128,768]{2,1,0:T(8,128)(2,1)} %copy-done.43, bf16[2,128,768]{2,1,0:T(8,128)(2,1)} %copy-done.44, ...), custom_call_target="tpu_custom_call" | custom-call | flops 6000000000 | bytes 4000000 | tf_op jit(solution)/shard_map/attend_student/pallas_call | solution.py:737
  146.2 2.0 copy.47
  149.2 5.0 %all-to-all-start = ((bf16[4,256,192]{1,2,0:T(8,128)(2,1)}), bf16[4,256,192]{1,2,0:T(8,128)(2,1)S(1)}, u32[]{:S(2)}, u32[]{:S(2)}) async-start(bf16[4,256,192]{1,2,0:T(8,128)(2,1)} %copy.47), calls=%async_computation | async-start | bytes 786432 | tf_op jit(solution)/shard_map/all_to_all | solution.py:1196
  158.4 4.6 %collective-permute-done.24.refs_23_ = bf16[192,768]{1,0:T(8,128)(2,1)S(1)} collective-permute-done((bf16[192,768]{1,0:T(8,128)(2,1)S(1)}, bf16[192,768]{1,0:T(8,128)(2,1)S(1)}, u32[]{:S(2)}, u32[]{:S(2)}) %collective-permute-start.24) | collective-permute-done | bytes 294944 | tf_op jit(solution)/shard_map/ppermute | solution.py:1192
  169.5 31.8 %middle.1 = (bf16[128,768]{1,0:T(8,128)(2,1)}, bf16[128,768]{1,0:T(8,128)(2,1)}, f32[256,768]{1,0:T(8,128)}, bf16[4,256,192]{2,1,0:T(8,128)(2,1)}, f32[16,1,768]...) custom-call(s32[8]{0:T(128)} %concatenate.56.info, ...), custom_call_target="tpu_custom_call" | custom-call | flops 15000000512 | bytes 30000000 | tf_op jit(solution)/shard_map/middle/pallas_call | solution.py:1097
  203.2 1.9 collective-permute-done.37
  207.4 2.5 collective-permute-done.38
  211.2 2.9 collective-permute-done.39
  214.1 1.8 collective-permute-start.40
  217.0 3.7 %all-to-all-start.2 = ((bf16[4,256,192]{1,2,0:T(8,128)(2,1)}), bf16[4,256,192]{1,2,0:T(8,128)(2,1)S(1)}, u32[]{:S(2)}, u32[]{:S(2)}) async-start(bf16[4,256,192]{1,2,0:T(8,128)(2,1)} %copy.51), calls=%async_computation.2 | async-start | bytes 786432 | tf_op jit(solution)/shard_map/all_to_all | solution.py:1196
  221.3 2.9 collective-permute-start.41
  224.9 7.5 %collective-permute-done.41 = f32[16,768]{1,0:T(8,128)S(1)} collective-permute-done((f32[16,768]{1,0:T(8,128)S(1)}, f32[16,768]{1,0:T(8,128)S(1)}, u32[]{:S(2)}, u32[]{:S(2)}) %collective-permute-start.41) | collective-permute-done | bytes 49184 | tf_op jit(solution)/shard_map/ppermute | solution.py:1183
  232.6 3.1 add_convert_fusion
  236.7 2.6 add_convert_fusion.1
  244.1 15.2 %attend_back.1 = (bf16[256,768]{1,0:T(8,128)(2,1)}, bf16[256,768]{1,0:T(8,128)(2,1)}, bf16[256,768]{1,0:T(8,128)(2,1)}, bf16[256,768]{1,0:T(8,128)(2,1)}, bf16[3...) custom-call(s32[8]{0:T(128)} %concatenate.56.info, bf16[2,128,768]{2,1,0:T(8,128)(2,1)} %copy-done.3, ...), custom_call_target="tpu_custom_call" | custom-call | flops 12000000000 | bytes 6000000 | tf_op jit(solution)/shard_map/attend_back/pallas_call | solution.py:864
  259.5 5.7 %collective-permute-done.48 = bf16[2,4,96,768]{3,2,1,0:T(8,128)(2,1)} collective-permute-done((bf16[2,4,96,768]{3,2,1,0:T(8,128)(2,1)}, bf16[2,4,96,768]{3,2,1,0:T(8,128)(2,1)}, u32[]{:S(2)}, u32[]{:S(2)}) %collective-permute-start.48) | collective-permute-done | bytes 1179680 | tf_op jit(solution)/shard_map/ppermute | solution.py:1192
  267.0 5.8 %collective-permute-done.52 = bf16[2,4,128,768]{3,2,1,0:T(8,128)(2,1)S(1)} collective-permute-done((bf16[2,4,128,768]{3,2,1,0:T(8,128)(2,1)}, bf16[2,4,128,768]{3,2,1,0:T(8,128)(2,1)S(1)}, u32[]{:S(2)}, u32[]{:S(2)}) %collective-permute-start.52) | collective-permute-done | bytes 1572896 | tf_op jit(solution)/shard_map/ppermute | solution.py:1192
  274.3 1.5 collective-permute-start.53
  277.0 5.1 %collective-permute-done.49 = bf16[4,96,768]{2,1,0:T(8,128)(2,1)S(1)} collective-permute-done((bf16[4,96,768]{2,1,0:T(8,128)(2,1)S(1)}, bf16[4,96,768]{2,1,0:T(8,128)(2,1)S(1)}, u32[]{:S(2)}, u32[]{:S(2)}) %collective-permute-start.49) | collective-permute-done | bytes 589856 | tf_op jit(solution)/shard_map/ppermute | solution.py:1192
  282.1 1.5 fusion.1
  283.7 8.2 %collective-permute-done.53 = bf16[4,128,768]{2,1,0:T(8,128)(2,1)S(1)} collective-permute-done((bf16[4,128,768]{2,1,0:T(8,128)(2,1)S(1)}, bf16[4,128,768]{2,1,0:T(8,128)(2,1)S(1)}, u32[]{:S(2)}, u32[]{:S(2)}) %collective-permute-start.53) | collective-permute-done | bytes 786464 | tf_op jit(solution)/shard_map/ppermute | solution.py:1192
  291.9 1.6 fusion
  294.6 4.1 %collective-permute-start.44 = (bf16[256,768]{1,0:T(8,128)(2,1)S(1)}, bf16[256,768]{1,0:T(8,128)(2,1)S(1)}, u32[]{:S(2)}, u32[]{:S(2)}) collective-permute-start(bf16[256,768]{1,0:T(8,128)(2,1)S(1)} %add_convert_fusion.7), channel_id=1, source_target_pairs={{0,4},{1,5},{4,6},{5,7},{6,2},{7,3},{2,0},{3,1},{8,12},{9,13},{12,... | collective-permute-start | bytes 1179656 | tf_op jit(solution)/shard_map/ppermute | solution.py:1183
  299.9 2.5 collective-permute-done.54
  302.5 2.7 collective-permute-start.55
  307.0 4.2 %collective-permute-done.55 = bf16[224,768]{1,0:T(8,128)(2,1)S(1)} collective-permute-done((bf16[224,768]{1,0:T(8,128)(2,1)S(1)}, bf16[224,768]{1,0:T(8,128)(2,1)S(1)}, u32[]{:S(2)}, u32[]{:S(2)}) %collective-permute-start.55) | collective-permute-done | bytes 344096 | tf_op jit(solution)/shard_map/ppermute | solution.py:1183
  311.3 2.2 collective-permute-start.56
  313.7 5.8 %collective-permute-done.56 = bf16[224,768]{1,0:T(8,128)(2,1)S(1)} collective-permute-done((bf16[224,768]{1,0:T(8,128)(2,1)S(1)}, bf16[224,768]{1,0:T(8,128)(2,1)S(1)}, u32[]{:S(2)}, u32[]{:S(2)}) %collective-permute-start.56) | collective-permute-done | bytes 344096 | tf_op jit(solution)/shard_map/ppermute | solution.py:1183
  319.6 1.5 collective-permute-start.57
  324.7 4.6 %collective-permute-done.57.refs_1_ = bf16[224,768]{1,0:T(8,128)(2,1)S(1)} collective-permute-done((bf16[224,768]{1,0:T(8,128)(2,1)S(1)}, bf16[224,768]{1,0:T(8,128)(2,1)S(1)}, u32[]{:S(2)}, u32[]{:S(2)}) %collective-permute-start.57) | collective-permute-done | bytes 344096 | tf_op jit(solution)/shard_map/ppermute | solution.py:1192
  329.3 4.8 %collective-permute-done.58.refs_2_ = bf16[224,768]{1,0:T(8,128)(2,1)S(1)} collective-permute-done((bf16[224,768]{1,0:T(8,128)(2,1)S(1)}, bf16[224,768]{1,0:T(8,128)(2,1)S(1)}, u32[]{:S(2)}, u32[]{:S(2)}) %collective-permute-start.58) | collective-permute-done | bytes 344096 | tf_op jit(solution)/shard_map/ppermute | solution.py:1192
  335.6 4.1 %finish.1 = (f32[384,768]{1,0:T(8,128)}, f32[96,3072]{1,0:T(8,128)}, f32[96,768]{1,0:T(8,128)}, f32[96,768]{1,0:T(8,128)}, f32[96,768]{1,0:T(8,128)}, /*index=5*/f32[96,768]{1,0:T(8,128)}) custom-call(s32[8]{0:T(128)} %concatenate.56.info, bf16[224,768]{1,0:T(8,128)(2,1)} %copy-done.7, bf16[224,768]{1,0:T(8,128)(2,1)} %copy-done.17, ...), custom_call_target="tpu_custom_call" | custom-call | flops 1000000 | bytes 8000000 | tf_op jit(solution)/shard_map/finish/pallas_call | solution.py:1142
  (278 shorter events, 77.5 us)
Async XLA Ops:
  8.9 18.6 %collective-permute-start.1 = (bf16[432,768]{1,0:T(8,128)(2,1)}, bf16[432,768]{1,0:T(8,128)(2,1)}, u32[]{:S(2)}, u32[]{:S(2)}) collective-permute-start(bf16[432,768]{1,0:T(8,128)(2,1)} %get-tuple-element.53), channel_id=1, source_target_pairs={{0,4},{1,5},{4,6},{5,7},{6,2},{7,3},{2,0},{3,1},{8,12},{9,13},{12,... | collective-permute-start | bytes 1990664 | tf_op jit(solution)/shard_map/ppermute | solution.py:1183
  13.0 16.0 %collective-permute-start.31 = (bf16[128,768]{1,0:T(8,128)(2,1)}, bf16[128,768]{1,0:T(8,128)(2,1)S(1)}, u32[]{:S(2)}, u32[]{:S(2)}) collective-permute-start(bf16[128,768]{1,0:T(8,128)(2,1)} %get-tuple-element.55), channel_id=1, source_target_pairs={{0,1},{1,0},{2,3},{3,2},{4,5},{5,4},{6,7},{7,6},{8,9},{9,8},{10,11... | collective-permute-start | bytes 589832 | tf_op jit(solution)/shard_map/ppermute | solution.py:1189
  27.5 18.9 %collective-permute-start.2 = (bf16[432,768]{1,0:T(8,128)(2,1)}, bf16[432,768]{1,0:T(8,128)(2,1)}, u32[]{:S(2)}, u32[]{:S(2)}) collective-permute-start(bf16[432,768]{1,0:T(8,128)(2,1)} %collective-permute-done.1.refs_0_), channel_id=1, source_target_pairs={{0,8},{8,0},{16,24},{24,16},{1,9},{9,1},{17,25},{25,17},{2,10},{10... | collective-permute-start | bytes 1990664 | tf_op jit(solution)/shard_map/ppermute | solution.py:1192
  30.0 13.0 %collective-permute-start.32 = (bf16[2,128,768]{2,1,0:T(8,128)(2,1)S(1)}, bf16[2,128,768]{2,1,0:T(8,128)(2,1)S(1)}, u32[]{:S(2)}, u32[]{:S(2)}) collective-permute-start(bf16[2,128,768]{2,1,0:T(8,128)(2,1)S(1)} %pad_maximum_fusion.refs_0_.refs_30_), channel_id=1, source_target_pairs={{0,4},{1,5},{4,6},{5,7},{6,2},{7,3},{2,0},{3,1},{8,12},{9,13},{12,... | collective-permute-start | bytes 1179656 | tf_op jit(solution)/shard_map/ppermute | solution.py:1183
  33.4 37.0 %collective-permute-start.35 = (bf16[2,3,96,768]{3,2,1,0:T(8,128)(2,1)}, bf16[2,3,96,768]{3,2,1,0:T(8,128)(2,1)S(1)}, u32[]{:S(2)}, u32[]{:S(2)}) collective-permute-start(bf16[2,3,96,768]{3,2,1,0:T(8,128)(2,1)} %get-tuple-element.56), channel_id=1, source_target_pairs={{0,1},{1,0},{2,3},{3,2},{4,5},{5,4},{6,7},{7,6},{8,9},{9,8},{10,11... | collective-permute-start | bytes 2654216 | tf_op jit(solution)/shard_map/ppermute | solution.py:1189
  33.4 32.1 %collective-permute-start.11 = (bf16[432,768]{1,0:T(8,128)(2,1)}, bf16[432,768]{1,0:T(8,128)(2,1)}, u32[]{:S(2)}, u32[]{:S(2)}) collective-permute-start(bf16[432,768]{1,0:T(8,128)(2,1)} %collective-permute-done.1.refs_0_), channel_id=1, source_target_pairs={{0,4},{1,5},{4,6},{5,7},{6,2},{7,3},{2,0},{3,1},{8,12},{9,13},{12,... | collective-permute-start | bytes 1990664 | tf_op jit(solution)/shard_map/ppermute | solution.py:1183
  34.1 34.8 %collective-permute-start.3 = (bf16[432,768]{1,0:T(8,128)(2,1)}, bf16[432,768]{1,0:T(8,128)(2,1)S(1)}, u32[]{:S(2)}, u32[]{:S(2)}) collective-permute-start(bf16[432,768]{1,0:T(8,128)(2,1)} %collective-permute-done.1.refs_0_), channel_id=1, source_target_pairs={{0,16},{8,24},{16,0},{24,8},{1,17},{9,25},{17,1},{25,9},{2,18},{10... | collective-permute-start | bytes 1990664 | tf_op jit(solution)/shard_map/ppermute | solution.py:1192
  43.0 20.3 %collective-permute-start.33 = (bf16[2,128,768]{2,1,0:T(8,128)(2,1)S(1)}, bf16[2,128,768]{2,1,0:T(8,128)(2,1)S(1)}, u32[]{:S(2)}, u32[]{:S(2)}) collective-permute-start(bf16[2,128,768]{2,1,0:T(8,128)(2,1)S(1)} %collective-permute-done.32.refs_1_), channel_id=1, source_target_pairs={{0,4},{1,5},{4,6},{5,7},{6,2},{7,3},{2,0},{3,1},{8,12},{9,13},{12,... | collective-permute-start | bytes 1179656 | tf_op jit(solution)/shard_map/ppermute | solution.py:1183
  46.4 25.9 %collective-permute-start.6 = (bf16[432,768]{1,0:T(8,128)(2,1)}, bf16[432,768]{1,0:T(8,128)(2,1)}, u32[]{:S(2)}, u32[]{:S(2)}) collective-permute-start(bf16[432,768]{1,0:T(8,128)(2,1)} %collective-permute-done.1.refs_0_), channel_id=1, source_target_pairs={{0,1},{1,0},{2,3},{3,2},{4,5},{5,4},{6,7},{7,6},{8,9},{9,8},{10,11... | collective-permute-start | bytes 1990664 | tf_op jit(solution)/shard_map/ppermute | solution.py:1189
  65.5 13.3 %collective-permute-start.34 = (bf16[2,128,768]{2,1,0:T(8,128)(2,1)}, bf16[2,128,768]{2,1,0:T(8,128)(2,1)S(1)}, u32[]{:S(2)}, u32[]{:S(2)}) collective-permute-start(bf16[2,128,768]{2,1,0:T(8,128)(2,1)} %copy-done.44), channel_id=1, source_target_pairs={{0,4},{1,5},{4,6},{5,7},{6,2},{7,3},{2,0},{3,1},{8,12},{9,13},{12,... | collective-permute-start | bytes 1179656 | tf_op jit(solution)/shard_map/ppermute | solution.py:1183
  68.9 20.6 %collective-permute-start.21 = (bf16[432,768]{1,0:T(8,128)(2,1)}, bf16[432,768]{1,0:T(8,128)(2,1)}, u32[]{:S(2)}, u32[]{:S(2)}) collective-permute-start(bf16[432,768]{1,0:T(8,128)(2,1)} %collective-permute-done.11.refs_10_), channel_id=1, source_target_pairs={{0,4},{1,5},{4,6},{5,7},{6,2},{7,3},{2,0},{3,1},{8,12},{9,13},{12,... | collective-permute-start | bytes 1990664 | tf_op jit(solution)/shard_map/ppermute | solution.py:1183
  72.3 20.1 %collective-permute-start.12 = (bf16[432,768]{1,0:T(8,128)(2,1)}, bf16[432,768]{1,0:T(8,128)(2,1)S(1)}, u32[]{:S(2)}, u32[]{:S(2)}) collective-permute-start(bf16[432,768]{1,0:T(8,128)(2,1)} %collective-permute-done.11.refs_10_), channel_id=1, source_target_pairs={{0,8},{8,0},{16,24},{24,16},{1,9},{9,1},{17,25},{25,17},{2,10},{10... | collective-permute-start | bytes 1990664 | tf_op jit(solution)/shard_map/ppermute | solution.py:1192
  78.8 77.7 %collective-permute-start = (bf16[4,432,768]{2,1,0:T(8,128)(2,1)}, bf16[4,432,768]{2,1,0:T(8,128)(2,1)}, u32[]{:S(2)}, u32[]{:S(2)}) collective-permute-start(bf16[4,432,768]{2,1,0:T(8,128)(2,1)} %get-tuple-element.52.own), channel_id=1, source_target_pairs={{0,1},{1,0},{2,3},{3,2},{4,5},{5,4},{6,7},{7,6},{8,9},{9,8},{10,11... | collective-permute-start | bytes 7962632 | tf_op jit(solution)/shard_map/ppermute | solution.py:1189
  82.0 15.7 %collective-permute-start.13 = (bf16[432,768]{1,0:T(8,128)(2,1)}, bf16[432,768]{1,0:T(8,128)(2,1)S(1)}, u32[]{:S(2)}, u32[]{:S(2)}) collective-permute-start(bf16[432,768]{1,0:T(8,128)(2,1)} %collective-permute-done.11.refs_10_), channel_id=1, source_target_pairs={{0,16},{8,24},{16,0},{24,8},{1,17},{9,25},{17,1},{25,9},{2,18},{10... | collective-permute-start | bytes 1990664 | tf_op jit(solution)/shard_map/ppermute | solution.py:1192
  82.5 15.2 %collective-permute-start.16 = (bf16[432,768]{1,0:T(8,128)(2,1)}, bf16[432,768]{1,0:T(8,128)(2,1)S(1)}, u32[]{:S(2)}, u32[]{:S(2)}) collective-permute-start(bf16[432,768]{1,0:T(8,128)(2,1)} %collective-permute-done.11.refs_10_), channel_id=1, source_target_pairs={{0,1},{1,0},{2,3},{3,2},{4,5},{5,4},{6,7},{7,6},{8,9},{9,8},{10,11... | collective-permute-start | bytes 1990664 | tf_op jit(solution)/shard_map/ppermute | solution.py:1189
  89.5 12.3 %collective-permute-start.7 = (bf16[432,768]{1,0:T(8,128)(2,1)}, bf16[432,768]{1,0:T(8,128)(2,1)}, u32[]{:S(2)}, u32[]{:S(2)}) collective-permute-start(bf16[432,768]{1,0:T(8,128)(2,1)} %collective-permute-done.2.refs_1_), channel_id=1, source_target_pairs={{0,1},{1,0},{2,3},{3,2},{4,5},{5,4},{6,7},{7,6},{8,9},{9,8},{10,11... | collective-permute-start | bytes 1990664 | tf_op jit(solution)/shard_map/ppermute | solution.py:1189
  92.4 11.7 %collective-permute-start.8 = (bf16[432,768]{1,0:T(8,128)(2,1)S(1)}, bf16[432,768]{1,0:T(8,128)(2,1)}, u32[]{:S(2)}, u32[]{:S(2)}) collective-permute-start(bf16[432,768]{1,0:T(8,128)(2,1)S(1)} %collective-permute-done.3.refs_2_), channel_id=1, source_target_pairs={{0,1},{1,0},{2,3},{3,2},{4,5},{5,4},{6,7},{7,6},{8,9},{9,8},{10,11... | collective-permute-start | bytes 1990664 | tf_op jit(solution)/shard_map/ppermute | solution.py:1189
  101.8 26.4 %collective-permute-start.23 = (bf16[432,768]{1,0:T(8,128)(2,1)}, bf16[432,768]{1,0:T(8,128)(2,1)}, u32[]{:S(2)}, u32[]{:S(2)}) collective-permute-start(bf16[432,768]{1,0:T(8,128)(2,1)} %collective-permute-done.21.refs_20_), channel_id=1, source_target_pairs={{0,16},{8,24},{16,0},{24,8},{1,17},{9,25},{17,1},{25,9},{2,18},{10... | collective-permute-start | bytes 1990664 | tf_op jit(solution)/shard_map/ppermute | solution.py:1192
  104.1 23.5 %collective-permute-start.15 = (bf16[240,768]{1,0:T(8,128)(2,1)S(1)}, bf16[240,768]{1,0:T(8,128)(2,1)S(1)}, u32[]{:S(2)}, u32[]{:S(2)}) collective-permute-start(bf16[240,768]{1,0:T(8,128)(2,1)S(1)} %slice.213), channel_id=1, source_target_pairs={{0,8},{8,0},{16,24},{24,16},{1,9},{9,1},{17,25},{25,17},{2,10},{10... | collective-permute-start | bytes 1105928 | tf_op jit(solution)/shard_map/ppermute | solution.py:1192
  104.7 27.4 %collective-permute-start.22 = (bf16[432,768]{1,0:T(8,128)(2,1)}, bf16[432,768]{1,0:T(8,128)(2,1)}, u32[]{:S(2)}, u32[]{:S(2)}) collective-permute-start(bf16[432,768]{1,0:T(8,128)(2,1)} %collective-permute-done.21.refs_20_), channel_id=1, source_target_pairs={{0,8},{8,0},{16,24},{24,16},{1,9},{9,1},{17,25},{25,17},{2,10},{10... | collective-permute-start | bytes 1990664 | tf_op jit(solution)/shard_map/ppermute | solution.py:1192
  107.7 20.2 %collective-permute-start.19 = (bf16[192,768]{1,0:T(8,128)(2,1)}, bf16[192,768]{1,0:T(8,128)(2,1)S(1)}, u32[]{:S(2)}, u32[]{:S(2)}) collective-permute-start(bf16[192,768]{1,0:T(8,128)(2,1)} %collective-permute-done.14.refs_13_), channel_id=1, source_target_pairs={{0,1},{1,0},{2,3},{3,2},{4,5},{5,4},{6,7},{7,6},{8,9},{9,8},{10,11... | collective-permute-start | bytes 884744 | tf_op jit(solution)/shard_map/ppermute | solution.py:1189
  123.0 26.2 %all-to-all-start.1 = ((bf16[4,256,192]{1,2,0:T(8,128)(2,1)}), bf16[4,256,192]{1,2,0:T(8,128)(2,1)S(1)}, u32[]{:S(2)}, u32[]{:S(2)}) async-start(bf16[4,256,192]{1,2,0:T(8,128)(2,1)} %copy.48), calls=%async_computation.1 | async-start | bytes 786432 | tf_op jit(solution)/shard_map/all_to_all | solution.py:1196
  127.6 26.6 %collective-permute-start.17 = (bf16[432,768]{1,0:T(8,128)(2,1)S(1)}, bf16[432,768]{1,0:T(8,128)(2,1)}, u32[]{:S(2)}, u32[]{:S(2)}) collective-permute-start(bf16[432,768]{1,0:T(8,128)(2,1)S(1)} %copy-done.25), channel_id=1, source_target_pairs={{0,1},{1,0},{2,3},{3,2},{4,5},{5,4},{6,7},{7,6},{8,9},{9,8},{10,11... | collective-permute-start | bytes 1990664 | tf_op jit(solution)/shard_map/ppermute | solution.py:1189
  127.9 26.8 %collective-permute-start.18 = (bf16[432,768]{1,0:T(8,128)(2,1)S(1)}, bf16[432,768]{1,0:T(8,128)(2,1)}, u32[]{:S(2)}, u32[]{:S(2)}) collective-permute-start(bf16[432,768]{1,0:T(8,128)(2,1)S(1)} %copy-done.22), channel_id=1, source_target_pairs={{0,1},{1,0},{2,3},{3,2},{4,5},{5,4},{6,7},{7,6},{8,9},{9,8},{10,11... | collective-permute-start | bytes 1990664 | tf_op jit(solution)/shard_map/ppermute | solution.py:1189
  128.2 26.6 %collective-permute-start.26 = (bf16[432,768]{1,0:T(8,128)(2,1)}, bf16[432,768]{1,0:T(8,128)(2,1)}, u32[]{:S(2)}, u32[]{:S(2)}) collective-permute-start(bf16[432,768]{1,0:T(8,128)(2,1)} %collective-permute-done.21.refs_20_), channel_id=1, source_target_pairs={{0,1},{1,0},{2,3},{3,2},{4,5},{5,4},{6,7},{7,6},{8,9},{9,8},{10,11... | collective-permute-start | bytes 1990664 | tf_op jit(solution)/shard_map/ppermute | solution.py:1189
  132.1 24.6 %collective-permute-start.25 = (bf16[240,768]{1,0:T(8,128)(2,1)S(1)}, bf16[240,768]{1,0:T(8,128)(2,1)}, u32[]{:S(2)}, u32[]{:S(2)}) collective-permute-start(bf16[240,768]{1,0:T(8,128)(2,1)S(1)} %slice.215), channel_id=1, source_target_pairs={{0,8},{8,0},{16,24},{24,16},{1,9},{9,1},{17,25},{25,17},{2,10},{10... | collective-permute-start | bytes 1105928 | tf_op jit(solution)/shard_map/ppermute | solution.py:1192
  149.2 18.0 %all-to-all-start = ((bf16[4,256,192]{1,2,0:T(8,128)(2,1)}), bf16[4,256,192]{1,2,0:T(8,128)(2,1)S(1)}, u32[]{:S(2)}, u32[]{:S(2)}) async-start(bf16[4,256,192]{1,2,0:T(8,128)(2,1)} %copy.47), calls=%async_computation | async-start | bytes 786432 | tf_op jit(solution)/shard_map/all_to_all | solution.py:1196
  154.7 13.5 %collective-permute-start.27 = (bf16[432,768]{1,0:T(8,128)(2,1)}, bf16[432,768]{1,0:T(8,128)(2,1)S(1)}, u32[]{:S(2)}, u32[]{:S(2)}) collective-permute-start(bf16[432,768]{1,0:T(8,128)(2,1)} %collective-permute-done.22.refs_21_), channel_id=1, source_target_pairs={{0,1},{1,0},{2,3},{3,2},{4,5},{5,4},{6,7},{7,6},{8,9},{9,8},{10,11... | collective-permute-start | bytes 1990664 | tf_op jit(solution)/shard_map/ppermute | solution.py:1189
  154.7 13.5 %collective-permute-start.28 = (bf16[432,768]{1,0:T(8,128)(2,1)}, bf16[432,768]{1,0:T(8,128)(2,1)S(1)}, u32[]{:S(2)}, u32[]{:S(2)}) collective-permute-start(bf16[432,768]{1,0:T(8,128)(2,1)} %collective-permute-done.23.refs_22_), channel_id=1, source_target_pairs={{0,1},{1,0},{2,3},{3,2},{4,5},{5,4},{6,7},{7,6},{8,9},{9,8},{10,11... | collective-permute-start | bytes 1990664 | tf_op jit(solution)/shard_map/ppermute | solution.py:1189
  156.6 11.7 %collective-permute-start.20 = (bf16[240,768]{1,0:T(8,128)(2,1)S(1)}, bf16[240,768]{1,0:T(8,128)(2,1)}, u32[]{:S(2)}, u32[]{:S(2)}) collective-permute-start(bf16[240,768]{1,0:T(8,128)(2,1)S(1)} %copy-done.49), channel_id=1, source_target_pairs={{0,1},{1,0},{2,3},{3,2},{4,5},{5,4},{6,7},{7,6},{8,9},{9,8},{10,11... | collective-permute-start | bytes 1105928 | tf_op jit(solution)/shard_map/ppermute | solution.py:1189
  201.3 31.2 %collective-permute-start.51 = (bf16[2,4,128,768]{3,2,1,0:T(8,128)(2,1)}, bf16[2,4,128,768]{3,2,1,0:T(8,128)(2,1)}, u32[]{:S(2)}, u32[]{:S(2)}) collective-permute-start(bf16[2,4,128,768]{3,2,1,0:T(8,128)(2,1)} %get-tuple-element.77), channel_id=1, source_target_pairs={{0,1},{1,0},{2,3},{3,2},{4,5},{5,4},{6,7},{7,6},{8,9},{9,8},{10,11... | collective-permute-start | bytes 4718600 | tf_op jit(solution)/shard_map/ppermute | solution.py:1189
  202.7 34.0 %collective-permute-start.47 = (bf16[2,4,96,768]{3,2,1,0:T(8,128)(2,1)}, bf16[2,4,96,768]{3,2,1,0:T(8,128)(2,1)}, u32[]{:S(2)}, u32[]{:S(2)}) collective-permute-start(bf16[2,4,96,768]{3,2,1,0:T(8,128)(2,1)} %get-tuple-element.73), channel_id=1, source_target_pairs={{0,1},{1,0},{2,3},{3,2},{4,5},{5,4},{6,7},{7,6},{8,9},{9,8},{10,11... | collective-permute-start | bytes 3538952 | tf_op jit(solution)/shard_map/ppermute | solution.py:1189
  217.0 26.1 %all-to-all-start.2 = ((bf16[4,256,192]{1,2,0:T(8,128)(2,1)}), bf16[4,256,192]{1,2,0:T(8,128)(2,1)S(1)}, u32[]{:S(2)}, u32[]{:S(2)}) async-start(bf16[4,256,192]{1,2,0:T(8,128)(2,1)} %copy.51), calls=%async_computation.2 | async-start | bytes 786432 | tf_op jit(solution)/shard_map/all_to_all | solution.py:1196
  220.7 38.8 %collective-permute-start.46 = (bf16[2,4,96,768]{3,2,1,0:T(8,128)(2,1)}, bf16[2,4,96,768]{3,2,1,0:T(8,128)(2,1)}, u32[]{:S(2)}, u32[]{:S(2)}) collective-permute-start(bf16[2,4,96,768]{3,2,1,0:T(8,128)(2,1)} %get-tuple-element.71), channel_id=1, source_target_pairs={{0,1},{1,0},{2,3},{3,2},{4,5},{5,4},{6,7},{7,6},{8,9},{9,8},{10,11... | collective-permute-start | bytes 3538952 | tf_op jit(solution)/shard_map/ppermute | solution.py:1189
  220.8 46.2 %collective-permute-start.50 = (bf16[2,4,128,768]{3,2,1,0:T(8,128)(2,1)}, bf16[2,4,128,768]{3,2,1,0:T(8,128)(2,1)}, u32[]{:S(2)}, u32[]{:S(2)}) collective-permute-start(bf16[2,4,128,768]{3,2,1,0:T(8,128)(2,1)} %get-tuple-element.75), channel_id=1, source_target_pairs={{0,1},{1,0},{2,3},{3,2},{4,5},{5,4},{6,7},{7,6},{8,9},{9,8},{10,11... | collective-permute-start | bytes 4718600 | tf_op jit(solution)/shard_map/ppermute | solution.py:1189
  235.7 37.1 %collective-permute-start.52 = (bf16[2,4,128,768]{3,2,1,0:T(8,128)(2,1)}, bf16[2,4,128,768]{3,2,1,0:T(8,128)(2,1)S(1)}, u32[]{:S(2)}, u32[]{:S(2)}) collective-permute-start(bf16[2,4,128,768]{3,2,1,0:T(8,128)(2,1)} %add_convert_fusion), channel_id=1, source_target_pairs={{0,16},{8,24},{16,0},{24,8},{1,17},{9,25},{17,1},{25,9},{2,18},{10... | collective-permute-start | bytes 4718600 | tf_op jit(solution)/shard_map/ppermute | solution.py:1192
  239.3 25.9 %collective-permute-start.48 = (bf16[2,4,96,768]{3,2,1,0:T(8,128)(2,1)}, bf16[2,4,96,768]{3,2,1,0:T(8,128)(2,1)}, u32[]{:S(2)}, u32[]{:S(2)}) collective-permute-start(bf16[2,4,96,768]{3,2,1,0:T(8,128)(2,1)} %add_convert_fusion.1), channel_id=1, source_target_pairs={{0,8},{8,0},{16,24},{24,16},{1,9},{9,1},{17,25},{25,17},{2,10},{10... | collective-permute-start | bytes 3538952 | tf_op jit(solution)/shard_map/ppermute | solution.py:1192
  259.3 16.7 %collective-permute-start.60 = (bf16[304,768]{1,0:T(8,128)(2,1)}, bf16[304,768]{1,0:T(8,128)(2,1)S(1)}, u32[]{:S(2)}, u32[]{:S(2)}) collective-permute-start(bf16[304,768]{1,0:T(8,128)(2,1)} %get-tuple-element.79), channel_id=1, source_target_pairs={{0,1},{1,0},{2,3},{3,2},{4,5},{5,4},{6,7},{7,6},{8,9},{9,8},{10,11... | collective-permute-start | bytes 1400840 | tf_op jit(solution)/shard_map/ppermute | solution.py:1189
  259.4 16.4 %collective-permute-start.42 = (bf16[256,768]{1,0:T(8,128)(2,1)}, bf16[256,768]{1,0:T(8,128)(2,1)S(1)}, u32[]{:S(2)}, u32[]{:S(2)}) collective-permute-start(bf16[256,768]{1,0:T(8,128)(2,1)} %get-tuple-element.66), channel_id=1, source_target_pairs={{0,4},{1,5},{4,6},{5,7},{6,2},{7,3},{2,0},{3,1},{8,12},{9,13},{12,... | collective-permute-start | bytes 1179656 | tf_op jit(solution)/shard_map/ppermute | solution.py:1183
  266.7 15.5 %collective-permute-start.49 = (bf16[4,96,768]{2,1,0:T(8,128)(2,1)S(1)}, bf16[4,96,768]{2,1,0:T(8,128)(2,1)S(1)}, u32[]{:S(2)}, u32[]{:S(2)}) collective-permute-start(bf16[4,96,768]{2,1,0:T(8,128)(2,1)S(1)} %fusion.6), channel_id=1, source_target_pairs={{0,16},{8,24},{16,0},{24,8},{1,17},{9,25},{17,1},{25,9},{2,18},{10... | collective-permute-start | bytes 1769480 | tf_op jit(solution)/shard_map/ppermute | solution.py:1192
  274.3 17.6 %collective-permute-start.53 = (bf16[4,128,768]{2,1,0:T(8,128)(2,1)S(1)}, bf16[4,128,768]{2,1,0:T(8,128)(2,1)S(1)}, u32[]{:S(2)}, u32[]{:S(2)}) collective-permute-start(bf16[4,128,768]{2,1,0:T(8,128)(2,1)S(1)} %fusion.2), channel_id=1, source_target_pairs={{0,8},{8,0},{16,24},{24,16},{1,9},{9,1},{17,25},{25,17},{2,10},{10... | collective-permute-start | bytes 2359304 | tf_op jit(solution)/shard_map/ppermute | solution.py:1192
  275.9 17.6 %collective-permute-start.43 = (bf16[256,768]{1,0:T(8,128)(2,1)S(1)}, bf16[256,768]{1,0:T(8,128)(2,1)S(1)}, u32[]{:S(2)}, u32[]{:S(2)}) collective-permute-start(bf16[256,768]{1,0:T(8,128)(2,1)S(1)} %add_convert_fusion.8), channel_id=1, source_target_pairs={{0,4},{1,5},{4,6},{5,7},{6,2},{7,3},{2,0},{3,1},{8,12},{9,13},{12,... | collective-permute-start | bytes 1179656 | tf_op jit(solution)/shard_map/ppermute | solution.py:1183
  276.2 22.5 %collective-permute-start.61 = (bf16[304,768]{1,0:T(8,128)(2,1)S(1)}, bf16[304,768]{1,0:T(8,128)(2,1)S(1)}, u32[]{:S(2)}, u32[]{:S(2)}) collective-permute-start(bf16[304,768]{1,0:T(8,128)(2,1)S(1)} %add_convert_fusion.6), channel_id=1, source_target_pairs={{0,8},{8,0},{16,24},{24,16},{1,9},{9,1},{17,25},{25,17},{2,10},{10... | collective-permute-start | bytes 1400840 | tf_op jit(solution)/shard_map/ppermute | solution.py:1192
  294.6 12.1 %collective-permute-start.44 = (bf16[256,768]{1,0:T(8,128)(2,1)S(1)}, bf16[256,768]{1,0:T(8,128)(2,1)S(1)}, u32[]{:S(2)}, u32[]{:S(2)}) collective-permute-start(bf16[256,768]{1,0:T(8,128)(2,1)S(1)} %add_convert_fusion.7), channel_id=1, source_target_pairs={{0,4},{1,5},{4,6},{5,7},{6,2},{7,3},{2,0},{3,1},{8,12},{9,13},{12,... | collective-permute-start | bytes 1179656 | tf_op jit(solution)/shard_map/ppermute | solution.py:1183
  298.8 14.7 %collective-permute-start.62 = (bf16[304,768]{1,0:T(8,128)(2,1)S(1)}, bf16[304,768]{1,0:T(8,128)(2,1)S(1)}, u32[]{:S(2)}, u32[]{:S(2)}) collective-permute-start(bf16[304,768]{1,0:T(8,128)(2,1)S(1)} %add_convert_fusion.5), channel_id=1, source_target_pairs={{0,16},{8,24},{16,0},{24,8},{1,17},{9,25},{17,1},{25,9},{2,18},{10... | collective-permute-start | bytes 1400840 | tf_op jit(solution)/shard_map/ppermute | solution.py:1192
  306.9 16.8 %collective-permute-start.45 = (f32[128,768]{1,0:T(8,128)S(1)}, f32[128,768]{1,0:T(8,128)S(1)}, u32[]{:S(2)}, u32[]{:S(2)}) collective-permute-start(f32[128,768]{1,0:T(8,128)S(1)} %get-tuple-element.99), channel_id=1, source_target_pairs={{0,1},{1,0},{2,3},{3,2},{4,5},{5,4},{6,7},{7,6},{8,9},{9,8},{10,11... | collective-permute-start | bytes 1179656 | tf_op jit(solution)/shard_map/ppermute | solution.py:1189
  321.1 13.0 %collective-permute-start.58 = (bf16[224,768]{1,0:T(8,128)(2,1)S(1)}, bf16[224,768]{1,0:T(8,128)(2,1)S(1)}, u32[]{:S(2)}, u32[]{:S(2)}) collective-permute-start(bf16[224,768]{1,0:T(8,128)(2,1)S(1)} %fusion.3.refs_0_), channel_id=1, source_target_pairs={{0,16},{8,24},{16,0},{24,8},{1,17},{9,25},{17,1},{25,9},{2,18},{10... | collective-permute-start | bytes 1032200 | tf_op jit(solution)/shard_map/ppermute | solution.py:1192
  322.1 12.0 %collective-permute-start.59 = (bf16[224,768]{1,0:T(8,128)(2,1)S(1)}, bf16[224,768]{1,0:T(8,128)(2,1)S(1)}, u32[]{:S(2)}, u32[]{:S(2)}) collective-permute-start(bf16[224,768]{1,0:T(8,128)(2,1)S(1)} %fusion.3.refs_0_), channel_id=1, source_target_pairs={{0,24},{8,16},{16,8},{24,0},{1,25},{9,17},{17,9},{25,1},{2,26},{10... | collective-permute-start | bytes 1032200 | tf_op jit(solution)/shard_map/ppermute | solution.py:1192
  (73 other events, 1345.6 us)

commit v2 on v1

--- a/solution.py
+++ b/solution.py
@@ -588,12 +588,8 @@
     return jnp.where(latent > 0, level, jnp.where(latent < 0, -level, 0.0)).astype(BF16)
 
 
-def pack_kernel(
-    info, hid, lq, lk, lv, lo, lu, ld, tq, tk, tv, to, tu, td, qkv, own, mine, keep, send
-):
-    core, rep = info[I_CORE], info[I_REP]
-    keep[...] = hid[core]
-    send[...] = hid[1 - core]
+def pack_kernel(info, lq, lk, lv, lo, lu, ld, tq, tk, tv, to, tu, td, qkv, own, mine):
+    rep = info[I_REP]
     for slot, ref in enumerate((lq, lk, lv)):
         qkv[0, slot] = binary_rows(ref[...])
     for slot, ref in enumerate((tq, tk, tv)):
@@ -616,25 +612,63 @@
     mine[...] = own[rep]
 
 
-def pack(info, hid, latents, tutors):
+def pack(info, latents, tutors):
     rows, width = latents[0].shape
     piece = 4 * rows + rows // 2
-    half = hid.shape[1:]
     return pl.pallas_call(
         pack_kernel,
         out_shape=(
             jax.ShapeDtypeStruct((2, 3, rows, width), BF16),
             jax.ShapeDtypeStruct((4, piece, width), BF16),
             jax.ShapeDtypeStruct((piece, width), BF16),
-            jax.ShapeDtypeStruct(half, BF16),
-            jax.ShapeDtypeStruct(half, BF16),
         ),
-        in_specs=[SM] + [VM] * 13,
-        out_specs=(VM,) * 5,
+        in_specs=[SM] + [VM] * 12,
+        out_specs=(VM,) * 3,
         compiler_params=params(),
         cost_estimate=cost(4e6, 12e6),
         name="pack",
-    )(info, hid, *latents, *tutors)
+    )(info, *latents, *tutors)
+
+
+def table_kernel(*refs):
+    heads_bias, vecs = refs[13:]
+    line, _, feats = heads_bias.shape[2:]
+    width = line * feats
+
+    def flat(ref):
+        return ref[...].reshape(1, ref.shape[0])
+
+    bq, bv, bo, bu, bd, g1, s1, g2, s2 = [flat(ref) for ref in refs[:9]]
+    biases, inner, gains, shifts = refs[9:13]
+    for net, pair in enumerate(((bq, bv), (biases[0:1], biases[1:2]))):
+        for slot, row in enumerate(pair):
+            for z in range(line):
+                heads_bias[net, slot, z] = row[:, z * feats : (z + 1) * feats]
+    rows = (
+        (bo, bd, g1, s1, g2, s2),
+        (biases[2:3], biases[3:4], gains[0:1], shifts[0:1], gains[1:2], shifts[1:2]),
+    )
+    for net, up in enumerate((bu, flat(inner))):
+        for slot, row in enumerate(rows[net]):
+            vecs[net, slot] = row
+        for r in range(4):
+            vecs[net, V_UP + r] = up[:, r * width : (r + 1) * width]
+
+
+def table(vectors, tutor_vectors, line):
+    width = vectors[0].shape[0]
+    return pl.pallas_call(
+        table_kernel,
+        out_shape=(
+            jax.ShapeDtypeStruct((2, 2, line, 1, width // line), F32),
+            jax.ShapeDtypeStruct((2, 10, 1, width), F32),
+        ),
+        in_specs=[VM] * 13,
+        out_specs=(VM,) * 2,
+        compiler_params=params(),
+        cost_estimate=cost(1e5, 2e5),
+        name="table",
+    )(*vectors, *tutor_vectors)
 
 
 def load_tokens(info, xs, pieces, sem):
@@ -645,23 +679,24 @@
             pltpu.make_async_copy(piece.at[j], xs.at[info[I_RING + k], spot], sem).start()
 
 
-def load_rows(info, ws, own, sib, sem):
+def load_rows(info, ws, own, sib, net, sem):
     core = info[I_CORE]
     for slot in range(3):
-        pltpu.make_async_copy(own.at[slot], ws.at[slot, core], sem).start()
-        pltpu.make_async_copy(sib.at[slot], ws.at[slot, 1 - core], sem).start()
+        pltpu.make_async_copy(own.at[net, slot], ws.at[slot, core], sem).start()
+        pltpu.make_async_copy(sib.at[net, slot], ws.at[slot, 1 - core], sem).start()
 
 
 def attend_kernel(student, info, *refs):
     pieces, refs = refs[:4], refs[4:]
-    own, sib, bq, bv, clip = refs[:5]
-    refs = refs[5:]
+    own, sib, heads_bias, clip = refs[:4]
+    refs = refs[4:]
+    net = 0 if student else 1
     if student:
-        out, qkv_out, lse_out, ctx_out, xs, ws, qs, ks, vt, ct, sems = refs
+        out, qkv_out, lse_out, ctx_out, xs, ws, qs, ks, vt, ct, low, sems = refs
     else:
-        out, xs, ws, qs, ks, vt, ct, sems = refs
+        _, out, xs, ws, qs, ks, vt, ct, low, sems = refs
     load_tokens(info, xs, pieces, sems.at[0])
-    load_rows(info, ws, own, sib, sems.at[1])
+    load_rows(info, ws, own, sib, net, sems.at[1])
     line, _, half, width = xs.shape
     block = 2 * half
     feats = qs.shape[1]
@@ -669,7 +704,7 @@
     heads = feats // DH
     place = info[I_Z]
     length = info[I_LEN]
-    bq_row, bv_row = bq[place], bv[place]
+    bq_row, bv_row = heads_bias[net, 0, place], heads_bias[net, 1, place]
     wait_all(xs, sems.at[0])
     wait_all(ws, sems.at[1])
 
@@ -716,18 +751,22 @@
 
     lax.fori_loop(0, line, mix, 0)
     for b in range(line):
-        out[b] = ct[:, b * block : (b + 1) * block].T.astype(BF16)
+        low[b] = ct[:, b * block : (b + 1) * block].astype(BF16)
+        pltpu.make_async_copy(low.at[b], out.at[b, net], sems.at[2 + b]).start()
     if student:
         ctx_out[...] = ct[...]
-
-
-def attend(info, pieces, own, sib, bq, bv, clip, student):
+    for b in range(line):
+        pltpu.make_async_copy(low.at[b], out.at[b, net], sems.at[2 + b]).wait()
+
+
+def attend(info, pieces, own, sib, heads_bias, clip, both=None):
     _, half, width = pieces[0].shape
     line = len(pieces)
     total = line * 2 * half
-    rows = own.shape[1]
+    rows = own.shape[2]
     feats = 2 * rows
-    outs = [jax.ShapeDtypeStruct((line, 2 * half, feats), BF16)]
+    student = both is None
+    outs = [jax.ShapeDtypeStruct((line, 2, feats, 2 * half), BF16)]
     if student:
         outs += [
             jax.ShapeDtypeStruct((3, total, feats), BF16),
@@ -737,8 +776,8 @@
     return pl.pallas_call(
         functools.partial(attend_kernel, student),
         out_shape=tuple(outs),
-        in_specs=[SM] + [ANY] * 6 + [VM] * 3,
-        out_specs=(VM,) * len(outs),
+        in_specs=[SM] + [ANY] * 6 + [VM] * 2 + ([] if student else [ANY]),
+        out_specs=(ANY,) + (VM,) * (len(outs) - 1),
         scratch_shapes=[
             pltpu.VMEM((line, 2, half, width), BF16),
             pltpu.VMEM((3, 2, rows, width), BF16),
@@ -746,12 +785,14 @@
             pltpu.VMEM((total, feats), BF16),
             pltpu.VMEM((feats, total), BF16),
             pltpu.VMEM((feats, total), F32),
-            pltpu.SemaphoreType.DMA((2,)),
+            pltpu.VMEM((line, feats, 2 * half), BF16),
+            pltpu.SemaphoreType.DMA((2 + line,)),
         ],
+        input_output_aliases={} if student else {9: 0},
         compiler_params=params(),
         cost_estimate=cost(6e9, 4e6, 3e6),
         name="attend_student" if student else "attend_tutor",
-    )(info, *pieces, own, sib, bq, bv, clip)
+    )(info, *pieces, own, sib, heads_bias, clip, *([] if student else [both]))
 
 
 def attend_back_kernel(info, *refs):
@@ -760,7 +801,7 @@
     (xs, ws, kt, dct, dq, dk, dv, sems) = refs[13:]
     parts = (part0, part1, part2, part3)
     load_tokens(info, xs, pieces, sems.at[0])
-    load_rows(info, ws, own, sib, sems.at[1])
+    load_rows(info, ws, own, sib, 0, sems.at[1])
     line, _, half, width = xs.shape
     block = 2 * half
     total, feats = dk.shape
@@ -771,13 +812,14 @@
     for b in range(line):
         cols = slice(b * block, (b + 1) * block)
         kt[:, cols] = qkv[1, cols].astype(F32).T.astype(BF16)
-        dct[:, cols] = dctx[b].astype(F32).T
+        dct[:, cols] = dctx[b].astype(F32)
     dk[...] = jnp.zeros_like(dk)
     dv[...] = jnp.zeros_like(dv)
     fill = jnp.where(
         lax.broadcasted_iota(jnp.int32, (total, 1), 0) < length, 0.0, NEG_FILL
     ).astype(F32)
     lane_head = lax.broadcasted_iota(jnp.int32, (1, feats), 1) // DH
+    row_head = lax.broadcasted_iota(jnp.int32, (feats, 1), 0) // DH
 
     def body(b, carry):
         rows = pl.ds(pl.multiple_of(b * block, block), block)
@@ -787,12 +829,12 @@
         for h in range(heads):
             head = slice(h * DH, (h + 1) * DH)
             q_h = jnp.where(lane_head == h, q, jnp.zeros_like(q))
-            g_h = jnp.where(lane_head == h, g, jnp.zeros_like(g))
+            g_h = jnp.where(row_head == h, g, jnp.zeros_like(g))
             delta = jnp.sum(dct[head, rows] * ctx[head, rows], axis=0, keepdims=True)
             probs = jnp.exp(dims(qkv[1], q_h, 1, 1) + fill - lse[h : h + 1, rows])
-            dprobs = dims(qkv[2], g_h, 1, 1)
+            dprobs = dims(qkv[2], g_h, 1, 0)
             dscores = (probs * (dprobs - delta)).astype(BF16)
-            dv_h = dims(probs.astype(BF16), g_h, 1, 0)
+            dv_h = dims(probs.astype(BF16), g_h, 1, 1)
             dk_h = dims(dscores, q_h, 1, 0)
             dk_add = dk_h if dk_add is None else dk_add + dk_h
             dv_add = dv_h if dv_add is None else dv_add + dv_h
@@ -857,7 +899,7 @@
     _, half, width = pieces[0].shape
     line = len(pieces)
     total = line * 2 * half
-    rows = own.shape[1]
+    rows = own.shape[2]
     feats = 2 * rows
     part = jax.ShapeDtypeStruct((2 * half, width), BF16)
     grad = jax.ShapeDtypeStruct((3 * rows + 16, width), BF16)
@@ -883,8 +925,8 @@
 
 
 V_OUT, V_DOWN, V_G1, V_S1, V_G2, V_S2, V_UP = 0, 1, 2, 3, 4, 5, 6
-S_OUT, S_DOWN, S_G1, S_S1, S_G2, S_S2, S_UP, S_ERR = 0, 1, 2, 3, 4, 5, 6, 10
-PAD = 32
+S_OUT, S_DOWN, S_G1, S_S1, S_G2, S_S2, S_UP = 0, 1, 2, 3, 4, 5, 6
+PAD = 16
 
 
 def norm_parts(v):
@@ -906,14 +948,14 @@
 
 
 def middle_kernel(info, own, sib, *refs):
-    chunks, refs = refs[:30], refs[30:]
-    (x_own, ctx_s, ctx_t, vecs) = refs[:4]
-    (out_keep, out_send, dfirst_keep, dctx_out, sums) = refs[4:9]
-    grads = refs[9:17]
-    (w_up, w_dn, w_out, gate_pre, lower, gup, gdn, base, aim, acc, sems) = refs[17:]
+    chunks, refs = refs[:26], refs[26:]
+    (x_own, ctx, vecs) = refs[:3]
+    (out_keep, out_send, dfirst_keep, dctx_out) = refs[3:7]
+    grads = refs[7:15]
+    (w_up, w_dn, w_out, gate_pre, lower, gup, gdn, sums, base, aim, acc, sems) = refs[15:]
     core, rep, place, length = info[I_CORE], info[I_REP], info[I_Z], info[I_LEN]
     _, groups, quarters, rows, width = w_up.shape
-    tokens = ctx_s.shape[1]
+    tokens = ctx.shape[3]
     line = groups // 2
     hidden = groups * rows
     half = rows // 2
@@ -940,12 +982,14 @@
     for k in range(1, line):
         for rel in range(2):
             member = 2 * info[I_RING + k] + (core if rel == 0 else 1 - core)
-            mine, from_x, from_y, far_a, far_b = chunks[((k - 1) * 2 + rel) * 5 :][:5]
-            place_piece(mine, 0, piece, rep, member)
-            place_piece(from_x, 0, piece, rep ^ 1, member)
-            place_piece(from_y, 0, piece, rep ^ 2, member)
-            place_piece(far_a, 0, 2 * rows, rep ^ 3, member)
-            place_piece(far_b, 2 * rows, piece, rep ^ 3, member)
+            got = chunks[(k - 1) * 8 + rel * (4 if k < line - 1 else 5) :]
+            for far in range(3):
+                place_piece(got[far], 0, piece, rep ^ far, member)
+            if k < line - 1:
+                place_piece(got[3], 0, piece, rep ^ 3, member)
+            else:
+                place_piece(got[3], 0, 2 * rows, rep ^ 3, member)
+                place_piece(got[4], 2 * rows, piece, rep ^ 3, member)
 
     wait_all(w_out, sems.at[4])
     x_low = jnp.concatenate(
@@ -955,8 +999,9 @@
     def row(net, which):
         return vecs[net, which]
 
-    def context_of(ref):
-        return jnp.concatenate([ref[zb] for zb in range(line)], axis=1)
+    def context_of(net):
+        flat = jnp.concatenate([ctx[zb, net] for zb in range(line)], axis=0)
+        return flat, flat.astype(F32).T.astype(BF16)
 
     def upper(net, ctx):
         first = (
@@ -983,9 +1028,9 @@
         lax.fori_loop(0, quarters, step, 0)
         return acc[...]
 
-    ctx_tutor = context_of(ctx_t)
+    _, ctx_tutor = context_of(1)
     _, _, first_norm = upper(1, ctx_tutor)
-    ctx_low = context_of(ctx_s)
+    ctx_flat, ctx_low = context_of(0)
     normed_one, inv_one, first_norm_s = upper(0, ctx_low)
     base[...] = first_norm_s
     wait_all(w_up.at[1], sems.at[2])
@@ -1013,7 +1058,6 @@
     dout = kept * aim[...]
     sums[...] = jnp.zeros_like(sums)
     error = 0.5 * jnp.sum(dout * dout)
-    sums[S_ERR] = jnp.full((1, width), error, F32)
     sums[S_G2] = jnp.sum(dout * normed_two, axis=0, keepdims=True)
     sums[S_S2] = jnp.sum(dout, axis=0, keepdims=True)
     dsecond = norm_back(dout * row(0, V_G2), normed_two, inv_two)
@@ -1033,7 +1077,7 @@
         dgate = dlower * slope
         sums[S_UP + r] = jnp.sum(dgate, axis=0, keepdims=True)
         gup_r = dims(turned(dgate), upper_in, 1, 0).astype(BF16)
-        gup[pl.ds(2 * r, 2)] = gup_r.reshape(2, quarters, rows, width)
+        gup[pl.ds(2 * r, 2), :, 0:rows] = gup_r.reshape(2, quarters, rows, width)
         acc[...] += dims(
             dgate.astype(BF16), w_up[0, pl.ds(2 * r, 2)].reshape(hidden, width), 1, 0
         )
@@ -1047,16 +1091,38 @@
     sums[S_OUT] = jnp.sum(dsum, axis=0, keepdims=True)
     dfirst_keep[...] = dsum
     g_out = dsum.astype(BF16)
-    dctx = dims(g_out, w_out[0].reshape(width, width), 1, 0).astype(BF16)
-    feats = width // line
-    for zb in range(line):
-        dctx_out[zb] = dctx[:, zb * feats : (zb + 1) * feats]
-    gout = dims(turned(dsum), ctx_low, 1, 0).reshape(groups, quarters, rows // quarters, width)
+    dctx = turned(dims(g_out, w_out[0].reshape(width, width), 1, 0))
+    dctx_out[...] = dctx.reshape(dctx_out.shape)
+    gout = dims(turned(dsum), ctx_flat, 1, 1).reshape(groups, quarters, rows // quarters, width)
+    number = rep * groups + 2 * place + core
+    high = error.astype(BF16).astype(F32)
+    middle_part = (error - high).astype(BF16).astype(F32)
+    lane = lax.broadcasted_iota(jnp.int32, (1, width), 1)
+    digits = jnp.zeros((1, width), F32)
+    for slot, digit in enumerate((high, middle_part, error - high - middle_part)):
+        digits = jnp.where(lane == 3 * number + slot, digit, digits)
+    ups = jnp.concatenate([sums[S_UP + r] for r in range(quarters)], axis=1)
     slim = rows // quarters
-    for r in range(quarters):
-        for g in range(groups):
-            gdn[r, g, rows : rows + slim] = gout[g, r].astype(BF16)
-            gdn[r, g, rows + slim :] = jnp.zeros((PAD - slim, width), BF16)
+    for g in range(groups):
+        own_rows = [sums[which][:, g * rows : (g + 1) * rows] for which in range(6)]
+        vectors = jnp.concatenate(
+            [
+                jnp.concatenate(own_rows, axis=0),
+                jnp.zeros((6, width - rows), F32),
+            ],
+            axis=1,
+        )
+        inner = jnp.concatenate(
+            [
+                ups[:, g * 4 * rows : (g + 1) * 4 * rows],
+                jnp.zeros((1, width - 4 * rows), F32),
+            ],
+            axis=1,
+        )
+        tail = jnp.concatenate([vectors, inner, digits], axis=0)
+        for r in range(quarters):
+            gup[g, r, rows:] = gout[g, r, :PAD].astype(BF16)
+            gdn[r, g, rows:] = jnp.concatenate([gout[g, r, PAD:slim], tail], axis=0).astype(BF16)
 
     for rel in range(2):
         a_keep, a_send, b_keep, b_send = grads[rel * 4 : rel * 4 + 4]
@@ -1078,35 +1144,34 @@
             wait_all(ref, sems.at[5 + rel * 4 + slot])
 
 
-def middle(info, own, sib, chunks, x_own, ctx_s, ctx_t, vecs):
-    line, tokens, feats = ctx_s.shape
+def middle(info, own, sib, chunks, x_own, ctx, vecs):
+    line, _, feats, tokens = ctx.shape
     width = line * feats
     quarters = own.shape[0]
     groups = 2 * line
     rows = width // groups
     half = (tokens // 2, width)
-    a_shape = jax.ShapeDtypeStruct((2, line, rows, width), BF16)
-    b_shape = jax.ShapeDtypeStruct((2, line, rows + PAD, width), BF16)
+    part = jax.ShapeDtypeStruct((2, line, rows + PAD, width), BF16)
     outs = (
         jax.ShapeDtypeStruct(half, BF16),
         jax.ShapeDtypeStruct(half, BF16),
         jax.ShapeDtypeStruct((tokens, width), F32),
-        jax.ShapeDtypeStruct((line, tokens, feats), BF16),
-        jax.ShapeDtypeStruct((16, 1, width), F32),
-    ) + (a_shape, a_shape, b_shape, b_shape) * 2
+        jax.ShapeDtypeStruct((line, feats, tokens), BF16),
+    ) + (part,) * 8
     return pl.pallas_call(
         middle_kernel,
         out_shape=outs,
-        in_specs=[SM] + [ANY] * 32 + [VM] * 4,
-        out_specs=(VM,) * 5 + (ANY,) * 8,
+        in_specs=[SM] + [ANY] * 28 + [VM] * 3,
+        out_specs=(VM,) * 4 + (ANY,) * 8,
         scratch_shapes=[
             pltpu.VMEM((2, groups, quarters, rows, width), BF16),
             pltpu.VMEM((2, quarters, groups, rows, width), BF16),
             pltpu.VMEM((2, groups, 2, rows // 2, width), BF16),
             pltpu.VMEM((quarters, tokens, width), F32),
             pltpu.VMEM((quarters, tokens, width), BF16),
-            pltpu.VMEM((groups, quarters, rows, width), BF16),
+            pltpu.VMEM((groups, quarters, rows + PAD, width), BF16),
             pltpu.VMEM((quarters, groups, rows + PAD, width), BF16),
+            pltpu.VMEM((S_UP + quarters, 1, width), F32),
             pltpu.VMEM((tokens, width), F32),
             pltpu.VMEM((tokens, width), F32),
             pltpu.VMEM((tokens, width), F32),
@@ -1115,32 +1180,46 @@
         compiler_params=params(),
         cost_estimate=cost(15e9, 30e6, 4e6),
         name="middle",
-    )(info, own, sib, *chunks, x_own, ctx_s, ctx_t, vecs)
-
-
-def finish_kernel(info, *refs):
+    )(info, own, sib, *chunks, x_own, ctx, vecs)
+
+
+def finish_kernel(entries, info, *refs):
     pieces, refs = refs[:4], refs[4:]
-    grad_qkv, up, down, out, gq, gk, gv, scr, sem = refs
+    grad_qkv, up, down, out, gq, gk, gv, loss, bq, bv, bu = refs[:11]
+    others, scr, sem = refs[11:17], refs[17], refs[18]
     rep = info[I_REP]
     for far, ref in enumerate(pieces):
         pltpu.make_async_copy(ref, scr.at[rep ^ far], sem.at[0]).start()
     rows, width = gq.shape
     for slot, ref in enumerate((gq, gk, gv)):
         ref[...] = grad_qkv[slot * rows : (slot + 1) * rows].astype(F32)
+    bias = grad_qkv[3 * rows :].astype(F32)
+    bq[...] = bias[0, :rows]
+    bv[...] = bias[0, rows : 2 * rows]
     wait_all(scr, sem.at[0])
     slim = rows // len(pieces)
+    high = rows + PAD
     for r in range(len(pieces)):
         up[r * rows : (r + 1) * rows] = scr[r, 0:rows].astype(F32)
-        down[:, r * width : (r + 1) * width] = scr[r, rows : 2 * rows].astype(F32)
-        out[r * slim : (r + 1) * slim] = scr[r, 2 * rows : 2 * rows + PAD].astype(F32)[:slim]
-
-
-def finish(info, pieces, grad_qkv):
+        down[:, r * width : (r + 1) * width] = scr[r, high : high + rows].astype(F32)
+        out[r * slim : r * slim + PAD] = scr[r, rows:high].astype(F32)
+        last = scr[r, high + rows :].astype(F32)
+        out[r * slim + PAD : (r + 1) * slim] = last[: slim - PAD]
+        if r == 0:
+            tail = last[slim - PAD :]
+            for slot, ref in enumerate(others):
+                ref[...] = tail[slot, :rows]
+            bu[...] = tail[S_UP, : 4 * rows]
+            loss[...] = jnp.full((1, 1), jnp.sum(tail[S_UP + 1 : S_UP + 2]) / entries, F32)
+
+
+def finish(info, pieces, grad_qkv, entries):
     high, width = pieces[0].shape
-    rows = (high - PAD) // 2
+    rows = high // 2 - PAD
     small = jax.ShapeDtypeStruct((rows, width), F32)
+    vector = jax.ShapeDtypeStruct((rows,), F32)
     return pl.pallas_call(
-        finish_kernel,
+        functools.partial(finish_kernel, entries),
         out_shape=(
             jax.ShapeDtypeStruct((4 * rows, width), F32),
             jax.ShapeDtypeStruct((rows, 4 * width), F32),
@@ -1148,9 +1227,14 @@
             small,
             small,
             small,
-        ),
+            jax.ShapeDtypeStruct((1, 1), F32),
+            vector,
+            vector,
+            jax.ShapeDtypeStruct((4 * rows,), F32),
+        )
+        + (vector,) * 6,
         in_specs=[SM] + [ANY] * 4 + [VM],
-        out_specs=(VM,) * 6,
+        out_specs=(VM,) * 16,
         scratch_shapes=[
             pltpu.VMEM((4, high, width), BF16),
             pltpu.SemaphoreType.DMA((1,)),
@@ -1168,16 +1252,19 @@
     return total.astype(BF16)
 
 
+def after(value, *others):
+    return lax.optimization_barrier((value,) + others)[0]
+
+
 def line_shards(line, *args):
     hidden_in, seq_lengths = args[0], args[1]
     latents, vectors, clip_input = args[2:8], args[8:17], args[17]
-    tutors = args[18:24]
-    tutor_biases, tutor_inner, tutor_gains, tutor_shifts = args[24:28]
+    tutors, tutor_vectors = args[18:24], args[24:28]
     micro_count, _, local_rows, width = hidden_in.shape
+    rows = latents[0].shape[0]
     rep, grp = lax.axis_index("rep"), lax.axis_index("grp")
-    place, core = grp // 2, lax.rem(grp, 2)
+    core = lax.rem(grp, 2)
     ring = z_ring(line)
-    behind = [[ring[(ring.index(z) - k) % line] for k in range(line)] for z in range(line)]
 
     def over_z(x, pairs):
         return lax.ppermute(x, "grp", [(2 * a + c, 2 * b + c) for a, b in pairs for c in range(2)])
@@ -1195,80 +1282,56 @@
         groups = [[2 * z + c for z in range(line)] for c in range(2)]
         return lax.all_to_all(x, "grp", 0, 0, axis_index_groups=groups, tiled=True)
 
-    length = seq_lengths[core, 0]
-    info = jnp.concatenate(
-        [
-            jnp.stack([core, rep, place, length]).astype(jnp.int32),
-            jnp.asarray(behind, jnp.int32)[place],
-        ]
-    )
+    scalars = [
+        [g % 2, 0, g // 2, 0] + [ring[(ring.index(g // 2) - k) % line] for k in range(line)]
+        for g in range(2 * line)
+    ]
+    lane = jnp.arange(4 + line, dtype=jnp.int32)
+    info = jnp.sum(
+        jnp.where(jnp.arange(2 * line)[:, None] == grp, jnp.asarray(scalars, jnp.int32), 0), axis=0
+    )
+    length = jnp.where(core == 0, seq_lengths[0, 0], seq_lengths[1, 0])
+    info = jnp.where(lane == I_REP, rep, jnp.where(lane == I_LEN, length, info)).astype(jnp.int32)
     clip = clip_input.reshape(1, width)
-    qkv_own, own, piece, keep, send = pack(info, hidden_in[:, 0], latents, tutors)
-    x_own = jnp.stack([keep, swap(send)])
+    tokens = hidden_in[:, 0]
+    keep = jnp.where(core == 0, tokens[0], tokens[1])
+    swapped = swap(jnp.where(core == 0, tokens[1], tokens[0]))
+    x_own = jnp.stack([keep, swapped])
+    x_1 = next_z(x_own)
+    qkv_own, own, piece = pack(after(info, x_own), latents, tutors)
+    heads_bias, vecs = table(vectors, tutor_vectors, line)
+
+    def to_sides(value):
+        return [value, to_rep(value, 1), to_rep(value, 2)]
+
+    piece_1 = next_z(piece)
     qkv_sib = swap(qkv_own)
     sib = swap(own)
-    tokens_in = [x_own]
-    for _ in range(line - 1):
-        tokens_in.append(next_z(tokens_in[-1]))
-
-    rows = latents[0].shape[0]
+    x_2 = next_z(after(x_1, sib, qkv_sib))
+    x_3 = next_z(after(x_2, piece_1))
+    piece_2 = next_z(piece_1)
+    got_1 = to_sides(piece_1)
+    tokens_in = [x_own, x_1, x_2, x_3]
+    mixed, qkv, lse, ctx = attend(info, tokens_in, qkv_own, qkv_sib, heads_bias, clip)
+    mixed = after(mixed, *got_1, piece_2)
+    piece_2 = after(piece_2, mixed)
+    piece_3 = next_z(piece_2)
+    got_2 = to_sides(piece_2)
+    got_1.append(to_rep(after(got_1[1], mixed), 2))
+    (mixed,) = attend(info, tokens_in, qkv_own, qkv_sib, heads_bias, clip, mixed)
+    got_2.append(to_rep(after(got_2[2], mixed), 1))
+    got_3 = to_sides(after(piece_3, mixed))
+    mixed = to_tokens(mixed)
+    got_3.append(to_rep(after(got_3[1][: 2 * rows], mixed), 2))
+    got_3.append(to_rep(after(got_3[2][2 * rows :], mixed), 1))
     chunks = []
-    for _ in range(line - 1):
-        piece = next_z(piece)
-        from_x, from_y = to_rep(piece, 1), to_rep(piece, 2)
-        far_a = to_rep(from_x[: 2 * rows], 2)
-        far_b = to_rep(from_y[2 * rows :], 1)
-        got = [piece, from_x, from_y, far_a, far_b]
-        chunks += got + [swap(one) for one in got]
-
-    def heads_row(vector):
-        return vector.reshape(line, 1, width // line)
-
-    ctx_s, qkv, lse, ctx = attend(
-        info,
-        tokens_in,
-        qkv_own[0],
-        qkv_sib[0],
-        heads_row(vectors[0]),
-        heads_row(vectors[1]),
-        clip,
-        True,
-    )
-    (ctx_t,) = attend(
-        info,
-        tokens_in,
-        qkv_own[1],
-        qkv_sib[1],
-        heads_row(tutor_biases[0]),
-        heads_row(tutor_biases[1]),
-        clip,
-        False,
-    )
-    ctx_s, ctx_t = to_tokens(ctx_s), to_tokens(ctx_t)
-    vecs = jnp.concatenate(
-        [
-            vectors[2],
-            vectors[4],
-            vectors[5],
-            vectors[6],
-            vectors[7],
-            vectors[8],
-            vectors[3],
-            tutor_biases[2],
-            tutor_biases[3],
-            tutor_gains[0],
-            tutor_shifts[0],
-            tutor_gains[1],
-            tutor_shifts[1],
-            tutor_inner,
-        ]
-    ).reshape(2, 10, 1, width)
+    for got in (got_1, got_2, got_3):
+        chunks += got + [swap(after(one, got_3[0])) for one in got]
     (
         out_keep,
         out_send,
         dfirst,
         dctx,
-        sums,
         a_keep,
         a_send,
         b_keep,
@@ -1277,20 +1340,24 @@
         a_send_sib,
         b_keep_sib,
         b_send_sib,
-    ) = middle(info, own, sib, chunks, x_own, ctx_s, ctx_t, vecs)
+    ) = middle(info, own, sib, chunks, x_own, mixed, vecs)
 
     def by_micro(kept, got):
-        return jnp.where(
-            core == 0, jnp.stack([kept, got]), jnp.stack([got, kept])
-        )[:, None]
+        return jnp.where(core == 0, jnp.stack([kept, got]), jnp.stack([got, kept]))[:, None]
 
     dctx = to_tokens(dctx)
     a_out = add_low(a_send, swap(a_send_sib))
     b_out = add_low(b_send, swap(b_send_sib))
+    a_in, b_in = to_rep(a_out, 1), to_rep(b_out, 2)
     a_keep_sib, b_keep_sib = swap(a_keep_sib), swap(b_keep_sib)
-    a_in, b_in = to_rep(a_out, 1), to_rep(b_out, 2)
-    a_next = to_rep(add_low(a_keep[1], a_keep_sib[1], a_in[1]), 2)
-    b_next = to_rep(add_low(b_keep[1], b_keep_sib[1], b_in[1]), 1)
+    part0, part1, part2, part3, gqkv, gqkv_sib = attend_back(
+        info, tokens_in, qkv_own, qkv_sib, clip, qkv, lse, ctx, after(dctx, a_out, b_out)
+    )
+    moving_1 = next_z(part1)
+    gqkv_sib = swap(gqkv_sib)
+    a_next = to_rep(add_low(a_keep[1], a_keep_sib[1], after(a_in, part1)[1]), 2)
+    b_next = to_rep(add_low(b_keep[1], b_keep_sib[1], after(b_in, part1)[1]), 1)
+    moving_2 = next_z(after(add_low(moving_1, part2), a_in, b_in))
     both = jnp.concatenate(
         [
             add_low(a_keep[0], a_keep_sib[0], a_in[0], a_next),
@@ -1298,53 +1365,33 @@
         ],
         axis=1,
     )
-    layer_out = by_micro(out_keep, swap(out_send))
-
-    part0, part1, part2, part3, gqkv, gqkv_sib = attend_back(
-        info, tokens_in, qkv_own[0], qkv_sib[0], clip, qkv, lse, ctx, dctx
-    )
-    moving = next_z(part1)
-    moving = next_z(add_low(moving, part2))
-    moving = next_z(add_low(moving, part3))
-    grads = next_z(both[1])
-    grads = next_z(add_low(grads, both[2]))
-    grads = next_z(add_low(grads, both[3]))
-    grads = add_low(grads, both[0])
-    quarter = [grads, to_rep(grads, 1), to_rep(grads, 2), to_rep(grads, 3)]
-
-    gqkv = add_low(gqkv, swap(gqkv_sib))
-    gqkv = add_low(gqkv, to_rep(gqkv, 1))
+    moving_3 = next_z(add_low(moving_2, part3))
+    grads_1 = next_z(both[1])
+    layer_out = by_micro(out_keep, swap(after(out_send, moving_2)))
+    gqkv = add_low(gqkv, gqkv_sib)
+    gqkv = add_low(gqkv, to_rep(after(gqkv, moving_2), 1))
+    grads_2 = next_z(after(add_low(grads_1, both[2]), gqkv))
     gqkv = add_low(gqkv, to_rep(gqkv, 2))
-    grad_up, grad_down, grad_out, grad_q, grad_k, grad_v = finish(info, quarter, gqkv)
-
-    total = sums.reshape(16, width)
-    total = total + swap(total)
-    total = total + to_rep(total, 1)
-    total = total + to_rep(total, 2)
-    bit = 1
-    while bit < line:
-        total = total + over_z(total, [(z, z ^ bit) for z in range(line)])
-        bit *= 2
-    own_cols = lax.dynamic_slice_in_dim(total.reshape(16, 2 * line, rows), grp, 1, 1)[:, 0]
-    own_up = lax.dynamic_slice_in_dim(
-        total[S_UP : S_UP + 4].reshape(2 * line, 4 * rows), grp, 1, 0
-    )[0]
+    grads_3 = next_z(after(add_low(grads_2, both[3]), gqkv))
+    grads = add_low(grads_3, both[0])
+    quarter = to_sides(grads) + [to_rep(grads, 3)]
     entries = micro_count * 4 * 2 * line * local_rows * width
-    loss = total[S_ERR, 0] / entries
-
-    order = jnp.stack([jnp.where(core == 0, 0, 1), jnp.where(core == 0, 1, 0)])
-    hidden_tokens = x_own[order].reshape(2 * local_rows, width).astype(F32)
-    dxin = moving.astype(F32) + part0.astype(F32)
+    ends = finish(info, quarter, gqkv, entries)
+    grad_up, grad_down, grad_out, grad_q, grad_k, grad_v, loss, bq, bv, bu = ends[:10]
+    bo, bd, g1, s1, g2, s2 = ends[10:]
+
+    hidden_tokens = jnp.where(core == 0, x_own, x_own[::-1])
+    hidden_tokens = hidden_tokens.reshape(2 * local_rows, width).astype(F32)
+    dxin = moving_3.astype(F32) + part0.astype(F32)
     grad_input = dfirst + jnp.where(jnp.abs(hidden_tokens) < clip, dxin, 0.0)
     halves = grad_input.reshape(2, local_rows, width)
     grad_input = by_micro(
         jnp.where(core == 0, halves[0], halves[1]),
         swap(jnp.where(core == 0, halves[1], halves[0])),
     )
-    bias = gqkv[3 * rows].astype(F32)
     return (
         layer_out,
-        loss,
+        loss.reshape(()),
         grad_input,
         grad_q,
         grad_k,
@@ -1352,15 +1399,15 @@
         grad_out,
         grad_up,
         grad_down,
-        bias[:rows],
-        bias[rows : 2 * rows],
-        own_cols[S_OUT],
-        own_up,
-        own_cols[S_DOWN],
-        own_cols[S_G1],
-        own_cols[S_S1],
-        own_cols[S_G2],
-        own_cols[S_S2],
+        bq,
+        bv,
+        bo,
+        bu,
+        bd,
+        g1,
+        s1,
+        g2,
+        s2,
     )
 
 

time: 343 us -> 296 us (0.86)
  local copies, waits for them, and re-layouts: 45.2 us -> 8.8 us
  starting transfers between devices: 69.9 us -> 59.4 us
    ppermute x14 -> x12, waiting for transfers between devices: 68.6 us -> 48.9 us  [over_z(): lax.ppermute(x, 'grp', [(2 * a + c, 2 * b + c) for a, b in pairs for c in...]
    unnamed x124 -> x78, local copies, waits for them, and re-layouts: 22.7 us -> 6.87 us
    ppermute x23 -> x19, waiting for transfers between devices: 52 us -> 65.5 us  [to_rep(): return lax.ppermute(x, 'rep', [(i, i ^ bit) for i in range(4)])]
    all_to_all x3 -> x2, starting transfers between devices: 13.2 us -> 7.35 us  [to_tokens(): return lax.all_to_all(x, 'grp', 0, 0, axis_index_groups=groups, tiled=True)]
    pallas_call x3 -> x0, local copies, waits for them, and re-layouts: 5.09 us -> none  [the longest x2 4.1 us: attend(): pl.pallas_call(functools.partial(attend_kernel, student), out_shape=tuple...]
    all_to_all x3 -> x2, waiting for transfers between devices: 0.01 us -> 4.3 us  [to_tokens(): return lax.all_to_all(x, 'grp', 0, 0, axis_index_groups=groups, tiled=True)]
    ppermute x23 -> x19, starting transfers between devices: 24.1 us -> 21 us  [to_rep(): return lax.ppermute(x, 'rep', [(i, i ^ bit) for i in range(4)])]
    ppermute x14 -> x12, starting transfers between devices: 28.9 us -> 26.3 us  [over_z(): lax.ppermute(x, 'grp', [(2 * a + c, 2 * b + c) for a, b in pairs for c in...]
  transfers between devices with their start and end apart: 66 -> 56, of which waited for: 24 -> 24; matrix products, arithmetic and copies ran while one was open for 16% -> 6% of each run, Pallas kernels for 12% -> 15%
where the time goes in v2:
time: 296 us; the launch traced here: 295 us
  waiting for transfers between devices  122 us (41%)
  Pallas kernels  84.8 us (29%)
  starting transfers between devices  59.4 us (20%)
  other arithmetic  17.9 us (6%)
  local copies, waits for them, and re-layouts  8.8 us (3%)
    ppermute x19, waiting for transfers between devices, to_rep(): return lax.ppermute(x, 'rep', [(i, i ^ bit) for i in range(4)])  65.5 us
    ppermute x12, waiting for transfers between devices, over_z(): lax.ppermute(x, 'grp', [(2 * a + c, 2 * b + c) for a, b in pairs for c in...  48.9 us
    pallas_call x1, Pallas kernels, middle(): pl.pallas_call(middle_kernel, out_shape=outs, in_specs=[SM] + [ANY] * 28...  31.4 us
    pallas_call x2, Pallas kernels, attend(): pl.pallas_call(functools.partial(attend_kernel, student), out_shape=tuple...  27.3 us
    ppermute x12, starting transfers between devices, over_z(): lax.ppermute(x, 'grp', [(2 * a + c, 2 * b + c) for a, b in pairs for c in...  26.3 us
    ppermute x19, starting transfers between devices, to_rep(): return lax.ppermute(x, 'rep', [(i, i ^ bit) for i in range(4)])  21 us
    pallas_call x1, Pallas kernels, attend_back(): pl.pallas_call(attend_back_kernel, out_shape=(part,) * 4 + (grad, grad),...  14.8 us
    convert_element_type x14, other arithmetic, add_low(): return total.astype(BF16)  13.5 us
  transfers between devices with their start and end apart: 56, of which 24 were waited for; matrix products, arithmetic and copies ran while one was open for 6% of the time, Pallas kernels for 15%

profile of v2, /device:TPU:0, one launch (start us, length us, event | category | flops | bytes accessed | tf_op | source)
XLA Modules:
  0.0 295.1 jit_solution(6918886491136552692)
XLA Ops:
  6.2 5.5 %pack.1 = (bf16[2,3,96,768]{3,2,1,0:T(8,128)(2,1)}, bf16[4,432,768]{2,1,0:T(8,128)(2,1)}, bf16[432,768]{1,0:T(8,128)(2,1)}) custom-call(s32[8]{0:T(128)} %compare_select_fusion.1.info, f32[96,768]{1,0:T(8,128)} %lq.1, f32[96,768]{1,0:T(8,128)} %lk.1, f32[96,768]{1,0:T(8,128)} %lv.1, f32[96,768]{1,0:T(8,128)} %lo.1, f32[384,768]{1,0:T(8,128)} %lu.1, ...), custom_call_target="tpu_custom_call" | custom-call | flops 4000000 | bytes 12000000 | tf_op jit(solution)/shard_map/pack/pallas_call | solution.py:618
  12.2 3.6 %collective-permute-start.5 = (bf16[2,128,768]{2,1,0:T(8,128)(2,1)S(1)}, bf16[2,128,768]{2,1,0:T(8,128)(2,1)S(1)}, u32[]{:S(2)}, u32[]{:S(2)}) collective-permute-start(bf16[2,128,768]{2,1,0:T(8,128)(2,1)S(1)} %pad_maximum_fusion.refs_0_.refs_26_), channel_id=1, source_target_pairs={{0,4},{1,5},{4,6},{5,7},{6,2},{7,3},{2,0},{3,1},{8,12},{9,13},{12,... | collective-permute-start | bytes 1179656 | tf_op jit(solution)/shard_map/ppermute | solution.py:1270
  15.9 1.6 collective-permute-start.2
  17.5 7.9 %collective-permute-done.5.refs_1_ = bf16[2,128,768]{2,1,0:T(8,128)(2,1)S(1)} collective-permute-done((bf16[2,128,768]{2,1,0:T(8,128)(2,1)S(1)}, bf16[2,128,768]{2,1,0:T(8,128)(2,1)S(1)}, u32[]{:S(2)}, u32[]{:S(2)}) %collective-permute-start.5) | collective-permute-done | bytes 393248 | tf_op jit(solution)/shard_map/ppermute | solution.py:1270
  25.3 3.4 %collective-permute-start.7 = (bf16[2,128,768]{2,1,0:T(8,128)(2,1)S(1)}, bf16[2,128,768]{2,1,0:T(8,128)(2,1)S(1)}, u32[]{:S(2)}, u32[]{:S(2)}) collective-permute-start(bf16[2,128,768]{2,1,0:T(8,128)(2,1)S(1)} %collective-permute-done.5.refs_1_), channel_id=1, source_target_pairs={{0,4},{1,5},{4,6},{5,7},{6,2},{7,3},{2,0},{3,1},{8,12},{9,13},{12,... | collective-permute-start | bytes 1179656 | tf_op jit(solution)/shard_map/ppermute | solution.py:1270
  28.8 10.9 %collective-permute-done.2.refs_0_ = bf16[432,768]{1,0:T(8,128)(2,1)S(1)} collective-permute-done((bf16[432,768]{1,0:T(8,128)(2,1)}, bf16[432,768]{1,0:T(8,128)(2,1)S(1)}, u32[]{:S(2)}, u32[]{:S(2)}) %collective-permute-start.2) | collective-permute-done | bytes 663584 | tf_op jit(solution)/shard_map/ppermute | solution.py:1270
  39.6 7.9 %collective-permute-done.7.refs_2_ = bf16[2,128,768]{2,1,0:T(8,128)(2,1)S(1)} collective-permute-done((bf16[2,128,768]{2,1,0:T(8,128)(2,1)S(1)}, bf16[2,128,768]{2,1,0:T(8,128)(2,1)S(1)}, u32[]{:S(2)}, u32[]{:S(2)}) %collective-permute-start.7) | collective-permute-done | bytes 393248 | tf_op jit(solution)/shard_map/ppermute | solution.py:1270
  47.5 3.4 %collective-permute-start.8 = (bf16[2,128,768]{2,1,0:T(8,128)(2,1)S(1)}, bf16[2,128,768]{2,1,0:T(8,128)(2,1)S(1)}, u32[]{:S(2)}, u32[]{:S(2)}) collective-permute-start(bf16[2,128,768]{2,1,0:T(8,128)(2,1)S(1)} %collective-permute-done.7.refs_2_), channel_id=1, source_target_pairs={{0,4},{1,5},{4,6},{5,7},{6,2},{7,3},{2,0},{3,1},{8,12},{9,13},{12,... | collective-permute-start | bytes 1179656 | tf_op jit(solution)/shard_map/ppermute | solution.py:1270
  52.4 1.5 collective-permute-start.4
  54.6 1.5 table.1
  56.7 3.7 %collective-permute-done.8.refs_3_ = bf16[2,128,768]{2,1,0:T(8,128)(2,1)S(1)} collective-permute-done((bf16[2,128,768]{2,1,0:T(8,128)(2,1)S(1)}, bf16[2,128,768]{2,1,0:T(8,128)(2,1)S(1)}, u32[]{:S(2)}, u32[]{:S(2)}) %collective-permute-start.8) | collective-permute-done | bytes 393248 | tf_op jit(solution)/shard_map/ppermute | solution.py:1270
  61.2 14.4 %attend_student.1 = (bf16[4,2,192,256]{3,2,1,0:T(8,128)(2,1)}, bf16[3,1024,192]{2,1,0:T(8,128)(2,1)}, f32[8,1024]{1,0:T(8,128)}, f32[192,1024]{1,0:T(8,128)}) custom-call(s32[8]{0:T(128)} %compare_select_fusion.1.info, bf16[2,128,768]{2,1,0:T(8,128)(2,1)} %copy-done, bf16[2,128,768]{2,1,0:T(8,128)(2,1)} %copy-done.31, bf16[2,128,768]{2,1,0:T(8,128)(2,1)} %copy-done.32, ...), custom_call_target="tpu_custom_call" | custom-call | flops 6000000000 | bytes 4000000 | tf_op jit(solution)/shard_map/attend_student/pallas_call | solution.py:776
  75.6 3.4 %collective-permute-start.11 = (bf16[432,768]{1,0:T(8,128)(2,1)}, bf16[432,768]{1,0:T(8,128)(2,1)}, u32[]{:S(2)}, u32[]{:S(2)}) collective-permute-start(bf16[432,768]{1,0:T(8,128)(2,1)} %collective-permute-done.9.refs_8_), channel_id=1, source_target_pairs={{0,4},{1,5},{4,6},{5,7},{6,2},{7,3},{2,0},{3,1},{8,12},{9,13},{12,... | collective-permute-start | bytes 1990664 | tf_op jit(solution)/shard_map/ppermute | solution.py:1270
  79.1 1.5 collective-permute-start.17
  82.6 12.9 %attend_tutor.1 = bf16[4,2,192,256]{3,2,1,0:T(8,128)(2,1)} custom-call(s32[8]{0:T(128)} %compare_select_fusion.1.info, bf16[2,128,768]{2,1,0:T(8,128)(2,1)} %copy-done, bf16[2,128,768]{2,1,0:T(8,128)(2,1)} %copy-done.31, bf16[2,128,768]{2,1,0:T(8,128)(2,1)} %copy-done.32, bf16[2,128,768]{2,1,0:T(8,128)(2,1)} %copy-done.33, ...), custom_call_target="tpu_custom_call", output_to_operand_aliasing={{}: (9, {})} | custom-call | flops 6000000000 | bytes 4000000 | tf_op jit(solution)/shard_map/attend_tutor/pallas_call | solution.py:776
  95.5 1.6 collective-permute-start.24
  97.7 3.7 %all-to-all-start = ((bf16[4,2,192,256]{3,2,1,0:T(8,128)(2,1)}), bf16[4,2,192,256]{3,2,1,0:T(8,128)(2,1)S(1)}, u32[]{:S(2)}, u32[]{:S(2)}) async-start(bf16[4,2,192,256]{3,2,1,0:T(8,128)(2,1)} %attend_tutor.1), calls=%async_computation | async-start | bytes 1572864 | tf_op jit(solution)/shard_map/all_to_all | solution.py:1283
  101.4 1.6 collective-permute-start.18
  102.9 8.5 %collective-permute-done.10.refs_3_ = bf16[432,768]{1,0:T(8,128)(2,1)} collective-permute-done((bf16[432,768]{1,0:T(8,128)(2,1)}, bf16[432,768]{1,0:T(8,128)(2,1)}, u32[]{:S(2)}, u32[]{:S(2)}) %collective-permute-start.10) | collective-permute-done | bytes 663584 | tf_op jit(solution)/shard_map/ppermute | solution.py:1279
  111.5 10.2 %collective-permute-done.24.refs_18_ = bf16[432,768]{1,0:T(8,128)(2,1)S(1)} collective-permute-done((bf16[432,768]{1,0:T(8,128)(2,1)}, bf16[432,768]{1,0:T(8,128)(2,1)S(1)}, u32[]{:S(2)}, u32[]{:S(2)}) %collective-permute-start.24) | collective-permute-done | bytes 663584 | tf_op jit(solution)/shard_map/ppermute | solution.py:1279
  122.2 2.2 collective-permute-done.18.refs_11_
  128.9 8.6 %collective-permute-done.26.refs_20_ = bf16[240,768]{1,0:T(8,128)(2,1)S(1)} collective-permute-done((bf16[240,768]{1,0:T(8,128)(2,1)S(1)}, bf16[240,768]{1,0:T(8,128)(2,1)S(1)}, u32[]{:S(2)}, u32[]{:S(2)}) %collective-permute-start.26) | collective-permute-done | bytes 368672 | tf_op jit(solution)/shard_map/ppermute | solution.py:1279
  138.1 2.5 collective-permute-done.30.refs_24_
  143.0 31.4 %middle.1 = (bf16[128,768]{1,0:T(8,128)(2,1)}, bf16[128,768]{1,0:T(8,128)(2,1)}, f32[256,768]{1,0:T(8,128)}, bf16[4,192,256]{2,1,0:T(8,128)(2,1)}, bf16[2,4,112,...) custom-call(s32[8]{0:T(128)} %compare_select_fusion.1.info, ...), custom_call_target="tpu_custom_call" | custom-call | flops 15000000512 | bytes 30000000 | tf_op jit(solution)/shard_map/middle/pallas_call | solution.py:1161
  175.0 3.7 %all-to-all-start.1 = ((bf16[4,192,256]{2,1,0:T(8,128)(2,1)}), bf16[4,192,256]{2,1,0:T(8,128)(2,1)S(1)}, u32[]{:S(2)}, u32[]{:S(2)}) async-start(bf16[4,192,256]{2,1,0:T(8,128)(2,1)} %get-tuple-element.126), calls=%async_computation.1 | async-start | bytes 786432 | tf_op jit(solution)/shard_map/all_to_all | solution.py:1283
  179.3 3.3 %add_convert_fusion = bf16[2,4,112,768]{3,2,1,0:T(8,128)(2,1)} fusion(bf16[2,4,112,768]{3,2,1,0:T(8,128)(2,1)} %collective-permute-done.33, bf16[2,4,112,768]{3,2,1,0:T(8,128)(2,1)} %get-tuple-element.129), kind=kLoop, calls=%fused_computation | loop fusion | flops 2752512 | bytes 4128768 | tf_op jit(solution)/shard_map/convert_element_type | solution.py:1252
  183.1 2.7 add_convert_fusion.1
  186.4 4.3 %all-to-all-done.1.refs_10_ = bf16[4,192,256]{2,1,0:T(8,128)(2,1)S(1)} async-done(((bf16[4,192,256]{2,1,0:T(8,128)(2,1)}), bf16[4,192,256]{2,1,0:T(8,128)(2,1)S(1)}, u32[]{:S(2)}, u32[]{:S(2)}) %all-to-all-start.1) | async-done | bytes 393248 | tf_op jit(solution)/shard_map/all_to_all | solution.py:1283
  191.4 14.8 %attend_back.1 = (bf16[256,768]{1,0:T(8,128)(2,1)}, bf16[256,768]{1,0:T(8,128)(2,1)}, bf16[256,768]{1,0:T(8,128)(2,1)}, bf16[256,768]{1,0:T(8,128)(2,1)}, bf16[3...) custom-call(s32[8]{0:T(128)} %compare_select_fusion.1.info, bf16[2,128,768]{2,1,0:T(8,128)(2,1)} %copy-done, ...), custom_call_target="tpu_custom_call" | custom-call | flops 12000000000 | bytes 6000000 | tf_op jit(solution)/shard_map/attend_back/pallas_call | solution.py:906
  206.3 8.8 %collective-permute-done.36 = bf16[2,4,112,768]{3,2,1,0:T(8,128)(2,1)} collective-permute-done((bf16[2,4,112,768]{3,2,1,0:T(8,128)(2,1)}, bf16[2,4,112,768]{3,2,1,0:T(8,128)(2,1)}, u32[]{:S(2)}, u32[]{:S(2)}) %collective-permute-start.36) | collective-permute-done | bytes 1376288 | tf_op jit(solution)/shard_map/ppermute | solution.py:1279
  218.1 2.5 collective-permute-start.37
  222.0 1.6 collective-permute-start.40
  223.7 4.9 %collective-permute-done.37 = bf16[256,768]{1,0:T(8,128)(2,1)S(1)} collective-permute-done((bf16[256,768]{1,0:T(8,128)(2,1)S(1)}, bf16[256,768]{1,0:T(8,128)(2,1)S(1)}, u32[]{:S(2)}, u32[]{:S(2)}) %collective-permute-start.37) | collective-permute-done | bytes 393248 | tf_op jit(solution)/shard_map/ppermute | solution.py:1270
  230.1 4.8 %collective-permute-done.42 = bf16[4,112,768]{2,1,0:T(8,128)(2,1)S(1)} collective-permute-done((bf16[4,112,768]{2,1,0:T(8,128)(2,1)S(1)}, bf16[4,112,768]{2,1,0:T(8,128)(2,1)S(1)}, u32[]{:S(2)}, u32[]{:S(2)}) %collective-permute-start.42) | collective-permute-done | bytes 688160 | tf_op jit(solution)/shard_map/ppermute | solution.py:1279
  236.4 2.3 collective-permute-done.40
  241.8 2.8 collective-permute-done.45
  245.3 3.2 %collective-permute-done.43 = bf16[224,768]{1,0:T(8,128)(2,1)S(1)} collective-permute-done((bf16[224,768]{1,0:T(8,128)(2,1)S(1)}, bf16[224,768]{1,0:T(8,128)(2,1)S(1)}, u32[]{:S(2)}, u32[]{:S(2)}) %collective-permute-start.43) | collective-permute-done | bytes 344096 | tf_op jit(solution)/shard_map/ppermute | solution.py:1270
  248.6 2.4 collective-permute-start.46
  251.5 5.6 %collective-permute-done.47 = bf16[304,768]{1,0:T(8,128)(2,1)S(1)} collective-permute-done((bf16[304,768]{1,0:T(8,128)(2,1)S(1)}, bf16[304,768]{1,0:T(8,128)(2,1)S(1)}, u32[]{:S(2)}, u32[]{:S(2)}) %collective-permute-start.47) | collective-permute-done | bytes 466976 | tf_op jit(solution)/shard_map/ppermute | solution.py:1279
  257.9 1.7 collective-permute-done.46
  259.7 3.3 %collective-permute-start.48 = (bf16[224,768]{1,0:T(8,128)(2,1)S(1)}, bf16[224,768]{1,0:T(8,128)(2,1)S(1)}, u32[]{:S(2)}, u32[]{:S(2)}) collective-permute-start(bf16[224,768]{1,0:T(8,128)(2,1)S(1)} %fusion.5), channel_id=1, source_target_pairs={{0,4},{1,5},{4,6},{5,7},{6,2},{7,3},{2,0},{3,1},{8,12},{9,13},{12,... | collective-permute-start | bytes 1032200 | tf_op jit(solution)/shard_map/ppermute | solution.py:1270
  263.0 5.0 %collective-permute-done.52 = bf16[256,768]{1,0:T(8,128)(2,1)S(1)} collective-permute-done((bf16[256,768]{1,0:T(8,128)(2,1)S(1)}, bf16[256,768]{1,0:T(8,128)(2,1)S(1)}, u32[]{:S(2)}, u32[]{:S(2)}) %collective-permute-start.52) | collective-permute-done | bytes 393248 | tf_op jit(solution)/shard_map/ppermute | solution.py:1270
  268.4 3.7 %collective-permute-done.48 = bf16[224,768]{1,0:T(8,128)(2,1)S(1)} collective-permute-done((bf16[224,768]{1,0:T(8,128)(2,1)S(1)}, bf16[224,768]{1,0:T(8,128)(2,1)S(1)}, u32[]{:S(2)}, u32[]{:S(2)}) %collective-permute-start.48) | collective-permute-done | bytes 344096 | tf_op jit(solution)/shard_map/ppermute | solution.py:1270
  272.2 2.8 collective-permute-start.49
  275.0 1.5 collective-permute-start.51
  278.3 5.7 %collective-permute-done.49.refs_1_ = bf16[224,768]{1,0:T(8,128)(2,1)S(1)} collective-permute-done((bf16[224,768]{1,0:T(8,128)(2,1)S(1)}, bf16[224,768]{1,0:T(8,128)(2,1)S(1)}, u32[]{:S(2)}, u32[]{:S(2)}) %collective-permute-start.49) | collective-permute-done | bytes 344096 | tf_op jit(solution)/shard_map/ppermute | solution.py:1279
  284.0 5.3 %collective-permute-done.50.refs_2_ = bf16[224,768]{1,0:T(8,128)(2,1)S(1)} collective-permute-done((bf16[224,768]{1,0:T(8,128)(2,1)S(1)}, bf16[224,768]{1,0:T(8,128)(2,1)S(1)}, u32[]{:S(2)}, u32[]{:S(2)}) %collective-permute-start.50) | collective-permute-done | bytes 344096 | tf_op jit(solution)/shard_map/ppermute | solution.py:1279
  290.8 4.2 %finish.1 = (f32[384,768]{1,0:T(8,128)}, f32[96,3072]{1,0:T(8,128)}, f32[96,768]{1,0:T(8,128)}, f32[96,768]{1,0:T(8,128)}, f32[96,768]{1,0:T(8,128)}, /*index=5*...) custom-call(s32[8]{0:T(128)} %compare_select_fusion.1.info, ...), custom_call_target="tpu_custom_call" | custom-call | flops 1000000 | bytes 8000000 | tf_op jit(solution)/shard_map/finish/pallas_call | solution.py:1221
  (178 shorter events, 38.2 us)
Async XLA Ops:
  11.7 13.6 %collective-permute-start.1 = (bf16[4,432,768]{2,1,0:T(8,128)(2,1)}, bf16[4,432,768]{2,1,0:T(8,128)(2,1)}, u32[]{:S(2)}, u32[]{:S(2)}) collective-permute-start(bf16[4,432,768]{2,1,0:T(8,128)(2,1)} %get-tuple-element.93.own), channel_id=1, source_target_pairs={{0,1},{1,0},{2,3},{3,2},{4,5},{5,4},{6,7},{7,6},{8,9},{9,8},{10,11... | collective-permute-start | bytes 7962632 | tf_op jit(solution)/shard_map/ppermute | solution.py:1276
  11.8 13.5 %collective-permute-start.6 = (bf16[2,3,96,768]{3,2,1,0:T(8,128)(2,1)}, bf16[2,3,96,768]{3,2,1,0:T(8,128)(2,1)S(1)}, u32[]{:S(2)}, u32[]{:S(2)}) collective-permute-start(bf16[2,3,96,768]{3,2,1,0:T(8,128)(2,1)} %get-tuple-element.95.refs_4_), channel_id=1, source_target_pairs={{0,1},{1,0},{2,3},{3,2},{4,5},{5,4},{6,7},{7,6},{8,9},{9,8},{10,11... | collective-permute-start | bytes 2654216 | tf_op jit(solution)/shard_map/ppermute | solution.py:1276
  12.2 13.1 %collective-permute-start.5 = (bf16[2,128,768]{2,1,0:T(8,128)(2,1)S(1)}, bf16[2,128,768]{2,1,0:T(8,128)(2,1)S(1)}, u32[]{:S(2)}, u32[]{:S(2)}) collective-permute-start(bf16[2,128,768]{2,1,0:T(8,128)(2,1)S(1)} %pad_maximum_fusion.refs_0_.refs_26_), channel_id=1, source_target_pairs={{0,4},{1,5},{4,6},{5,7},{6,2},{7,3},{2,0},{3,1},{8,12},{9,13},{12,... | collective-permute-start | bytes 1179656 | tf_op jit(solution)/shard_map/ppermute | solution.py:1270
  15.9 23.8 %collective-permute-start.2 = (bf16[432,768]{1,0:T(8,128)(2,1)}, bf16[432,768]{1,0:T(8,128)(2,1)S(1)}, u32[]{:S(2)}, u32[]{:S(2)}) collective-permute-start(bf16[432,768]{1,0:T(8,128)(2,1)} %get-tuple-element.94), channel_id=1, source_target_pairs={{0,4},{1,5},{4,6},{5,7},{6,2},{7,3},{2,0},{3,1},{8,12},{9,13},{12,... | collective-permute-start | bytes 1990664 | tf_op jit(solution)/shard_map/ppermute | solution.py:1270
  25.3 22.2 %collective-permute-start.7 = (bf16[2,128,768]{2,1,0:T(8,128)(2,1)S(1)}, bf16[2,128,768]{2,1,0:T(8,128)(2,1)S(1)}, u32[]{:S(2)}, u32[]{:S(2)}) collective-permute-start(bf16[2,128,768]{2,1,0:T(8,128)(2,1)S(1)} %collective-permute-done.5.refs_1_), channel_id=1, source_target_pairs={{0,4},{1,5},{4,6},{5,7},{6,2},{7,3},{2,0},{3,1},{8,12},{9,13},{12,... | collective-permute-start | bytes 1179656 | tf_op jit(solution)/shard_map/ppermute | solution.py:1270
  47.5 12.9 %collective-permute-start.8 = (bf16[2,128,768]{2,1,0:T(8,128)(2,1)S(1)}, bf16[2,128,768]{2,1,0:T(8,128)(2,1)S(1)}, u32[]{:S(2)}, u32[]{:S(2)}) collective-permute-start(bf16[2,128,768]{2,1,0:T(8,128)(2,1)S(1)} %collective-permute-done.7.refs_2_), channel_id=1, source_target_pairs={{0,4},{1,5},{4,6},{5,7},{6,2},{7,3},{2,0},{3,1},{8,12},{9,13},{12,... | collective-permute-start | bytes 1179656 | tf_op jit(solution)/shard_map/ppermute | solution.py:1270
  50.9 24.7 %collective-permute-start.3 = (bf16[432,768]{1,0:T(8,128)(2,1)S(1)}, bf16[432,768]{1,0:T(8,128)(2,1)}, u32[]{:S(2)}, u32[]{:S(2)}) collective-permute-start(bf16[432,768]{1,0:T(8,128)(2,1)S(1)} %collective-permute-done.2.refs_0_), channel_id=1, source_target_pairs={{0,8},{8,0},{16,24},{24,16},{1,9},{9,1},{17,25},{25,17},{2,10},{10... | collective-permute-start | bytes 1990664 | tf_op jit(solution)/shard_map/ppermute | solution.py:1279
  52.4 23.2 %collective-permute-start.4 = (bf16[432,768]{1,0:T(8,128)(2,1)S(1)}, bf16[432,768]{1,0:T(8,128)(2,1)S(1)}, u32[]{:S(2)}, u32[]{:S(2)}) collective-permute-start(bf16[432,768]{1,0:T(8,128)(2,1)S(1)} %collective-permute-done.2.refs_0_), channel_id=1, source_target_pairs={{0,16},{8,24},{16,0},{24,8},{1,17},{9,25},{17,1},{25,9},{2,18},{10... | collective-permute-start | bytes 1990664 | tf_op jit(solution)/shard_map/ppermute | solution.py:1279
  53.9 21.7 %collective-permute-start.9 = (bf16[432,768]{1,0:T(8,128)(2,1)S(1)}, bf16[432,768]{1,0:T(8,128)(2,1)}, u32[]{:S(2)}, u32[]{:S(2)}) collective-permute-start(bf16[432,768]{1,0:T(8,128)(2,1)S(1)} %collective-permute-done.2.refs_0_), channel_id=1, source_target_pairs={{0,4},{1,5},{4,6},{5,7},{6,2},{7,3},{2,0},{3,1},{8,12},{9,13},{12,... | collective-permute-start | bytes 1990664 | tf_op jit(solution)/shard_map/ppermute | solution.py:1270
  75.6 19.9 %collective-permute-start.11 = (bf16[432,768]{1,0:T(8,128)(2,1)}, bf16[432,768]{1,0:T(8,128)(2,1)}, u32[]{:S(2)}, u32[]{:S(2)}) collective-permute-start(bf16[432,768]{1,0:T(8,128)(2,1)} %collective-permute-done.9.refs_8_), channel_id=1, source_target_pairs={{0,4},{1,5},{4,6},{5,7},{6,2},{7,3},{2,0},{3,1},{8,12},{9,13},{12,... | collective-permute-start | bytes 1990664 | tf_op jit(solution)/shard_map/ppermute | solution.py:1270
  79.1 22.3 %collective-permute-start.17 = (bf16[432,768]{1,0:T(8,128)(2,1)}, bf16[432,768]{1,0:T(8,128)(2,1)}, u32[]{:S(2)}, u32[]{:S(2)}) collective-permute-start(bf16[432,768]{1,0:T(8,128)(2,1)} %collective-permute-done.9.refs_8_), channel_id=1, source_target_pairs={{0,16},{8,24},{16,0},{24,8},{1,17},{9,25},{17,1},{25,9},{2,18},{10... | collective-permute-start | bytes 1990664 | tf_op jit(solution)/shard_map/ppermute | solution.py:1279
  80.6 22.3 %collective-permute-start.16 = (bf16[432,768]{1,0:T(8,128)(2,1)}, bf16[432,768]{1,0:T(8,128)(2,1)}, u32[]{:S(2)}, u32[]{:S(2)}) collective-permute-start(bf16[432,768]{1,0:T(8,128)(2,1)} %collective-permute-done.9.refs_8_), channel_id=1, source_target_pairs={{0,8},{8,0},{16,24},{24,16},{1,9},{9,1},{17,25},{25,17},{2,10},{10... | collective-permute-start | bytes 1990664 | tf_op jit(solution)/shard_map/ppermute | solution.py:1279
  82.1 29.4 %collective-permute-start.10 = (bf16[432,768]{1,0:T(8,128)(2,1)}, bf16[432,768]{1,0:T(8,128)(2,1)}, u32[]{:S(2)}, u32[]{:S(2)}) collective-permute-start(bf16[432,768]{1,0:T(8,128)(2,1)} %collective-permute-done.3.refs_1_), channel_id=1, source_target_pairs={{0,16},{8,24},{16,0},{24,8},{1,17},{9,25},{17,1},{25,9},{2,18},{10... | collective-permute-start | bytes 1990664 | tf_op jit(solution)/shard_map/ppermute | solution.py:1279
  95.5 26.1 %collective-permute-start.24 = (bf16[432,768]{1,0:T(8,128)(2,1)}, bf16[432,768]{1,0:T(8,128)(2,1)S(1)}, u32[]{:S(2)}, u32[]{:S(2)}) collective-permute-start(bf16[432,768]{1,0:T(8,128)(2,1)} %collective-permute-done.11.refs_16_), channel_id=1, source_target_pairs={{0,16},{8,24},{16,0},{24,8},{1,17},{9,25},{17,1},{25,9},{2,18},{10... | collective-permute-start | bytes 1990664 | tf_op jit(solution)/shard_map/ppermute | solution.py:1279
  97.1 24.6 %collective-permute-start.23 = (bf16[432,768]{1,0:T(8,128)(2,1)}, bf16[432,768]{1,0:T(8,128)(2,1)S(1)}, u32[]{:S(2)}, u32[]{:S(2)}) collective-permute-start(bf16[432,768]{1,0:T(8,128)(2,1)} %collective-permute-done.11.refs_16_), channel_id=1, source_target_pairs={{0,8},{8,0},{16,24},{24,16},{1,9},{9,1},{17,25},{25,17},{2,10},{10... | collective-permute-start | bytes 1990664 | tf_op jit(solution)/shard_map/ppermute | solution.py:1279
  97.7 29.0 %all-to-all-start = ((bf16[4,2,192,256]{3,2,1,0:T(8,128)(2,1)}), bf16[4,2,192,256]{3,2,1,0:T(8,128)(2,1)S(1)}, u32[]{:S(2)}, u32[]{:S(2)}) async-start(bf16[4,2,192,256]{3,2,1,0:T(8,128)(2,1)} %attend_tutor.1), calls=%async_computation | async-start | bytes 1572864 | tf_op jit(solution)/shard_map/all_to_all | solution.py:1283
  101.4 23.0 %collective-permute-start.18 = (bf16[432,768]{1,0:T(8,128)(2,1)}, bf16[432,768]{1,0:T(8,128)(2,1)S(1)}, u32[]{:S(2)}, u32[]{:S(2)}) collective-permute-start(bf16[432,768]{1,0:T(8,128)(2,1)} %collective-permute-done.17.refs_10_), channel_id=1, source_target_pairs={{0,8},{8,0},{16,24},{24,16},{1,9},{9,1},{17,25},{25,17},{2,10},{10... | collective-permute-start | bytes 1990664 | tf_op jit(solution)/shard_map/ppermute | solution.py:1279
  102.9 21.5 %collective-permute-start.21 = (bf16[432,768]{1,0:T(8,128)(2,1)}, bf16[432,768]{1,0:T(8,128)(2,1)S(1)}, u32[]{:S(2)}, u32[]{:S(2)}) collective-permute-start(bf16[432,768]{1,0:T(8,128)(2,1)} %collective-permute-done.17.refs_10_), channel_id=1, source_target_pairs={{0,1},{1,0},{2,3},{3,2},{4,5},{5,4},{6,7},{7,6},{8,9},{9,8},{10,11... | collective-permute-start | bytes 1990664 | tf_op jit(solution)/shard_map/ppermute | solution.py:1276
  111.5 13.4 %collective-permute-start.20 = (bf16[432,768]{1,0:T(8,128)(2,1)}, bf16[432,768]{1,0:T(8,128)(2,1)S(1)}, u32[]{:S(2)}, u32[]{:S(2)}) collective-permute-start(bf16[432,768]{1,0:T(8,128)(2,1)} %collective-permute-done.16.refs_9_), channel_id=1, source_target_pairs={{0,1},{1,0},{2,3},{3,2},{4,5},{5,4},{6,7},{7,6},{8,9},{9,8},{10,11... | collective-permute-start | bytes 1990664 | tf_op jit(solution)/shard_map/ppermute | solution.py:1276
  121.7 5.0 %collective-permute-start.19 = (bf16[432,768]{1,0:T(8,128)(2,1)}, bf16[432,768]{1,0:T(8,128)(2,1)}, u32[]{:S(2)}, u32[]{:S(2)}) collective-permute-start(bf16[432,768]{1,0:T(8,128)(2,1)} %collective-permute-done.9.refs_8_), channel_id=1, source_target_pairs={{0,1},{1,0},{2,3},{3,2},{4,5},{5,4},{6,7},{7,6},{8,9},{9,8},{10,11... | collective-permute-start | bytes 1990664 | tf_op jit(solution)/shard_map/ppermute | solution.py:1276
  121.7 5.6 %collective-permute-start.15 = (bf16[432,768]{1,0:T(8,128)(2,1)}, bf16[432,768]{1,0:T(8,128)(2,1)}, u32[]{:S(2)}, u32[]{:S(2)}) collective-permute-start(bf16[432,768]{1,0:T(8,128)(2,1)} %collective-permute-done.10.refs_3_), channel_id=1, source_target_pairs={{0,1},{1,0},{2,3},{3,2},{4,5},{5,4},{6,7},{7,6},{8,9},{9,8},{10,11... | collective-permute-start | bytes 1990664 | tf_op jit(solution)/shard_map/ppermute | solution.py:1276
  126.7 10.8 %collective-permute-start.26 = (bf16[240,768]{1,0:T(8,128)(2,1)S(1)}, bf16[240,768]{1,0:T(8,128)(2,1)S(1)}, u32[]{:S(2)}, u32[]{:S(2)}) collective-permute-start(bf16[240,768]{1,0:T(8,128)(2,1)S(1)} %slice.105), channel_id=1, source_target_pairs={{0,8},{8,0},{16,24},{24,16},{1,9},{9,1},{17,25},{25,17},{2,10},{10... | collective-permute-start | bytes 1105928 | tf_op jit(solution)/shard_map/ppermute | solution.py:1279
  127.3 10.7 %collective-permute-start.27 = (bf16[432,768]{1,0:T(8,128)(2,1)}, bf16[432,768]{1,0:T(8,128)(2,1)S(1)}, u32[]{:S(2)}, u32[]{:S(2)}) collective-permute-start(bf16[432,768]{1,0:T(8,128)(2,1)} %collective-permute-done.11.refs_16_), channel_id=1, source_target_pairs={{0,1},{1,0},{2,3},{3,2},{4,5},{5,4},{6,7},{7,6},{8,9},{9,8},{10,11... | collective-permute-start | bytes 1990664 | tf_op jit(solution)/shard_map/ppermute | solution.py:1276
  127.3 10.1 %collective-permute-start.25 = (bf16[192,768]{1,0:T(8,128)(2,1)S(1)}, bf16[192,768]{1,0:T(8,128)(2,1)S(1)}, u32[]{:S(2)}, u32[]{:S(2)}) collective-permute-start(bf16[192,768]{1,0:T(8,128)(2,1)S(1)} %slice.104), channel_id=1, source_target_pairs={{0,16},{8,24},{16,0},{24,8},{1,17},{9,25},{17,1},{25,9},{2,18},{10... | collective-permute-start | bytes 884744 | tf_op jit(solution)/shard_map/ppermute | solution.py:1279
  127.9 12.6 %collective-permute-start.29 = (bf16[432,768]{1,0:T(8,128)(2,1)S(1)}, bf16[432,768]{1,0:T(8,128)(2,1)S(1)}, u32[]{:S(2)}, u32[]{:S(2)}) collective-permute-start(bf16[432,768]{1,0:T(8,128)(2,1)S(1)} %collective-permute-done.24.refs_18_), channel_id=1, source_target_pairs={{0,1},{1,0},{2,3},{3,2},{4,5},{5,4},{6,7},{7,6},{8,9},{9,8},{10,11... | collective-permute-start | bytes 1990664 | tf_op jit(solution)/shard_map/ppermute | solution.py:1276
  128.6 12.0 %collective-permute-start.28 = (bf16[432,768]{1,0:T(8,128)(2,1)S(1)}, bf16[432,768]{1,0:T(8,128)(2,1)S(1)}, u32[]{:S(2)}, u32[]{:S(2)}) collective-permute-start(bf16[432,768]{1,0:T(8,128)(2,1)S(1)} %collective-permute-done.23.refs_17_), channel_id=1, source_target_pairs={{0,1},{1,0},{2,3},{3,2},{4,5},{5,4},{6,7},{7,6},{8,9},{9,8},{10,11... | collective-permute-start | bytes 1990664 | tf_op jit(solution)/shard_map/ppermute | solution.py:1276
  174.6 8.5 %collective-permute-start.32 = (bf16[2,4,112,768]{3,2,1,0:T(8,128)(2,1)}, bf16[2,4,112,768]{3,2,1,0:T(8,128)(2,1)}, u32[]{:S(2)}, u32[]{:S(2)}) collective-permute-start(bf16[2,4,112,768]{3,2,1,0:T(8,128)(2,1)} %get-tuple-element.128), channel_id=1, source_target_pairs={{0,1},{1,0},{2,3},{3,2},{4,5},{5,4},{6,7},{7,6},{8,9},{9,8},{10,11... | collective-permute-start | bytes 4128776 | tf_op jit(solution)/shard_map/ppermute | solution.py:1276
  175.0 15.7 %all-to-all-start.1 = ((bf16[4,192,256]{2,1,0:T(8,128)(2,1)}), bf16[4,192,256]{2,1,0:T(8,128)(2,1)S(1)}, u32[]{:S(2)}, u32[]{:S(2)}) async-start(bf16[4,192,256]{2,1,0:T(8,128)(2,1)} %get-tuple-element.126), calls=%async_computation.1 | async-start | bytes 786432 | tf_op jit(solution)/shard_map/all_to_all | solution.py:1283
  178.7 36.4 %collective-permute-start.41 = (bf16[2,4,112,768]{3,2,1,0:T(8,128)(2,1)}, bf16[2,4,112,768]{3,2,1,0:T(8,128)(2,1)S(1)}, u32[]{:S(2)}, u32[]{:S(2)}) collective-permute-start(bf16[2,4,112,768]{3,2,1,0:T(8,128)(2,1)} %get-tuple-element.140), channel_id=1, source_target_pairs={{0,1},{1,0},{2,3},{3,2},{4,5},{5,4},{6,7},{7,6},{8,9},{9,8},{10,11... | collective-permute-start | bytes 4128776 | tf_op jit(solution)/shard_map/ppermute | solution.py:1276
  178.9 41.7 %collective-permute-start.39 = (bf16[2,4,112,768]{3,2,1,0:T(8,128)(2,1)}, bf16[2,4,112,768]{3,2,1,0:T(8,128)(2,1)S(1)}, u32[]{:S(2)}, u32[]{:S(2)}) collective-permute-start(bf16[2,4,112,768]{3,2,1,0:T(8,128)(2,1)} %get-tuple-element.137), channel_id=1, source_target_pairs={{0,1},{1,0},{2,3},{3,2},{4,5},{5,4},{6,7},{7,6},{8,9},{9,8},{10,11... | collective-permute-start | bytes 4128776 | tf_op jit(solution)/shard_map/ppermute | solution.py:1276
  182.6 32.5 %collective-permute-start.36 = (bf16[2,4,112,768]{3,2,1,0:T(8,128)(2,1)}, bf16[2,4,112,768]{3,2,1,0:T(8,128)(2,1)}, u32[]{:S(2)}, u32[]{:S(2)}) collective-permute-start(bf16[2,4,112,768]{3,2,1,0:T(8,128)(2,1)} %add_convert_fusion), channel_id=1, source_target_pairs={{0,16},{8,24},{16,0},{24,8},{1,17},{9,25},{17,1},{25,9},{2,18},{10... | collective-permute-start | bytes 4128776 | tf_op jit(solution)/shard_map/ppermute | solution.py:1279
  185.8 32.3 %collective-permute-start.35 = (bf16[2,4,112,768]{3,2,1,0:T(8,128)(2,1)}, bf16[2,4,112,768]{3,2,1,0:T(8,128)(2,1)}, u32[]{:S(2)}, u32[]{:S(2)}) collective-permute-start(bf16[2,4,112,768]{3,2,1,0:T(8,128)(2,1)} %add_convert_fusion.1), channel_id=1, source_target_pairs={{0,8},{8,0},{16,24},{24,16},{1,9},{9,1},{17,25},{25,17},{2,10},{10... | collective-permute-start | bytes 4128776 | tf_op jit(solution)/shard_map/ppermute | solution.py:1279
  206.3 11.0 %collective-permute-start.34 = (bf16[256,768]{1,0:T(8,128)(2,1)}, bf16[256,768]{1,0:T(8,128)(2,1)S(1)}, u32[]{:S(2)}, u32[]{:S(2)}) collective-permute-start(bf16[256,768]{1,0:T(8,128)(2,1)} %get-tuple-element.132), channel_id=1, source_target_pairs={{0,4},{1,5},{4,6},{5,7},{6,2},{7,3},{2,0},{3,1},{8,12},{9,13},{12,... | collective-permute-start | bytes 1179656 | tf_op jit(solution)/shard_map/ppermute | solution.py:1270
  215.1 8.5 %collective-permute-start.44 = (bf16[304,768]{1,0:T(8,128)(2,1)}, bf16[304,768]{1,0:T(8,128)(2,1)S(1)}, u32[]{:S(2)}, u32[]{:S(2)}) collective-permute-start(bf16[304,768]{1,0:T(8,128)(2,1)} %get-tuple-element.143), channel_id=1, source_target_pairs={{0,1},{1,0},{2,3},{3,2},{4,5},{5,4},{6,7},{7,6},{8,9},{9,8},{10,11... | collective-permute-start | bytes 1400840 | tf_op jit(solution)/shard_map/ppermute | solution.py:1276
  216.6 18.3 %collective-permute-start.42 = (bf16[4,112,768]{2,1,0:T(8,128)(2,1)S(1)}, bf16[4,112,768]{2,1,0:T(8,128)(2,1)S(1)}, u32[]{:S(2)}, u32[]{:S(2)}) collective-permute-start(bf16[4,112,768]{2,1,0:T(8,128)(2,1)S(1)} %fusion.3), channel_id=1, source_target_pairs={{0,8},{8,0},{16,24},{24,16},{1,9},{9,1},{17,25},{25,17},{2,10},{10... | collective-permute-start | bytes 2064392 | tf_op jit(solution)/shard_map/ppermute | solution.py:1279
  218.1 10.5 %collective-permute-start.37 = (bf16[256,768]{1,0:T(8,128)(2,1)S(1)}, bf16[256,768]{1,0:T(8,128)(2,1)S(1)}, u32[]{:S(2)}, u32[]{:S(2)}) collective-permute-start(bf16[256,768]{1,0:T(8,128)(2,1)S(1)} %add_convert_fusion.8), channel_id=1, source_target_pairs={{0,4},{1,5},{4,6},{5,7},{6,2},{7,3},{2,0},{3,1},{8,12},{9,13},{12,... | collective-permute-start | bytes 1179656 | tf_op jit(solution)/shard_map/ppermute | solution.py:1270
  222.0 16.6 %collective-permute-start.40 = (bf16[4,112,768]{2,1,0:T(8,128)(2,1)S(1)}, bf16[4,112,768]{2,1,0:T(8,128)(2,1)S(1)}, u32[]{:S(2)}, u32[]{:S(2)}) collective-permute-start(bf16[4,112,768]{2,1,0:T(8,128)(2,1)S(1)} %fusion.2), channel_id=1, source_target_pairs={{0,16},{8,24},{16,0},{24,8},{1,17},{9,25},{17,1},{25,9},{2,18},{10... | collective-permute-start | bytes 2064392 | tf_op jit(solution)/shard_map/ppermute | solution.py:1279
  228.6 15.9 %collective-permute-start.45 = (bf16[304,768]{1,0:T(8,128)(2,1)S(1)}, bf16[304,768]{1,0:T(8,128)(2,1)S(1)}, u32[]{:S(2)}, u32[]{:S(2)}) collective-permute-start(bf16[304,768]{1,0:T(8,128)(2,1)S(1)} %add_convert_fusion.6), channel_id=1, source_target_pairs={{0,8},{8,0},{16,24},{24,16},{1,9},{9,1},{17,25},{25,17},{2,10},{10... | collective-permute-start | bytes 1400840 | tf_op jit(solution)/shard_map/ppermute | solution.py:1279
  240.2 8.3 %collective-permute-start.43 = (bf16[224,768]{1,0:T(8,128)(2,1)S(1)}, bf16[224,768]{1,0:T(8,128)(2,1)S(1)}, u32[]{:S(2)}, u32[]{:S(2)}) collective-permute-start(bf16[224,768]{1,0:T(8,128)(2,1)S(1)} %fusion.10), channel_id=1, source_target_pairs={{0,4},{1,5},{4,6},{5,7},{6,2},{7,3},{2,0},{3,1},{8,12},{9,13},{12,... | collective-permute-start | bytes 1032200 | tf_op jit(solution)/shard_map/ppermute | solution.py:1270
  244.7 12.4 %collective-permute-start.47 = (bf16[304,768]{1,0:T(8,128)(2,1)S(1)}, bf16[304,768]{1,0:T(8,128)(2,1)S(1)}, u32[]{:S(2)}, u32[]{:S(2)}) collective-permute-start(bf16[304,768]{1,0:T(8,128)(2,1)S(1)} %add_convert_fusion.5), channel_id=1, source_target_pairs={{0,16},{8,24},{16,0},{24,8},{1,17},{9,25},{17,1},{25,9},{2,18},{10... | collective-permute-start | bytes 1400840 | tf_op jit(solution)/shard_map/ppermute | solution.py:1279
  248.6 11.1 %collective-permute-start.46 = (bf16[224,768]{1,0:T(8,128)(2,1)S(1)}, bf16[224,768]{1,0:T(8,128)(2,1)S(1)}, u32[]{:S(2)}, u32[]{:S(2)}) collective-permute-start(bf16[224,768]{1,0:T(8,128)(2,1)S(1)} %fusion.6), channel_id=1, source_target_pairs={{0,4},{1,5},{4,6},{5,7},{6,2},{7,3},{2,0},{3,1},{8,12},{9,13},{12,... | collective-permute-start | bytes 1032200 | tf_op jit(solution)/shard_map/ppermute | solution.py:1270
  251.1 17.0 %collective-permute-start.52 = (bf16[256,768]{1,0:T(8,128)(2,1)S(1)}, bf16[256,768]{1,0:T(8,128)(2,1)S(1)}, u32[]{:S(2)}, u32[]{:S(2)}) collective-permute-start(bf16[256,768]{1,0:T(8,128)(2,1)S(1)} %add_convert_fusion.7), channel_id=1, source_target_pairs={{0,4},{1,5},{4,6},{5,7},{6,2},{7,3},{2,0},{3,1},{8,12},{9,13},{12,... | collective-permute-start | bytes 1179656 | tf_op jit(solution)/shard_map/ppermute | solution.py:1270
  251.5 25.0 %collective-permute-start.38 = (bf16[128,768]{1,0:T(8,128)(2,1)S(1)}, bf16[128,768]{1,0:T(8,128)(2,1)S(1)}, u32[]{:S(2)}, u32[]{:S(2)}) collective-permute-start(bf16[128,768]{1,0:T(8,128)(2,1)S(1)} %copy-done.38), channel_id=1, source_target_pairs={{0,1},{1,0},{2,3},{3,2},{4,5},{5,4},{6,7},{7,6},{8,9},{9,8},{10,11... | collective-permute-start | bytes 589832 | tf_op jit(solution)/shard_map/ppermute | solution.py:1276
  259.7 12.4 %collective-permute-start.48 = (bf16[224,768]{1,0:T(8,128)(2,1)S(1)}, bf16[224,768]{1,0:T(8,128)(2,1)S(1)}, u32[]{:S(2)}, u32[]{:S(2)}) collective-permute-start(bf16[224,768]{1,0:T(8,128)(2,1)S(1)} %fusion.5), channel_id=1, source_target_pairs={{0,4},{1,5},{4,6},{5,7},{6,2},{7,3},{2,0},{3,1},{8,12},{9,13},{12,... | collective-permute-start | bytes 1032200 | tf_op jit(solution)/shard_map/ppermute | solution.py:1270
  268.3 9.0 %collective-permute-start.53 = (f32[128,768]{1,0:T(8,128)S(1)}, f32[128,768]{1,0:T(8,128)S(1)}, u32[]{:S(2)}, u32[]{:S(2)}) collective-permute-start(f32[128,768]{1,0:T(8,128)S(1)} %get-tuple-element.167), channel_id=1, source_target_pairs={{0,1},{1,0},{2,3},{3,2},{4,5},{5,4},{6,7},{7,6},{8,9},{9,8},{10,11... | collective-permute-start | bytes 1179656 | tf_op jit(solution)/shard_map/ppermute | solution.py:1276
  272.2 11.8 %collective-permute-start.49 = (bf16[224,768]{1,0:T(8,128)(2,1)S(1)}, bf16[224,768]{1,0:T(8,128)(2,1)S(1)}, u32[]{:S(2)}, u32[]{:S(2)}) collective-permute-start(bf16[224,768]{1,0:T(8,128)(2,1)S(1)} %fusion.4.refs_0_), channel_id=1, source_target_pairs={{0,8},{8,0},{16,24},{24,16},{1,9},{9,1},{17,25},{25,17},{2,10},{10... | collective-permute-start | bytes 1032200 | tf_op jit(solution)/shard_map/ppermute | solution.py:1279
  275.0 14.3 %collective-permute-start.50 = (bf16[224,768]{1,0:T(8,128)(2,1)S(1)}, bf16[224,768]{1,0:T(8,128)(2,1)S(1)}, u32[]{:S(2)}, u32[]{:S(2)}) collective-permute-start(bf16[224,768]{1,0:T(8,128)(2,1)S(1)} %fusion.4.refs_0_), channel_id=1, source_target_pairs={{0,16},{8,24},{16,0},{24,8},{1,17},{9,25},{17,1},{25,9},{2,18},{10... | collective-permute-start | bytes 1032200 | tf_op jit(solution)/shard_map/ppermute | solution.py:1279
  275.0 14.3 %collective-permute-start.51 = (bf16[224,768]{1,0:T(8,128)(2,1)S(1)}, bf16[224,768]{1,0:T(8,128)(2,1)S(1)}, u32[]{:S(2)}, u32[]{:S(2)}) collective-permute-start(bf16[224,768]{1,0:T(8,128)(2,1)S(1)} %fusion.4.refs_0_), channel_id=1, source_target_pairs={{0,24},{8,16},{16,8},{24,0},{1,25},{9,17},{17,9},{25,1},{2,26},{10... | collective-permute-start | bytes 1032200 | tf_op jit(solution)/shard_map/ppermute | solution.py:1279
  (47 other events, 465.3 us)

commit v3 on v2

--- a/solution.py
+++ b/solution.py
@@ -727,7 +727,7 @@
             qkv_out[2, rows] = v
         return carry
 
-    lax.fori_loop(0, line, project, 0)
+    lax.fori_loop(0, line, project, 0, unroll=True)
     fill = jnp.where(
         lax.broadcasted_iota(jnp.int32, (total, 1), 0) < length, 0.0, NEG_FILL
     ).astype(F32)
@@ -948,50 +948,52 @@
 
 
 def middle_kernel(info, own, sib, *refs):
-    chunks, refs = refs[:26], refs[26:]
+    chunks, refs = refs[:30], refs[30:]
     (x_own, ctx, vecs) = refs[:3]
     (out_keep, out_send, dfirst_keep, dctx_out) = refs[3:7]
     grads = refs[7:15]
-    (w_up, w_dn, w_out, gate_pre, lower, gup, gdn, sums, base, aim, acc, sems) = refs[15:]
+    (weights, w_out, slopes, lower, gup, gdn, sums, base, aim, acc, sems) = refs[15:]
     core, rep, place, length = info[I_CORE], info[I_REP], info[I_Z], info[I_LEN]
-    _, groups, quarters, rows, width = w_up.shape
+    _, quarters, groups, pair, width = weights.shape
+    rows = pair // 2
     tokens = ctx.shape[3]
     line = groups // 2
     hidden = groups * rows
     half = rows // 2
 
-    def place_piece(src, first, last, r, g):
-        fields = (
-            (0, rows, lambda: w_up.at[0, g, r], 0),
-            (rows, 2 * rows, lambda: w_dn.at[0, r, g], 1),
-            (2 * rows, 3 * rows, lambda: w_up.at[1, g, r], 2),
-            (3 * rows, 4 * rows, lambda: w_dn.at[1, r, g], 3),
-            (4 * rows, 4 * rows + half, lambda: w_out.at[r // 2, g, lax.rem(r, 2)], 4),
-        )
-        for lo, hi, dst, sem in fields:
-            if first <= lo and hi <= last:
-                pltpu.make_async_copy(
-                    src.at[pl.ds(lo - first, hi - lo)], dst(), sems.at[sem]
-                ).start()
-
-    piece = 4 * rows + half
+    piece = 2 * pair + half
+    found = []
     for rel, ref in ((0, own), (1, sib)):
         member = 2 * place + (core if rel == 0 else 1 - core)
-        for r in range(quarters):
-            place_piece(ref.at[r], 0, piece, r, member)
+        found += [(ref.at[r], 0, piece, r, member) for r in range(quarters)]
     for k in range(1, line):
         for rel in range(2):
             member = 2 * info[I_RING + k] + (core if rel == 0 else 1 - core)
-            got = chunks[(k - 1) * 8 + rel * (4 if k < line - 1 else 5) :]
-            for far in range(3):
-                place_piece(got[far], 0, piece, rep ^ far, member)
-            if k < line - 1:
-                place_piece(got[3], 0, piece, rep ^ 3, member)
-            else:
-                place_piece(got[3], 0, 2 * rows, rep ^ 3, member)
-                place_piece(got[4], 2 * rows, piece, rep ^ 3, member)
-
-    wait_all(w_out, sems.at[4])
+            got = chunks[((k - 1) * 2 + rel) * 5 :]
+            found += [(got[far], 0, piece, rep ^ far, member) for far in range(3)]
+            found.append((got[3], 0, pair, rep ^ 3, member))
+            found.append((got[4], pair, piece, rep ^ 3, member))
+    fields = (
+        (2 * pair, piece, lambda r, g: w_out.at[r // 2, g, lax.rem(r, 2)], 2),
+        (pair, 2 * pair, lambda r, g: weights.at[1, r, g], 1),
+        (0, pair, lambda r, g: weights.at[0, r, g], 0),
+    )
+    for lo, hi, target, sem in fields:
+        for src, first, last, r, g in found:
+            if first <= lo and hi <= last:
+                pltpu.make_async_copy(
+                    src.at[pl.ds(lo - first, hi - lo)], target(r, g), sems.at[sem]
+                ).start()
+
+    def up_rows(net, r):
+        return jnp.concatenate(
+            [weights[net, q, 2 * r + g, 0:rows] for g in range(2) for q in range(quarters)], axis=0
+        )
+
+    def down_rows(net, r):
+        return weights[net, r, :, rows:].reshape(width, hidden)
+
+    wait_all(w_out, sems.at[2])
     x_low = jnp.concatenate(
         [x_own[jnp.where(core == j, 0, 1)] for j in range(2)], axis=0
     ).astype(F32)
@@ -1015,17 +1017,18 @@
 
         def step(r, carry):
             gate = (
-                dims(upper_in, w_up[net, pl.ds(2 * r, 2)].reshape(hidden, width), 1, 1)
+                dims(upper_in, up_rows(net, r), 1, 1)
                 + vecs[net, V_UP + r]
             )
-            low = gelu_exact(gate).astype(BF16)
+            below = 0.5 * (1.0 + lax.erf(gate * 0.7071067811865476))
+            low = (gate * below).astype(BF16)
             if keep:
-                gate_pre[r] = gate
+                slopes[r] = below + gate * (0.3989422804014327 * jnp.exp(-0.5 * gate * gate))
                 lower[r] = low
-            acc[...] += dims(low, w_dn[net, r].reshape(width, hidden), 1, 1)
+            acc[...] += dims(low, down_rows(net, r), 1, 1)
             return carry
 
-        lax.fori_loop(0, quarters, step, 0)
+        lax.fori_loop(0, quarters, step, 0, unroll=True)
         return acc[...]
 
     _, ctx_tutor = context_of(1)
@@ -1033,14 +1036,12 @@
     ctx_flat, ctx_low = context_of(0)
     normed_one, inv_one, first_norm_s = upper(0, ctx_low)
     base[...] = first_norm_s
-    wait_all(w_up.at[1], sems.at[2])
-    wait_all(w_dn.at[1], sems.at[3])
+    wait_all(weights.at[1], sems.at[1])
     second = first_norm + lower_half(1, first_norm.astype(BF16), False) + row(1, V_DOWN)
     normed, _ = norm_parts(second)
     aim[...] = normed * row(1, V_G2) + row(1, V_S2)
 
-    wait_all(w_up.at[0], sems.at[0])
-    wait_all(w_dn.at[0], sems.at[1])
+    wait_all(weights.at[0], sems.at[0])
     upper_in = first_norm_s.astype(BF16)
     second = base[...] + lower_half(0, upper_in, True) + row(0, V_DOWN)
     normed_two, inv_two = norm_parts(second)
@@ -1066,21 +1067,44 @@
     g_down_t = turned(dsecond)
     acc[...] = dsecond
 
+    def member_of(rel, z):
+        return 2 * z + (core if rel == 0 else 1 - core)
+
+    def send_up(rel, far, k, z, part):
+        ref = grads[rel * 4 + (far & 1)].at[far >> 1, k, part]
+        src = gup.at[member_of(rel, z), rep ^ far, part]
+        pltpu.make_async_copy(src, ref, sems.at[3 + rel * 4 + (far & 1)]).start()
+
+    def send_down(rel, high, low, k, z, r, part):
+        ref = grads[rel * 4 + 2 + high].at[low, k, part]
+        src = gdn.at[r, member_of(rel, z), part]
+        pltpu.make_async_copy(src, ref, sems.at[5 + rel * 4 + high]).start()
+
+    main, rest = pl.ds(0, rows), pl.ds(rows, PAD)
+
     def back(r, carry):
         low = lower[r]
         gdn[r, :, 0:rows] = dims(g_down_t, low, 1, 0).astype(BF16).reshape(groups, rows, hidden)
-        dlower = dims(g_down, w_dn[0, r].reshape(width, hidden), 1, 0)
-        gate = gate_pre[r]
-        slope = 0.5 * (1.0 + lax.erf(gate * 0.7071067811865476)) + gate * (
-            0.3989422804014327 * jnp.exp(-0.5 * gate * gate)
-        )
-        dgate = dlower * slope
+        dlower = dims(g_down, down_rows(0, r), 1, 0)
+        dgate = dlower * slopes[r]
         sums[S_UP + r] = jnp.sum(dgate, axis=0, keepdims=True)
         gup_r = dims(turned(dgate), upper_in, 1, 0).astype(BF16)
         gup[pl.ds(2 * r, 2), :, 0:rows] = gup_r.reshape(2, quarters, rows, width)
-        acc[...] += dims(
-            dgate.astype(BF16), w_up[0, pl.ds(2 * r, 2)].reshape(hidden, width), 1, 0
-        )
+        acc[...] += dims(dgate.astype(BF16), up_rows(0, r), 1, 0)
+        hops = 0
+        for k in range(1, line):
+            hops = jnp.where(info[I_RING + k] == r, k, hops)
+        far = r ^ rep
+        for rel in range(2):
+            for way in range(4):
+                send_up(rel, way, hops, r, main)
+            for high in range(2):
+
+                @pl.when(far // 2 == high)
+                def _():
+                    for k in range(line):
+                        send_down(rel, high, far & 1, k, info[I_RING + k], r, main)
+
         return carry
 
     lax.fori_loop(0, quarters, back, 0)
@@ -1125,23 +1149,13 @@
             gdn[r, g, rows:] = jnp.concatenate([gout[g, r, PAD:slim], tail], axis=0).astype(BF16)
 
     for rel in range(2):
-        a_keep, a_send, b_keep, b_send = grads[rel * 4 : rel * 4 + 4]
         for far in range(4):
-            r = rep ^ far
             for k in range(line):
-                g = 2 * info[I_RING + k] + (core if rel == 0 else 1 - core)
-                a_ref = a_send if far & 1 else a_keep
-                b_ref = b_send if far & 2 else b_keep
-                pltpu.make_async_copy(
-                    gup.at[g, r], a_ref.at[far >> 1, k], sems.at[5 + rel * 4 + (far & 1)]
-                ).start()
-                pltpu.make_async_copy(
-                    gdn.at[r, g], b_ref.at[far & 1, k], sems.at[7 + rel * 4 + (far >> 1)]
-                ).start()
-    for rel in range(2):
-        for slot in range(4):
-            ref = grads[rel * 4 + slot]
-            wait_all(ref, sems.at[5 + rel * 4 + slot])
+                z = info[I_RING + k]
+                send_up(rel, far, k, z, rest)
+                send_down(rel, far >> 1, far & 1, k, z, rep ^ far, rest)
+    for slot in range(8):
+        wait_all(grads[slot], sems.at[3 + slot])
 
 
 def middle(info, own, sib, chunks, x_own, ctx, vecs):
@@ -1161,11 +1175,10 @@
     return pl.pallas_call(
         middle_kernel,
         out_shape=outs,
-        in_specs=[SM] + [ANY] * 28 + [VM] * 3,
+        in_specs=[SM] + [ANY] * 32 + [VM] * 3,
         out_specs=(VM,) * 4 + (ANY,) * 8,
         scratch_shapes=[
-            pltpu.VMEM((2, groups, quarters, rows, width), BF16),
-            pltpu.VMEM((2, quarters, groups, rows, width), BF16),
+            pltpu.VMEM((2, quarters, groups, 2 * rows, width), BF16),
             pltpu.VMEM((2, groups, 2, rows // 2, width), BF16),
             pltpu.VMEM((quarters, tokens, width), F32),
             pltpu.VMEM((quarters, tokens, width), BF16),
@@ -1175,7 +1188,7 @@
             pltpu.VMEM((tokens, width), F32),
             pltpu.VMEM((tokens, width), F32),
             pltpu.VMEM((tokens, width), F32),
-            pltpu.SemaphoreType.DMA((13,)),
+            pltpu.SemaphoreType.DMA((11,)),
         ],
         compiler_params=params(),
         cost_estimate=cost(15e9, 30e6, 4e6),
@@ -1183,27 +1196,78 @@
     )(info, own, sib, *chunks, x_own, ctx, vecs)
 
 
-def finish_kernel(entries, info, *refs):
-    pieces, refs = refs[:4], refs[4:]
-    grad_qkv, up, down, out, gq, gk, gv, loss, bq, bv, bu = refs[:11]
-    others, scr, sem = refs[11:17], refs[17], refs[18]
+def finish_up_kernel(info, *refs):
+    pieces, (up, out, scr, sem) = refs[:4], refs[4:]
     rep = info[I_REP]
     for far, ref in enumerate(pieces):
         pltpu.make_async_copy(ref, scr.at[rep ^ far], sem.at[0]).start()
-    rows, width = gq.shape
+    wait_all(scr, sem.at[0])
+    rows = up.shape[0] // len(pieces)
+    for r in range(len(pieces)):
+        up[r * rows : (r + 1) * rows] = scr[r, 0:rows].astype(F32)
+        out[r * PAD : (r + 1) * PAD] = scr[r, rows:].astype(F32)
+
+
+def finish_up(info, pieces):
+    high, width = pieces[0].shape
+    rows = high - PAD
+    return pl.pallas_call(
+        finish_up_kernel,
+        out_shape=(
+            jax.ShapeDtypeStruct((4 * rows, width), F32),
+            jax.ShapeDtypeStruct((4 * PAD, width), F32),
+        ),
+        in_specs=[SM] + [ANY] * 4,
+        out_specs=(VM,) * 2,
+        scratch_shapes=[
+            pltpu.VMEM((4, high, width), BF16),
+            pltpu.SemaphoreType.DMA((1,)),
+        ],
+        compiler_params=params(),
+        cost_estimate=cost(1e6, 3e6),
+        name="finish_up",
+    )(info, *pieces)
+
+
+def finish_heads_kernel(grad_qkv, gq, gk, gv, bq, bv):
+    rows = gq.shape[0]
     for slot, ref in enumerate((gq, gk, gv)):
         ref[...] = grad_qkv[slot * rows : (slot + 1) * rows].astype(F32)
     bias = grad_qkv[3 * rows :].astype(F32)
     bq[...] = bias[0, :rows]
     bv[...] = bias[0, rows : 2 * rows]
+
+
+def finish_heads(grad_qkv):
+    high, width = grad_qkv.shape
+    rows = (high - 16) // 3
+    return pl.pallas_call(
+        finish_heads_kernel,
+        out_shape=(jax.ShapeDtypeStruct((rows, width), F32),) * 3
+        + (jax.ShapeDtypeStruct((rows,), F32),) * 2,
+        in_specs=[VM],
+        out_specs=(VM,) * 5,
+        compiler_params=params(),
+        cost_estimate=cost(1e6, 2e6),
+        name="finish_heads",
+    )(grad_qkv)
+
+
+def finish_kernel(entries, info, *refs):
+    pieces, refs = refs[:4], refs[4:]
+    firsts, down, out, loss, bu = refs[:5]
+    others, scr, sem = refs[5:11], refs[11], refs[12]
+    rep = info[I_REP]
+    for far, ref in enumerate(pieces):
+        pltpu.make_async_copy(ref, scr.at[rep ^ far], sem.at[0]).start()
+    rows, width = out.shape
+    slim = rows // len(pieces)
+    for r in range(len(pieces)):
+        out[r * slim : r * slim + PAD] = firsts[r * PAD : (r + 1) * PAD]
     wait_all(scr, sem.at[0])
-    slim = rows // len(pieces)
-    high = rows + PAD
     for r in range(len(pieces)):
-        up[r * rows : (r + 1) * rows] = scr[r, 0:rows].astype(F32)
-        down[:, r * width : (r + 1) * width] = scr[r, high : high + rows].astype(F32)
-        out[r * slim : r * slim + PAD] = scr[r, rows:high].astype(F32)
-        last = scr[r, high + rows :].astype(F32)
+        down[:, r * width : (r + 1) * width] = scr[r, 0:rows].astype(F32)
+        last = scr[r, rows:].astype(F32)
         out[r * slim + PAD : (r + 1) * slim] = last[: slim - PAD]
         if r == 0:
             tail = last[slim - PAD :]
@@ -1213,36 +1277,29 @@
             loss[...] = jnp.full((1, 1), jnp.sum(tail[S_UP + 1 : S_UP + 2]) / entries, F32)
 
 
-def finish(info, pieces, grad_qkv, entries):
+def finish(info, pieces, firsts, entries):
     high, width = pieces[0].shape
-    rows = high // 2 - PAD
-    small = jax.ShapeDtypeStruct((rows, width), F32)
+    rows = high - PAD
     vector = jax.ShapeDtypeStruct((rows,), F32)
     return pl.pallas_call(
         functools.partial(finish_kernel, entries),
         out_shape=(
-            jax.ShapeDtypeStruct((4 * rows, width), F32),
             jax.ShapeDtypeStruct((rows, 4 * width), F32),
-            small,
-            small,
-            small,
-            small,
+            jax.ShapeDtypeStruct((rows, width), F32),
             jax.ShapeDtypeStruct((1, 1), F32),
-            vector,
-            vector,
             jax.ShapeDtypeStruct((4 * rows,), F32),
         )
         + (vector,) * 6,
         in_specs=[SM] + [ANY] * 4 + [VM],
-        out_specs=(VM,) * 16,
+        out_specs=(VM,) * 10,
         scratch_shapes=[
             pltpu.VMEM((4, high, width), BF16),
             pltpu.SemaphoreType.DMA((1,)),
         ],
         compiler_params=params(),
-        cost_estimate=cost(1e6, 8e6),
+        cost_estimate=cost(1e6, 4e6),
         name="finish",
-    )(info, *pieces, grad_qkv)
+    )(info, *pieces, firsts)
 
 
 def add_low(*terms):
@@ -1298,35 +1355,42 @@
     swapped = swap(jnp.where(core == 0, tokens[1], tokens[0]))
     x_own = jnp.stack([keep, swapped])
     x_1 = next_z(x_own)
-    qkv_own, own, piece = pack(after(info, x_own), latents, tutors)
+    qkv_own, own, piece = pack(info, latents, tutors)
     heads_bias, vecs = table(vectors, tutor_vectors, line)
 
     def to_sides(value):
         return [value, to_rep(value, 1), to_rep(value, 2)]
 
+    def to_far(got, *ready):
+        got.append(to_rep(after(got[1][: 2 * rows], *ready), 2))
+        got.append(to_rep(after(got[2][2 * rows :], *ready), 1))
+
     piece_1 = next_z(piece)
+    x_1 = next_z(after(x_own, piece))
     qkv_sib = swap(qkv_own)
     sib = swap(own)
-    x_2 = next_z(after(x_1, sib, qkv_sib))
-    x_3 = next_z(after(x_2, piece_1))
-    piece_2 = next_z(piece_1)
     got_1 = to_sides(piece_1)
+    x_2 = next_z(after(x_1, piece_1, qkv_sib))
+    x_3 = next_z(after(x_2, sib, *got_1))
+    piece_2 = next_z(after(piece_1, x_2))
+    to_far(got_1, x_2)
     tokens_in = [x_own, x_1, x_2, x_3]
     mixed, qkv, lse, ctx = attend(info, tokens_in, qkv_own, qkv_sib, heads_bias, clip)
-    mixed = after(mixed, *got_1, piece_2)
+    mixed = after(mixed, piece_2, *got_1)
     piece_2 = after(piece_2, mixed)
     piece_3 = next_z(piece_2)
     got_2 = to_sides(piece_2)
-    got_1.append(to_rep(after(got_1[1], mixed), 2))
     (mixed,) = attend(info, tokens_in, qkv_own, qkv_sib, heads_bias, clip, mixed)
-    got_2.append(to_rep(after(got_2[2], mixed), 1))
     got_3 = to_sides(after(piece_3, mixed))
     mixed = to_tokens(mixed)
-    got_3.append(to_rep(after(got_3[1][: 2 * rows], mixed), 2))
-    got_3.append(to_rep(after(got_3[2][2 * rows :], mixed), 1))
+    to_far(got_3, got_3[1], got_3[2])
+    to_far(got_2, got_3[1], got_3[2])
     chunks = []
     for got in (got_1, got_2, got_3):
-        chunks += got + [swap(after(one, got_3[0])) for one in got]
+        ready = mixed if got is got_3 else got_3[0]
+        chunks += got
+        chunks += [swap(after(one, got_3[0])) for one in got[:3]]
+        chunks += [swap(after(far, ready)) for far in got[3:]]
     (
         out_keep,
         out_send,
@@ -1355,30 +1419,27 @@
     )
     moving_1 = next_z(part1)
     gqkv_sib = swap(gqkv_sib)
-    a_next = to_rep(add_low(a_keep[1], a_keep_sib[1], after(a_in, part1)[1]), 2)
-    b_next = to_rep(add_low(b_keep[1], b_keep_sib[1], after(b_in, part1)[1]), 1)
-    moving_2 = next_z(after(add_low(moving_1, part2), a_in, b_in))
-    both = jnp.concatenate(
-        [
-            add_low(a_keep[0], a_keep_sib[0], a_in[0], a_next),
-            add_low(b_keep[0], b_keep_sib[0], b_in[0], b_next),
-        ],
-        axis=1,
-    )
+    a_next = add_low(a_keep[1], a_keep_sib[1], after(a_in, part1)[1])
+    b_next = add_low(b_keep[1], b_keep_sib[1], after(b_in, part1)[1])
+    moving_2 = next_z(after(add_low(moving_1, part2), a_next, b_next))
+    a_next, b_next = to_rep(a_next, 2), to_rep(b_next, 1)
+    part_a = add_low(a_keep[0], a_keep_sib[0], a_in[0], a_next)
+    part_b = add_low(b_keep[0], b_keep_sib[0], b_in[0], b_next)
     moving_3 = next_z(add_low(moving_2, part3))
-    grads_1 = next_z(both[1])
     layer_out = by_micro(out_keep, swap(after(out_send, moving_2)))
     gqkv = add_low(gqkv, gqkv_sib)
+    a_1, b_1 = next_z(part_a[1]), next_z(part_b[1])
     gqkv = add_low(gqkv, to_rep(after(gqkv, moving_2), 1))
-    grads_2 = next_z(after(add_low(grads_1, both[2]), gqkv))
+    a_2, b_2 = next_z(add_low(a_1, part_a[2])), next_z(after(add_low(b_1, part_b[2]), gqkv))
     gqkv = add_low(gqkv, to_rep(gqkv, 2))
-    grads_3 = next_z(after(add_low(grads_2, both[3]), gqkv))
-    grads = add_low(grads_3, both[0])
-    quarter = to_sides(grads) + [to_rep(grads, 3)]
+    a_3, b_3 = next_z(add_low(a_2, part_a[3])), next_z(after(add_low(b_2, part_b[3]), gqkv))
+    grad_q, grad_k, grad_v, bq, bv = finish_heads(gqkv)
+    a_all, b_all = add_low(a_3, part_a[0]), add_low(b_3, part_b[0])
+    a_all = to_sides(a_all) + [to_rep(a_all, 3)]
+    b_all = to_sides(b_all) + [to_rep(b_all, 3)]
+    grad_up, firsts = finish_up(info, a_all)
     entries = micro_count * 4 * 2 * line * local_rows * width
-    ends = finish(info, quarter, gqkv, entries)
-    grad_up, grad_down, grad_out, grad_q, grad_k, grad_v, loss, bq, bv, bu = ends[:10]
-    bo, bd, g1, s1, g2, s2 = ends[10:]
+    grad_down, grad_out, loss, bu, bo, bd, g1, s1, g2, s2 = finish(info, b_all, firsts, entries)
 
     hidden_tokens = jnp.where(core == 0, x_own, x_own[::-1])
     hidden_tokens = hidden_tokens.reshape(2 * local_rows, width).astype(F32)

time: 296 us -> 269 us (0.909)
  waiting for transfers between devices: 122 us -> 84.9 us
  starting transfers between devices: 59.4 us -> 75.9 us
  Pallas kernels: 84.8 us -> 78.2 us
    ppermute x19 -> x24, waiting for transfers between devices: 65.5 us -> 26.9 us  [to_rep(): return lax.ppermute(x, 'rep', [(i, i ^ bit) for i in range(4)])]
    ppermute x19 -> x24, starting transfers between devices: 21 us -> 30.9 us  [to_rep(): return lax.ppermute(x, 'rep', [(i, i ^ bit) for i in range(4)])]
    ppermute x12 -> x15, starting transfers between devices: 26.3 us -> 32.5 us  [over_z(): lax.ppermute(x, 'grp', [(2 * a + c, 2 * b + c) for a, b in pairs for c in...]
    pallas_call x1 -> x3, Pallas kernels: 31.4 us -> 27.4 us  [the longest x1 22.5 us: middle(): pl.pallas_call(middle_kernel, out_shape=outs, in_specs=[SM] + [ANY] * 32...]
    slice x2 -> x6, local copies, waits for them, and re-layouts: 0.04 us -> 3.02 us  [the longest x3 2.94 us: to_far(): got.append(to_rep(after(got[1][:2 * rows], *ready), 2))]
    ppermute x12 -> x15, waiting for transfers between devices: 48.9 us -> 50.3 us  [over_z(): lax.ppermute(x, 'grp', [(2 * a + c, 2 * b + c) for a, b in pairs for c in...]
    convert_element_type x14 -> x17, other arithmetic: 13.5 us -> 12.3 us  [add_low(): return total.astype(BF16)]
    unnamed x78 -> x88, local copies, waits for them, and re-layouts: 6.87 us -> 5.68 us
  transfers between devices with their start and end apart: 56 -> 66, of which waited for: 24 -> 24; matrix products, arithmetic and copies ran while one was open for 6% -> 7% of each run, Pallas kernels for 15% -> 18%
where the time goes in v3:
time: 269 us; the launch traced here: 268 us
  waiting for transfers between devices  84.9 us (32%)
  Pallas kernels  78.2 us (29%)
  starting transfers between devices  75.9 us (28%)
  other arithmetic  15.7 us (6%)
  local copies, waits for them, and re-layouts  10.6 us (4%)
  between operations  2.87 us (1%)
    ppermute x15, waiting for transfers between devices, over_z(): lax.ppermute(x, 'grp', [(2 * a + c, 2 * b + c) for a, b in pairs for c in...  50.3 us
    ppermute x15, starting transfers between devices, over_z(): lax.ppermute(x, 'grp', [(2 * a + c, 2 * b + c) for a, b in pairs for c in...  32.5 us
    ppermute x24, starting transfers between devices, to_rep(): return lax.ppermute(x, 'rep', [(i, i ^ bit) for i in range(4)])  30.9 us
    ppermute x24, waiting for transfers between devices, to_rep(): return lax.ppermute(x, 'rep', [(i, i ^ bit) for i in range(4)])  26.9 us
    pallas_call x2, Pallas kernels, attend(): pl.pallas_call(functools.partial(attend_kernel, student), out_shape=tuple...  25.7 us
    pallas_call x1, Pallas kernels, middle(): pl.pallas_call(middle_kernel, out_shape=outs, in_specs=[SM] + [ANY] * 32...  22.5 us
    pallas_call x1, Pallas kernels, attend_back(): pl.pallas_call(attend_back_kernel, out_shape=(part,) * 4 + (grad, grad),...  14.8 us
    convert_element_type x17, other arithmetic, add_low(): return total.astype(BF16)  12.3 us
  transfers between devices with their start and end apart: 66, of which 24 were waited for; matrix products, arithmetic and copies ran while one was open for 7% of the time, Pallas kernels for 18%

profile of v3, /device:TPU:0, one launch (start us, length us, event | category | flops | bytes accessed | tf_op | source)
XLA Modules:
  0.0 268.2 jit_solution(4382567810927448203)
XLA Ops:
  4.6 5.4 %pack.1 = (bf16[2,3,96,768]{3,2,1,0:T(8,128)(2,1)}, bf16[4,432,768]{2,1,0:T(8,128)(2,1)}, bf16[432,768]{1,0:T(8,128)(2,1)}) custom-call(s32[8]{0:T(128)} %compare_select_fusion.1.info, f32[96,768]{1,0:T(8,128)} %lq.1, f32[96,768]{1,0:T(8,128)} %lk.1, f32[96,768]{1,0:T(8,128)} %lv.1, f32[96,768]{1,0:T(8,128)} %lo.1, f32[384,768]{1,0:T(8,128)} %lu.1, ...), custom_call_target="tpu_custom_call" | custom-call | flops 4000000 | bytes 12000000 | tf_op jit(solution)/shard_map/pack/pallas_call | solution.py:618
  10.5 3.6 %collective-permute-start.1 = (bf16[432,768]{1,0:T(8,128)(2,1)}, bf16[432,768]{1,0:T(8,128)(2,1)S(1)}, u32[]{:S(2)}, u32[]{:S(2)}) collective-permute-start(bf16[432,768]{1,0:T(8,128)(2,1)} %get-tuple-element.99), channel_id=1, source_target_pairs={{0,4},{1,5},{4,6},{5,7},{6,2},{7,3},{2,0},{3,1},{8,12},{9,13},{12,... | collective-permute-start | bytes 1990664 | tf_op jit(solution)/shard_map/ppermute | solution.py:1327
  14.7 2.1 collective-permute-done.4
  16.9 2.8 %collective-permute-start.5 = (bf16[2,128,768]{2,1,0:T(8,128)(2,1)S(1)}, bf16[2,128,768]{2,1,0:T(8,128)(2,1)S(1)}, u32[]{:S(2)}, u32[]{:S(2)}) collective-permute-start(bf16[2,128,768]{2,1,0:T(8,128)(2,1)S(1)} %pad_maximum_fusion.refs_0_.refs_30_), channel_id=1, source_target_pairs={{0,4},{1,5},{4,6},{5,7},{6,2},{7,3},{2,0},{3,1},{8,12},{9,13},{12,... | collective-permute-start | bytes 1179656 | tf_op jit(solution)/shard_map/ppermute | solution.py:1327
  19.7 10.0 %collective-permute-done.1.refs_0_ = bf16[432,768]{1,0:T(8,128)(2,1)S(1)} collective-permute-done((bf16[432,768]{1,0:T(8,128)(2,1)}, bf16[432,768]{1,0:T(8,128)(2,1)S(1)}, u32[]{:S(2)}, u32[]{:S(2)}) %collective-permute-start.1) | collective-permute-done | bytes 663584 | tf_op jit(solution)/shard_map/ppermute | solution.py:1327
  32.7 4.9 %collective-permute-done.5.refs_1_ = bf16[2,128,768]{2,1,0:T(8,128)(2,1)S(1)} collective-permute-done((bf16[2,128,768]{2,1,0:T(8,128)(2,1)S(1)}, bf16[2,128,768]{2,1,0:T(8,128)(2,1)S(1)}, u32[]{:S(2)}, u32[]{:S(2)}) %collective-permute-start.5) | collective-permute-done | bytes 393248 | tf_op jit(solution)/shard_map/ppermute | solution.py:1327
  37.5 3.4 %collective-permute-start.7 = (bf16[2,128,768]{2,1,0:T(8,128)(2,1)S(1)}, bf16[2,128,768]{2,1,0:T(8,128)(2,1)}, u32[]{:S(2)}, u32[]{:S(2)}) collective-permute-start(bf16[2,128,768]{2,1,0:T(8,128)(2,1)S(1)} %collective-permute-done.5.refs_1_), channel_id=1, source_target_pairs={{0,4},{1,5},{4,6},{5,7},{6,2},{7,3},{2,0},{3,1},{8,12},{9,13},{12,... | collective-permute-start | bytes 1179656 | tf_op jit(solution)/shard_map/ppermute | solution.py:1327
  41.0 8.2 %collective-permute-done.7.refs_2_ = bf16[2,128,768]{2,1,0:T(8,128)(2,1)} collective-permute-done((bf16[2,128,768]{2,1,0:T(8,128)(2,1)S(1)}, bf16[2,128,768]{2,1,0:T(8,128)(2,1)}, u32[]{:S(2)}, u32[]{:S(2)}) %collective-permute-start.7) | collective-permute-done | bytes 393248 | tf_op jit(solution)/shard_map/ppermute | solution.py:1327
  49.2 3.5 %collective-permute-start.11 = (bf16[2,128,768]{2,1,0:T(8,128)(2,1)}, bf16[2,128,768]{2,1,0:T(8,128)(2,1)}, u32[]{:S(2)}, u32[]{:S(2)}) collective-permute-start(bf16[2,128,768]{2,1,0:T(8,128)(2,1)} %collective-permute-done.7.refs_2_), channel_id=1, source_target_pairs={{0,4},{1,5},{4,6},{5,7},{6,2},{7,3},{2,0},{3,1},{8,12},{9,13},{12,... | collective-permute-start | bytes 1179656 | tf_op jit(solution)/shard_map/ppermute | solution.py:1327
  55.0 1.6 collective-permute-start.9
  57.5 1.6 collective-permute-start.8
  59.1 3.5 %collective-permute-done.11.refs_3_ = bf16[2,128,768]{2,1,0:T(8,128)(2,1)} collective-permute-done((bf16[2,128,768]{2,1,0:T(8,128)(2,1)}, bf16[2,128,768]{2,1,0:T(8,128)(2,1)}, u32[]{:S(2)}, u32[]{:S(2)}) %collective-permute-start.11) | collective-permute-done | bytes 393248 | tf_op jit(solution)/shard_map/ppermute | solution.py:1327
  62.6 13.6 %attend_student.1 = (bf16[4,2,192,256]{3,2,1,0:T(8,128)(2,1)}, bf16[3,1024,192]{2,1,0:T(8,128)(2,1)}, f32[8,1024]{1,0:T(8,128)}, f32[192,1024]{1,0:T(8,128)}) custom-call(s32[8]{0:T(128)} %compare_select_fusion.1.info, bf16[2,128,768]{2,1,0:T(8,128)(2,1)} %copy-done, bf16[2,128,768]{2,1,0:T(8,128)(2,1)} %copy-done.36, ...), custom_call_target="tpu_custom_call" | custom-call | flops 6000000000 | bytes 4000000 | tf_op jit(solution)/shard_map/attend_student/pallas_call | solution.py:776
  76.2 3.4 %collective-permute-start.12 = (bf16[432,768]{1,0:T(8,128)(2,1)}, bf16[432,768]{1,0:T(8,128)(2,1)}, u32[]{:S(2)}, u32[]{:S(2)}) collective-permute-start(bf16[432,768]{1,0:T(8,128)(2,1)} %collective-permute-done.10.refs_10_), channel_id=1, source_target_pairs={{0,4},{1,5},{4,6},{5,7},{6,2},{7,3},{2,0},{3,1},{8,12},{9,13},{12,... | collective-permute-start | bytes 1990664 | tf_op jit(solution)/shard_map/ppermute | solution.py:1327
  82.7 12.1 %attend_tutor.1 = bf16[4,2,192,256]{3,2,1,0:T(8,128)(2,1)} custom-call(s32[8]{0:T(128)} %compare_select_fusion.1.info, bf16[2,128,768]{2,1,0:T(8,128)(2,1)} %copy-done, bf16[2,128,768]{2,1,0:T(8,128)(2,1)} %copy-done.36, bf16[2,128,768]{2,1,0:T(8,128)(2,1)} %collective-permute-done.7.refs_2_, ...), custom_call_target="tpu_custom_call", output_to_operand_aliasing={{}: (9, {})} | custom-call | flops 6000000000 | bytes 4000000 | tf_op jit(solution)/shard_map/attend_tutor/pallas_call | solution.py:776
  96.6 3.7 %all-to-all-start = ((bf16[4,2,192,256]{3,2,1,0:T(8,128)(2,1)}), bf16[4,2,192,256]{3,2,1,0:T(8,128)(2,1)S(1)}, u32[]{:S(2)}, u32[]{:S(2)}) async-start(bf16[4,2,192,256]{3,2,1,0:T(8,128)(2,1)} %attend_tutor.1), calls=%async_computation | async-start | bytes 1572864 | tf_op jit(solution)/shard_map/all_to_all | solution.py:1340
  100.8 6.4 %collective-permute-done.21.refs_22_ = bf16[432,768]{1,0:T(8,128)(2,1)S(1)} collective-permute-done((bf16[432,768]{1,0:T(8,128)(2,1)}, bf16[432,768]{1,0:T(8,128)(2,1)S(1)}, u32[]{:S(2)}, u32[]{:S(2)}) %collective-permute-start.21) | collective-permute-done | bytes 663584 | tf_op jit(solution)/shard_map/ppermute | solution.py:1336
  108.8 1.6 collective-permute-start.30
  114.0 6.8 %collective-permute-done.29.refs_23_ = bf16[192,768]{1,0:T(8,128)(2,1)S(1)} collective-permute-done((bf16[192,768]{1,0:T(8,128)(2,1)S(1)}, bf16[192,768]{1,0:T(8,128)(2,1)S(1)}, u32[]{:S(2)}, u32[]{:S(2)}) %collective-permute-start.29) | collective-permute-done | bytes 294944 | tf_op jit(solution)/shard_map/ppermute | solution.py:1336
  123.2 4.6 %collective-permute-done.23.refs_14_ = bf16[240,768]{1,0:T(8,128)(2,1)} collective-permute-done((bf16[240,768]{1,0:T(8,128)(2,1)S(1)}, bf16[240,768]{1,0:T(8,128)(2,1)}, u32[]{:S(2)}, u32[]{:S(2)}) %collective-permute-start.23) | collective-permute-done | bytes 368672 | tf_op jit(solution)/shard_map/ppermute | solution.py:1336
  128.3 2.8 %collective-permute-done.22.refs_13_ = bf16[192,768]{1,0:T(8,128)(2,1)} collective-permute-done((bf16[192,768]{1,0:T(8,128)(2,1)S(1)}, bf16[192,768]{1,0:T(8,128)(2,1)}, u32[]{:S(2)}, u32[]{:S(2)}) %collective-permute-start.22) | collective-permute-done | bytes 294944 | tf_op jit(solution)/shard_map/ppermute | solution.py:1336
  131.6 1.8 collective-permute-done.27.refs_18_
  134.8 22.5 %middle.1 = (bf16[128,768]{1,0:T(8,128)(2,1)}, bf16[128,768]{1,0:T(8,128)(2,1)}, f32[256,768]{1,0:T(8,128)}, bf16[4,192,256]{2,1,0:T(8,128)(2,1)}, bf16[2,4,112,...) custom-call(s32[8]{0:T(128)} %compare_select_fusion.1.info, ...), custom_call_target="tpu_custom_call" | custom-call | flops 15000000512 | bytes 30000000 | tf_op jit(solution)/shard_map/middle/pallas_call | solution.py:1175
  157.9 3.7 %all-to-all-start.1 = ((bf16[4,192,256]{2,1,0:T(8,128)(2,1)}), bf16[4,192,256]{2,1,0:T(8,128)(2,1)S(1)}, u32[]{:S(2)}, u32[]{:S(2)}) async-start(bf16[4,192,256]{2,1,0:T(8,128)(2,1)} %get-tuple-element.137), calls=%async_computation.1 | async-start | bytes 786432 | tf_op jit(solution)/shard_map/all_to_all | solution.py:1340
  162.1 2.9 %add_convert_fusion = bf16[2,4,112,768]{3,2,1,0:T(8,128)(2,1)} fusion(bf16[2,4,112,768]{3,2,1,0:T(8,128)(2,1)S(1)} %collective-permute-done.37, bf16[2,4,112,768]{3,2,1,0:T(8,128)(2,1)} %get-tuple-element.140), kind=kLoop, calls=%fused_computation | loop fusion | flops 2752512 | bytes 4128768 | tf_op jit(solution)/shard_map/convert_element_type | solution.py:1309
  166.0 2.8 %add_convert_fusion.1 = bf16[2,4,112,768]{3,2,1,0:T(8,128)(2,1)} fusion(bf16[2,4,112,768]{3,2,1,0:T(8,128)(2,1)} %collective-permute-done.36, bf16[2,4,112,768]{3,2,1,0:T(8,128)(2,1)S(1)} %copy-done.4), kind=kLoop, calls=%fused_computation.1 | loop fusion | flops 2752512 | bytes 4128768 | tf_op jit(solution)/shard_map/convert_element_type | solution.py:1309
  169.8 3.8 %all-to-all-done.1.refs_10_ = bf16[4,192,256]{2,1,0:T(8,128)(2,1)S(1)} async-done(((bf16[4,192,256]{2,1,0:T(8,128)(2,1)}), bf16[4,192,256]{2,1,0:T(8,128)(2,1)S(1)}, u32[]{:S(2)}, u32[]{:S(2)}) %all-to-all-start.1) | async-done | bytes 393248 | tf_op jit(solution)/shard_map/all_to_all | solution.py:1340
  174.3 14.8 %attend_back.1 = (bf16[256,768]{1,0:T(8,128)(2,1)}, bf16[256,768]{1,0:T(8,128)(2,1)}, bf16[256,768]{1,0:T(8,128)(2,1)}, bf16[256,768]{1,0:T(8,128)(2,1)}, bf16[3...) custom-call(s32[8]{0:T(128)} %compare_select_fusion.1.info, bf16[2,128,768]{2,1,0:T(8,128)(2,1)} %copy-done, ...), custom_call_target="tpu_custom_call" | custom-call | flops 12000000000 | bytes 6000000 | tf_op jit(solution)/shard_map/attend_back/pallas_call | solution.py:906
  189.3 10.5 %collective-permute-done.38 = bf16[256,768]{1,0:T(8,128)(2,1)S(1)} collective-permute-done((bf16[256,768]{1,0:T(8,128)(2,1)}, bf16[256,768]{1,0:T(8,128)(2,1)S(1)}, u32[]{:S(2)}, u32[]{:S(2)}) %collective-permute-start.38) | collective-permute-done | bytes 393248 | tf_op jit(solution)/shard_map/ppermute | solution.py:1327
  201.1 1.7 fusion.2
  204.2 2.5 collective-permute-start.43
  206.9 1.6 collective-permute-start.45
  208.5 6.8 %collective-permute-done.43 = bf16[256,768]{1,0:T(8,128)(2,1)S(1)} collective-permute-done((bf16[256,768]{1,0:T(8,128)(2,1)S(1)}, bf16[256,768]{1,0:T(8,128)(2,1)S(1)}, u32[]{:S(2)}, u32[]{:S(2)}) %collective-permute-start.43) | collective-permute-done | bytes 393248 | tf_op jit(solution)/shard_map/ppermute | solution.py:1327
  215.4 2.1 collective-permute-start.62
  218.8 1.7 collective-permute-done.55
  220.5 1.7 fusion
  223.5 1.9 collective-permute-done.45
  227.6 2.7 %collective-permute-done.56 = bf16[112,768]{1,0:T(8,128)(2,1)S(1)} collective-permute-done((bf16[112,768]{1,0:T(8,128)(2,1)S(1)}, bf16[112,768]{1,0:T(8,128)(2,1)S(1)}, u32[]{:S(2)}, u32[]{:S(2)}) %collective-permute-start.56) | collective-permute-done | bytes 172064 | tf_op jit(solution)/shard_map/ppermute | solution.py:1327
  230.4 2.1 collective-permute-start.57
  234.2 1.9 collective-permute-start.49
  236.0 1.7 collective-permute-done.57
  237.8 3.0 %collective-permute-start.58 = (bf16[112,768]{1,0:T(8,128)(2,1)S(1)}, bf16[112,768]{1,0:T(8,128)(2,1)S(1)}, u32[]{:S(2)}, u32[]{:S(2)}) collective-permute-start(bf16[112,768]{1,0:T(8,128)(2,1)S(1)} %fusion.5), channel_id=1, source_target_pairs={{0,4},{1,5},{4,6},{5,7},{6,2},{7,3},{2,0},{3,1},{8,12},{9,13},{12,... | collective-permute-start | bytes 516104 | tf_op jit(solution)/shard_map/ppermute | solution.py:1327
  246.7 1.7 collective-permute-start.60
  249.4 2.8 %collective-permute-start.61 = (bf16[112,768]{1,0:T(8,128)(2,1)S(1)}, bf16[112,768]{1,0:T(8,128)(2,1)S(1)}, u32[]{:S(2)}, u32[]{:S(2)}) collective-permute-start(bf16[112,768]{1,0:T(8,128)(2,1)S(1)} %fusion.4.refs_0_), channel_id=1, source_target_pairs={{0,24},{8,16},{16,8},{24,0},{1,25},{9,17},{17,9},{25,1},{2,26},{10... | collective-permute-start | bytes 516104 | tf_op jit(solution)/shard_map/ppermute | solution.py:1336
  253.0 2.8 %collective-permute-start.54 = (bf16[112,768]{1,0:T(8,128)(2,1)S(1)}, bf16[112,768]{1,0:T(8,128)(2,1)S(1)}, u32[]{:S(2)}, u32[]{:S(2)}) collective-permute-start(bf16[112,768]{1,0:T(8,128)(2,1)S(1)} %fusion.7.refs_0_), channel_id=1, source_target_pairs={{0,24},{8,16},{16,8},{24,0},{1,25},{9,17},{17,9},{25,1},{2,26},{10... | collective-permute-start | bytes 516104 | tf_op jit(solution)/shard_map/ppermute | solution.py:1336
  257.6 2.0 finish_heads.1
  260.9 3.0 %finish_up.1 = (f32[384,768]{1,0:T(8,128)}, f32[64,768]{1,0:T(8,128)}) custom-call(s32[8]{0:T(128)} %compare_select_fusion.1.info, bf16[112,768]{1,0:T(8,128)(2,1)} %copy-done.8, bf16[112,768]{1,0:T(8,128)(2,1)} %copy-done.19, bf16[112,768]{1,0:T(8,128)(2,1)} %copy-done.20, bf16[112,768]{1,0:T(8,128)(2,1)} %copy-done.22), custom_call_target="tpu_custom_call" | custom-call | flops 1000000 | bytes 3000000 | tf_op jit(solution)/shard_map/finish_up/pallas_call | solution.py:1214
  264.7 3.3 %finish.1 = (f32[96,3072]{1,0:T(8,128)}, f32[96,768]{1,0:T(8,128)}, f32[1,1]{1,0:T(1,128)}, f32[384]{0:T(512)}, f32[96]{0:T(128)}, /*index=5*/f32[96]{0:T(128)},...) custom-call(s32[8]{0:T(128)} %compare_select_fusion.1.info, bf16[112,768]{1,0:T(8,128)(2,1)} %copy-done.7, ...), custom_call_target="tpu_custom_call" | custom-call | flops 1000000 | bytes 4000000 | tf_op jit(solution)/shard_map/finish/pallas_call | solution.py:1284
  (218 shorter events, 50.2 us)
Async XLA Ops:
  10.0 39.2 %collective-permute-start = (bf16[4,432,768]{2,1,0:T(8,128)(2,1)}, bf16[4,432,768]{2,1,0:T(8,128)(2,1)}, u32[]{:S(2)}, u32[]{:S(2)}) collective-permute-start(bf16[4,432,768]{2,1,0:T(8,128)(2,1)} %get-tuple-element.98.own), channel_id=1, source_target_pairs={{0,1},{1,0},{2,3},{3,2},{4,5},{5,4},{6,7},{7,6},{8,9},{9,8},{10,11... | collective-permute-start | bytes 7962632 | tf_op jit(solution)/shard_map/ppermute | solution.py:1333
  10.5 19.2 %collective-permute-start.1 = (bf16[432,768]{1,0:T(8,128)(2,1)}, bf16[432,768]{1,0:T(8,128)(2,1)S(1)}, u32[]{:S(2)}, u32[]{:S(2)}) collective-permute-start(bf16[432,768]{1,0:T(8,128)(2,1)} %get-tuple-element.99), channel_id=1, source_target_pairs={{0,4},{1,5},{4,6},{5,7},{6,2},{7,3},{2,0},{3,1},{8,12},{9,13},{12,... | collective-permute-start | bytes 1990664 | tf_op jit(solution)/shard_map/ppermute | solution.py:1327
  14.1 23.4 %collective-permute-start.6 = (bf16[2,3,96,768]{3,2,1,0:T(8,128)(2,1)}, bf16[2,3,96,768]{3,2,1,0:T(8,128)(2,1)S(1)}, u32[]{:S(2)}, u32[]{:S(2)}) collective-permute-start(bf16[2,3,96,768]{3,2,1,0:T(8,128)(2,1)} %get-tuple-element.101.refs_4_), channel_id=1, source_target_pairs={{0,1},{1,0},{2,3},{3,2},{4,5},{5,4},{6,7},{7,6},{8,9},{9,8},{10,11... | collective-permute-start | bytes 2654216 | tf_op jit(solution)/shard_map/ppermute | solution.py:1333
  16.9 20.7 %collective-permute-start.5 = (bf16[2,128,768]{2,1,0:T(8,128)(2,1)S(1)}, bf16[2,128,768]{2,1,0:T(8,128)(2,1)S(1)}, u32[]{:S(2)}, u32[]{:S(2)}) collective-permute-start(bf16[2,128,768]{2,1,0:T(8,128)(2,1)S(1)} %pad_maximum_fusion.refs_0_.refs_30_), channel_id=1, source_target_pairs={{0,4},{1,5},{4,6},{5,7},{6,2},{7,3},{2,0},{3,1},{8,12},{9,13},{12,... | collective-permute-start | bytes 1179656 | tf_op jit(solution)/shard_map/ppermute | solution.py:1327
  29.7 19.5 %collective-permute-start.2 = (bf16[432,768]{1,0:T(8,128)(2,1)S(1)}, bf16[432,768]{1,0:T(8,128)(2,1)}, u32[]{:S(2)}, u32[]{:S(2)}) collective-permute-start(bf16[432,768]{1,0:T(8,128)(2,1)S(1)} %collective-permute-done.1.refs_0_), channel_id=1, source_target_pairs={{0,8},{8,0},{16,24},{24,16},{1,9},{9,1},{17,25},{25,17},{2,10},{10... | collective-permute-start | bytes 1990664 | tf_op jit(solution)/shard_map/ppermute | solution.py:1336
  31.2 18.0 %collective-permute-start.3 = (bf16[432,768]{1,0:T(8,128)(2,1)S(1)}, bf16[432,768]{1,0:T(8,128)(2,1)S(1)}, u32[]{:S(2)}, u32[]{:S(2)}) collective-permute-start(bf16[432,768]{1,0:T(8,128)(2,1)S(1)} %collective-permute-done.1.refs_0_), channel_id=1, source_target_pairs={{0,16},{8,24},{16,0},{24,8},{1,17},{9,25},{17,1},{25,9},{2,18},{10... | collective-permute-start | bytes 1990664 | tf_op jit(solution)/shard_map/ppermute | solution.py:1336
  37.5 11.6 %collective-permute-start.7 = (bf16[2,128,768]{2,1,0:T(8,128)(2,1)S(1)}, bf16[2,128,768]{2,1,0:T(8,128)(2,1)}, u32[]{:S(2)}, u32[]{:S(2)}) collective-permute-start(bf16[2,128,768]{2,1,0:T(8,128)(2,1)S(1)} %collective-permute-done.5.refs_1_), channel_id=1, source_target_pairs={{0,4},{1,5},{4,6},{5,7},{6,2},{7,3},{2,0},{3,1},{8,12},{9,13},{12,... | collective-permute-start | bytes 1179656 | tf_op jit(solution)/shard_map/ppermute | solution.py:1327
  49.2 13.4 %collective-permute-start.11 = (bf16[2,128,768]{2,1,0:T(8,128)(2,1)}, bf16[2,128,768]{2,1,0:T(8,128)(2,1)}, u32[]{:S(2)}, u32[]{:S(2)}) collective-permute-start(bf16[2,128,768]{2,1,0:T(8,128)(2,1)} %collective-permute-done.7.refs_2_), channel_id=1, source_target_pairs={{0,4},{1,5},{4,6},{5,7},{6,2},{7,3},{2,0},{3,1},{8,12},{9,13},{12,... | collective-permute-start | bytes 1179656 | tf_op jit(solution)/shard_map/ppermute | solution.py:1327
  52.7 23.5 %collective-permute-start.10 = (bf16[432,768]{1,0:T(8,128)(2,1)S(1)}, bf16[432,768]{1,0:T(8,128)(2,1)}, u32[]{:S(2)}, u32[]{:S(2)}) collective-permute-start(bf16[432,768]{1,0:T(8,128)(2,1)S(1)} %collective-permute-done.1.refs_0_), channel_id=1, source_target_pairs={{0,4},{1,5},{4,6},{5,7},{6,2},{7,3},{2,0},{3,1},{8,12},{9,13},{12,... | collective-permute-start | bytes 1990664 | tf_op jit(solution)/shard_map/ppermute | solution.py:1327
  55.0 21.3 %collective-permute-start.9 = (bf16[240,768]{1,0:T(8,128)(2,1)S(1)}, bf16[240,768]{1,0:T(8,128)(2,1)}, u32[]{:S(2)}, u32[]{:S(2)}) collective-permute-start(bf16[240,768]{1,0:T(8,128)(2,1)S(1)} %slice.137), channel_id=1, source_target_pairs={{0,8},{8,0},{16,24},{24,16},{1,9},{9,1},{17,25},{25,17},{2,10},{10... | collective-permute-start | bytes 1105928 | tf_op jit(solution)/shard_map/ppermute | solution.py:1336
  57.5 18.7 %collective-permute-start.8 = (bf16[192,768]{1,0:T(8,128)(2,1)S(1)}, bf16[192,768]{1,0:T(8,128)(2,1)}, u32[]{:S(2)}, u32[]{:S(2)}) collective-permute-start(bf16[192,768]{1,0:T(8,128)(2,1)S(1)} %slice.136), channel_id=1, source_target_pairs={{0,16},{8,24},{16,0},{24,8},{1,17},{9,25},{17,1},{25,9},{2,18},{10... | collective-permute-start | bytes 884744 | tf_op jit(solution)/shard_map/ppermute | solution.py:1336
  76.2 18.6 %collective-permute-start.12 = (bf16[432,768]{1,0:T(8,128)(2,1)}, bf16[432,768]{1,0:T(8,128)(2,1)}, u32[]{:S(2)}, u32[]{:S(2)}) collective-permute-start(bf16[432,768]{1,0:T(8,128)(2,1)} %collective-permute-done.10.refs_10_), channel_id=1, source_target_pairs={{0,4},{1,5},{4,6},{5,7},{6,2},{7,3},{2,0},{3,1},{8,12},{9,13},{12,... | collective-permute-start | bytes 1990664 | tf_op jit(solution)/shard_map/ppermute | solution.py:1327
  79.7 16.3 %collective-permute-start.19 = (bf16[432,768]{1,0:T(8,128)(2,1)}, bf16[432,768]{1,0:T(8,128)(2,1)S(1)}, u32[]{:S(2)}, u32[]{:S(2)}) collective-permute-start(bf16[432,768]{1,0:T(8,128)(2,1)} %collective-permute-done.10.refs_10_), channel_id=1, source_target_pairs={{0,16},{8,24},{16,0},{24,8},{1,17},{9,25},{17,1},{25,9},{2,18},{10... | collective-permute-start | bytes 1990664 | tf_op jit(solution)/shard_map/ppermute | solution.py:1336
  81.2 15.3 %collective-permute-start.18 = (bf16[432,768]{1,0:T(8,128)(2,1)}, bf16[432,768]{1,0:T(8,128)(2,1)S(1)}, u32[]{:S(2)}, u32[]{:S(2)}) collective-permute-start(bf16[432,768]{1,0:T(8,128)(2,1)} %collective-permute-done.10.refs_10_), channel_id=1, source_target_pairs={{0,8},{8,0},{16,24},{24,16},{1,9},{9,1},{17,25},{25,17},{2,10},{10... | collective-permute-start | bytes 1990664 | tf_op jit(solution)/shard_map/ppermute | solution.py:1336
  94.9 12.3 %collective-permute-start.21 = (bf16[432,768]{1,0:T(8,128)(2,1)}, bf16[432,768]{1,0:T(8,128)(2,1)S(1)}, u32[]{:S(2)}, u32[]{:S(2)}) collective-permute-start(bf16[432,768]{1,0:T(8,128)(2,1)} %collective-permute-done.12.refs_20_), channel_id=1, source_target_pairs={{0,16},{8,24},{16,0},{24,8},{1,17},{9,25},{17,1},{25,9},{2,18},{10... | collective-permute-start | bytes 1990664 | tf_op jit(solution)/shard_map/ppermute | solution.py:1336
  95.4 12.7 %collective-permute-start.20 = (bf16[432,768]{1,0:T(8,128)(2,1)}, bf16[432,768]{1,0:T(8,128)(2,1)}, u32[]{:S(2)}, u32[]{:S(2)}) collective-permute-start(bf16[432,768]{1,0:T(8,128)(2,1)} %collective-permute-done.12.refs_20_), channel_id=1, source_target_pairs={{0,8},{8,0},{16,24},{24,16},{1,9},{9,1},{17,25},{25,17},{2,10},{10... | collective-permute-start | bytes 1990664 | tf_op jit(solution)/shard_map/ppermute | solution.py:1336
  96.0 12.1 %collective-permute-start.26 = (bf16[432,768]{1,0:T(8,128)(2,1)S(1)}, bf16[432,768]{1,0:T(8,128)(2,1)}, u32[]{:S(2)}, u32[]{:S(2)}) collective-permute-start(bf16[432,768]{1,0:T(8,128)(2,1)S(1)} %collective-permute-done.19.refs_12_), channel_id=1, source_target_pairs={{0,1},{1,0},{2,3},{3,2},{4,5},{5,4},{6,7},{7,6},{8,9},{9,8},{10,11... | collective-permute-start | bytes 1990664 | tf_op jit(solution)/shard_map/ppermute | solution.py:1333
  96.6 26.6 %all-to-all-start = ((bf16[4,2,192,256]{3,2,1,0:T(8,128)(2,1)}), bf16[4,2,192,256]{3,2,1,0:T(8,128)(2,1)S(1)}, u32[]{:S(2)}, u32[]{:S(2)}) async-start(bf16[4,2,192,256]{3,2,1,0:T(8,128)(2,1)} %attend_tutor.1), calls=%async_computation | async-start | bytes 1572864 | tf_op jit(solution)/shard_map/all_to_all | solution.py:1340
  100.3 8.4 %collective-permute-start.25 = (bf16[432,768]{1,0:T(8,128)(2,1)S(1)}, bf16[432,768]{1,0:T(8,128)(2,1)S(1)}, u32[]{:S(2)}, u32[]{:S(2)}) collective-permute-start(bf16[432,768]{1,0:T(8,128)(2,1)S(1)} %collective-permute-done.18.refs_11_), channel_id=1, source_target_pairs={{0,1},{1,0},{2,3},{3,2},{4,5},{5,4},{6,7},{7,6},{8,9},{9,8},{10,11... | collective-permute-start | bytes 1990664 | tf_op jit(solution)/shard_map/ppermute | solution.py:1333
  108.7 19.1 %collective-permute-start.31 = (bf16[432,768]{1,0:T(8,128)(2,1)}, bf16[432,768]{1,0:T(8,128)(2,1)}, u32[]{:S(2)}, u32[]{:S(2)}) collective-permute-start(bf16[432,768]{1,0:T(8,128)(2,1)} %collective-permute-done.12.refs_20_), channel_id=1, source_target_pairs={{0,1},{1,0},{2,3},{3,2},{4,5},{5,4},{6,7},{7,6},{8,9},{9,8},{10,11... | collective-permute-start | bytes 1990664 | tf_op jit(solution)/shard_map/ppermute | solution.py:1333
  108.8 12.0 %collective-permute-start.30 = (bf16[240,768]{1,0:T(8,128)(2,1)S(1)}, bf16[240,768]{1,0:T(8,128)(2,1)S(1)}, u32[]{:S(2)}, u32[]{:S(2)}) collective-permute-start(bf16[240,768]{1,0:T(8,128)(2,1)S(1)} %slice.141), channel_id=1, source_target_pairs={{0,8},{8,0},{16,24},{24,16},{1,9},{9,1},{17,25},{25,17},{2,10},{10... | collective-permute-start | bytes 1105928 | tf_op jit(solution)/shard_map/ppermute | solution.py:1336
  111.4 16.4 %collective-permute-start.23 = (bf16[240,768]{1,0:T(8,128)(2,1)S(1)}, bf16[240,768]{1,0:T(8,128)(2,1)}, u32[]{:S(2)}, u32[]{:S(2)}) collective-permute-start(bf16[240,768]{1,0:T(8,128)(2,1)S(1)} %slice.139), channel_id=1, source_target_pairs={{0,8},{8,0},{16,24},{24,16},{1,9},{9,1},{17,25},{25,17},{2,10},{10... | collective-permute-start | bytes 1105928 | tf_op jit(solution)/shard_map/ppermute | solution.py:1336
  112.1 8.7 %collective-permute-start.29 = (bf16[192,768]{1,0:T(8,128)(2,1)S(1)}, bf16[192,768]{1,0:T(8,128)(2,1)S(1)}, u32[]{:S(2)}, u32[]{:S(2)}) collective-permute-start(bf16[192,768]{1,0:T(8,128)(2,1)S(1)} %slice.140), channel_id=1, source_target_pairs={{0,16},{8,24},{16,0},{24,8},{1,17},{9,25},{17,1},{25,9},{2,18},{10... | collective-permute-start | bytes 884744 | tf_op jit(solution)/shard_map/ppermute | solution.py:1336
  113.9 19.5 %collective-permute-start.33 = (bf16[432,768]{1,0:T(8,128)(2,1)S(1)}, bf16[432,768]{1,0:T(8,128)(2,1)S(1)}, u32[]{:S(2)}, u32[]{:S(2)}) collective-permute-start(bf16[432,768]{1,0:T(8,128)(2,1)S(1)} %collective-permute-done.21.refs_22_), channel_id=1, source_target_pairs={{0,1},{1,0},{2,3},{3,2},{4,5},{5,4},{6,7},{7,6},{8,9},{9,8},{10,11... | collective-permute-start | bytes 1990664 | tf_op jit(solution)/shard_map/ppermute | solution.py:1333
  120.8 12.6 %collective-permute-start.32 = (bf16[432,768]{1,0:T(8,128)(2,1)}, bf16[432,768]{1,0:T(8,128)(2,1)S(1)}, u32[]{:S(2)}, u32[]{:S(2)}) collective-permute-start(bf16[432,768]{1,0:T(8,128)(2,1)} %collective-permute-done.20.refs_21_), channel_id=1, source_target_pairs={{0,1},{1,0},{2,3},{3,2},{4,5},{5,4},{6,7},{7,6},{8,9},{9,8},{10,11... | collective-permute-start | bytes 1990664 | tf_op jit(solution)/shard_map/ppermute | solution.py:1333
  122.2 8.9 %collective-permute-start.22 = (bf16[192,768]{1,0:T(8,128)(2,1)S(1)}, bf16[192,768]{1,0:T(8,128)(2,1)}, u32[]{:S(2)}, u32[]{:S(2)}) collective-permute-start(bf16[192,768]{1,0:T(8,128)(2,1)S(1)} %slice.138), channel_id=1, source_target_pairs={{0,16},{8,24},{16,0},{24,8},{1,17},{9,25},{17,1},{25,9},{2,18},{10... | collective-permute-start | bytes 884744 | tf_op jit(solution)/shard_map/ppermute | solution.py:1336
  157.5 8.5 %collective-permute-start.36 = (bf16[2,4,112,768]{3,2,1,0:T(8,128)(2,1)}, bf16[2,4,112,768]{3,2,1,0:T(8,128)(2,1)}, u32[]{:S(2)}, u32[]{:S(2)}) collective-permute-start(bf16[2,4,112,768]{3,2,1,0:T(8,128)(2,1)} %get-tuple-element.139), channel_id=1, source_target_pairs={{0,1},{1,0},{2,3},{3,2},{4,5},{5,4},{6,7},{7,6},{8,9},{9,8},{10,11... | collective-permute-start | bytes 4128776 | tf_op jit(solution)/shard_map/ppermute | solution.py:1333
  157.9 15.7 %all-to-all-start.1 = ((bf16[4,192,256]{2,1,0:T(8,128)(2,1)}), bf16[4,192,256]{2,1,0:T(8,128)(2,1)S(1)}, u32[]{:S(2)}, u32[]{:S(2)}) async-start(bf16[4,192,256]{2,1,0:T(8,128)(2,1)} %get-tuple-element.137), calls=%async_computation.1 | async-start | bytes 786432 | tf_op jit(solution)/shard_map/all_to_all | solution.py:1340
  161.6 42.3 %collective-permute-start.41 = (bf16[2,4,112,768]{3,2,1,0:T(8,128)(2,1)}, bf16[2,4,112,768]{3,2,1,0:T(8,128)(2,1)S(1)}, u32[]{:S(2)}, u32[]{:S(2)}) collective-permute-start(bf16[2,4,112,768]{3,2,1,0:T(8,128)(2,1)} %get-tuple-element.149), channel_id=1, source_target_pairs={{0,1},{1,0},{2,3},{3,2},{4,5},{5,4},{6,7},{7,6},{8,9},{9,8},{10,11... | collective-permute-start | bytes 4128776 | tf_op jit(solution)/shard_map/ppermute | solution.py:1333
  161.8 39.3 %collective-permute-start.39 = (bf16[2,4,112,768]{3,2,1,0:T(8,128)(2,1)}, bf16[2,4,112,768]{3,2,1,0:T(8,128)(2,1)}, u32[]{:S(2)}, u32[]{:S(2)}) collective-permute-start(bf16[2,4,112,768]{3,2,1,0:T(8,128)(2,1)} %get-tuple-element.146), channel_id=1, source_target_pairs={{0,1},{1,0},{2,3},{3,2},{4,5},{5,4},{6,7},{7,6},{8,9},{9,8},{10,11... | collective-permute-start | bytes 4128776 | tf_op jit(solution)/shard_map/ppermute | solution.py:1333
  165.1 35.8 %collective-permute-start.42 = (bf16[2,4,112,768]{3,2,1,0:T(8,128)(2,1)}, bf16[2,4,112,768]{3,2,1,0:T(8,128)(2,1)S(1)}, u32[]{:S(2)}, u32[]{:S(2)}) collective-permute-start(bf16[2,4,112,768]{3,2,1,0:T(8,128)(2,1)} %add_convert_fusion), channel_id=1, source_target_pairs={{0,16},{8,24},{16,0},{24,8},{1,17},{9,25},{17,1},{25,9},{2,18},{10... | collective-permute-start | bytes 4128776 | tf_op jit(solution)/shard_map/ppermute | solution.py:1336
  168.8 32.3 %collective-permute-start.40 = (bf16[2,4,112,768]{3,2,1,0:T(8,128)(2,1)}, bf16[2,4,112,768]{3,2,1,0:T(8,128)(2,1)}, u32[]{:S(2)}, u32[]{:S(2)}) collective-permute-start(bf16[2,4,112,768]{3,2,1,0:T(8,128)(2,1)} %add_convert_fusion.1), channel_id=1, source_target_pairs={{0,8},{8,0},{16,24},{24,16},{1,9},{9,1},{17,25},{25,17},{2,10},{10... | collective-permute-start | bytes 4128776 | tf_op jit(solution)/shard_map/ppermute | solution.py:1336
  189.2 10.6 %collective-permute-start.38 = (bf16[256,768]{1,0:T(8,128)(2,1)}, bf16[256,768]{1,0:T(8,128)(2,1)S(1)}, u32[]{:S(2)}, u32[]{:S(2)}) collective-permute-start(bf16[256,768]{1,0:T(8,128)(2,1)} %get-tuple-element.143), channel_id=1, source_target_pairs={{0,4},{1,5},{4,6},{5,7},{6,2},{7,3},{2,0},{3,1},{8,12},{9,13},{12,... | collective-permute-start | bytes 1179656 | tf_op jit(solution)/shard_map/ppermute | solution.py:1327
  202.7 17.8 %collective-permute-start.55 = (bf16[4,112,768]{2,1,0:T(8,128)(2,1)S(1)}, bf16[4,112,768]{2,1,0:T(8,128)(2,1)S(1)}, u32[]{:S(2)}, u32[]{:S(2)}) collective-permute-start(bf16[4,112,768]{2,1,0:T(8,128)(2,1)S(1)} %fusion.2), channel_id=1, source_target_pairs={{0,16},{8,24},{16,0},{24,8},{1,17},{9,25},{17,1},{25,9},{2,18},{10... | collective-permute-start | bytes 2064392 | tf_op jit(solution)/shard_map/ppermute | solution.py:1336
  204.2 11.1 %collective-permute-start.43 = (bf16[256,768]{1,0:T(8,128)(2,1)S(1)}, bf16[256,768]{1,0:T(8,128)(2,1)S(1)}, u32[]{:S(2)}, u32[]{:S(2)}) collective-permute-start(bf16[256,768]{1,0:T(8,128)(2,1)S(1)} %add_convert_fusion.8), channel_id=1, source_target_pairs={{0,4},{1,5},{4,6},{5,7},{6,2},{7,3},{2,0},{3,1},{8,12},{9,13},{12,... | collective-permute-start | bytes 1179656 | tf_op jit(solution)/shard_map/ppermute | solution.py:1327
  206.9 18.4 %collective-permute-start.45 = (bf16[4,112,768]{2,1,0:T(8,128)(2,1)S(1)}, bf16[4,112,768]{2,1,0:T(8,128)(2,1)S(1)}, u32[]{:S(2)}, u32[]{:S(2)}) collective-permute-start(bf16[4,112,768]{2,1,0:T(8,128)(2,1)S(1)} %fusion.3), channel_id=1, source_target_pairs={{0,8},{8,0},{16,24},{24,16},{1,9},{9,1},{17,25},{25,17},{2,10},{10... | collective-permute-start | bytes 2064392 | tf_op jit(solution)/shard_map/ppermute | solution.py:1336
  215.4 11.9 %collective-permute-start.62 = (bf16[256,768]{1,0:T(8,128)(2,1)S(1)}, bf16[256,768]{1,0:T(8,128)(2,1)S(1)}, u32[]{:S(2)}, u32[]{:S(2)}) collective-permute-start(bf16[256,768]{1,0:T(8,128)(2,1)S(1)} %add_convert_fusion.7), channel_id=1, source_target_pairs={{0,4},{1,5},{4,6},{5,7},{6,2},{7,3},{2,0},{3,1},{8,12},{9,13},{12,... | collective-permute-start | bytes 1179656 | tf_op jit(solution)/shard_map/ppermute | solution.py:1327
  217.5 15.3 %collective-permute-start.48 = (bf16[304,768]{1,0:T(8,128)(2,1)S(1)}, bf16[304,768]{1,0:T(8,128)(2,1)S(1)}, u32[]{:S(2)}, u32[]{:S(2)}) collective-permute-start(bf16[304,768]{1,0:T(8,128)(2,1)S(1)} %add_convert_fusion.6), channel_id=1, source_target_pairs={{0,8},{8,0},{16,24},{24,16},{1,9},{9,1},{17,25},{25,17},{2,10},{10... | collective-permute-start | bytes 1400840 | tf_op jit(solution)/shard_map/ppermute | solution.py:1336
  218.8 33.5 %collective-permute-start.44 = (bf16[128,768]{1,0:T(8,128)(2,1)S(1)}, bf16[128,768]{1,0:T(8,128)(2,1)S(1)}, u32[]{:S(2)}, u32[]{:S(2)}) collective-permute-start(bf16[128,768]{1,0:T(8,128)(2,1)S(1)} %copy-done.43), channel_id=1, source_target_pairs={{0,1},{1,0},{2,3},{3,2},{4,5},{5,4},{6,7},{7,6},{8,9},{9,8},{10,11... | collective-permute-start | bytes 589832 | tf_op jit(solution)/shard_map/ppermute | solution.py:1333
  222.2 8.1 %collective-permute-start.56 = (bf16[112,768]{1,0:T(8,128)(2,1)S(1)}, bf16[112,768]{1,0:T(8,128)(2,1)S(1)}, u32[]{:S(2)}, u32[]{:S(2)}) collective-permute-start(bf16[112,768]{1,0:T(8,128)(2,1)S(1)} %slice_bitcast_fusion.3), channel_id=1, source_target_pairs={{0,4},{1,5},{4,6},{5,7},{6,2},{7,3},{2,0},{3,1},{8,12},{9,13},{12,... | collective-permute-start | bytes 516104 | tf_op jit(solution)/shard_map/ppermute | solution.py:1327
  225.7 8.4 %collective-permute-start.46 = (bf16[112,768]{1,0:T(8,128)(2,1)S(1)}, bf16[112,768]{1,0:T(8,128)(2,1)S(1)}, u32[]{:S(2)}, u32[]{:S(2)}) collective-permute-start(bf16[112,768]{1,0:T(8,128)(2,1)S(1)} %slice_bitcast_fusion.7), channel_id=1, source_target_pairs={{0,4},{1,5},{4,6},{5,7},{6,2},{7,3},{2,0},{3,1},{8,12},{9,13},{12,... | collective-permute-start | bytes 516104 | tf_op jit(solution)/shard_map/ppermute | solution.py:1327
  227.6 24.8 %collective-permute-start.63 = (f32[128,768]{1,0:T(8,128)S(1)}, f32[128,768]{1,0:T(8,128)S(1)}, u32[]{:S(2)}, u32[]{:S(2)}) collective-permute-start(f32[128,768]{1,0:T(8,128)S(1)} %get-tuple-element.179), channel_id=1, source_target_pairs={{0,1},{1,0},{2,3},{3,2},{4,5},{5,4},{6,7},{7,6},{8,9},{9,8},{10,11... | collective-permute-start | bytes 1179656 | tf_op jit(solution)/shard_map/ppermute | solution.py:1333
  232.9 10.2 %collective-permute-start.50 = (bf16[304,768]{1,0:T(8,128)(2,1)S(1)}, bf16[304,768]{1,0:T(8,128)(2,1)S(1)}, u32[]{:S(2)}, u32[]{:S(2)}) collective-permute-start(bf16[304,768]{1,0:T(8,128)(2,1)S(1)} %add_convert_fusion.5), channel_id=1, source_target_pairs={{0,16},{8,24},{16,0},{24,8},{1,17},{9,25},{17,1},{25,9},{2,18},{10... | collective-permute-start | bytes 1400840 | tf_op jit(solution)/shard_map/ppermute | solution.py:1336
  246.7 12.8 %collective-permute-start.60 = (bf16[112,768]{1,0:T(8,128)(2,1)S(1)}, bf16[112,768]{1,0:T(8,128)(2,1)S(1)}, u32[]{:S(2)}, u32[]{:S(2)}) collective-permute-start(bf16[112,768]{1,0:T(8,128)(2,1)S(1)} %fusion.4.refs_0_), channel_id=1, source_target_pairs={{0,16},{8,24},{16,0},{24,8},{1,17},{9,25},{17,1},{25,9},{2,18},{10... | collective-permute-start | bytes 516104 | tf_op jit(solution)/shard_map/ppermute | solution.py:1336
  249.4 10.2 %collective-permute-start.61 = (bf16[112,768]{1,0:T(8,128)(2,1)S(1)}, bf16[112,768]{1,0:T(8,128)(2,1)S(1)}, u32[]{:S(2)}, u32[]{:S(2)}) collective-permute-start(bf16[112,768]{1,0:T(8,128)(2,1)S(1)} %fusion.4.refs_0_), channel_id=1, source_target_pairs={{0,24},{8,16},{16,8},{24,0},{1,25},{9,17},{17,9},{25,1},{2,26},{10... | collective-permute-start | bytes 516104 | tf_op jit(solution)/shard_map/ppermute | solution.py:1336
  252.3 11.6 %collective-permute-start.52 = (bf16[112,768]{1,0:T(8,128)(2,1)S(1)}, bf16[112,768]{1,0:T(8,128)(2,1)S(1)}, u32[]{:S(2)}, u32[]{:S(2)}) collective-permute-start(bf16[112,768]{1,0:T(8,128)(2,1)S(1)} %fusion.7.refs_0_), channel_id=1, source_target_pairs={{0,8},{8,0},{16,24},{24,16},{1,9},{9,1},{17,25},{25,17},{2,10},{10... | collective-permute-start | bytes 516104 | tf_op jit(solution)/shard_map/ppermute | solution.py:1336
  252.4 11.5 %collective-permute-start.53 = (bf16[112,768]{1,0:T(8,128)(2,1)S(1)}, bf16[112,768]{1,0:T(8,128)(2,1)S(1)}, u32[]{:S(2)}, u32[]{:S(2)}) collective-permute-start(bf16[112,768]{1,0:T(8,128)(2,1)S(1)} %fusion.7.refs_0_), channel_id=1, source_target_pairs={{0,16},{8,24},{16,0},{24,8},{1,17},{9,25},{17,1},{25,9},{2,18},{10... | collective-permute-start | bytes 516104 | tf_op jit(solution)/shard_map/ppermute | solution.py:1336
  253.0 10.9 %collective-permute-start.54 = (bf16[112,768]{1,0:T(8,128)(2,1)S(1)}, bf16[112,768]{1,0:T(8,128)(2,1)S(1)}, u32[]{:S(2)}, u32[]{:S(2)}) collective-permute-start(bf16[112,768]{1,0:T(8,128)(2,1)S(1)} %fusion.7.refs_0_), channel_id=1, source_target_pairs={{0,24},{8,16},{16,8},{24,0},{1,25},{9,17},{17,9},{25,1},{2,26},{10... | collective-permute-start | bytes 516104 | tf_op jit(solution)/shard_map/ppermute | solution.py:1336
  (62 other events, 585.3 us)
